TPU v7x, 128 devices: a whole 4x4x4 slice. The times are simulated.
128 devices in a mesh: gx: 8 (over z, core), gy: 16 (over y, x).
Axes of the slice: x: 4, y: 4, z: 4, core: 2. Of those that a mesh axis runs over, the one named last changes fastest.
Arguments:
- a_vals: bfloat16 [1, 2048, 5, 128, 128], P(None, ('gx', 'gy')), may hold values from -1.796875 to 1.796875
- a_cols: int32 [1, 2048, 5], P(None, ('gx', 'gy')), may hold values from 0 to 2047, as said below
- p_vals: bfloat16 [1, 2048, 2, 128, 128], P(None, ('gx', 'gy')), may hold values from -0.5 to 0.5
- p_cols: int32 [1, 2048, 2], P(None, ('gx', 'gy')), may hold values from 0 to 511, as said below
- p2_vals: bfloat16 [1, 512, 2, 128, 128], P(None, ('gx', 'gy')), may hold values from -0.5 to 0.5
- p2_cols: int32 [1, 512, 2], P(None, ('gx', 'gy')), may hold values from 0 to 127, as said below
Outputs:
- coarse: bfloat16 [1, 512, 7, 128, 128], P(None, ('gx', 'gy'))
- coarsest: bfloat16 [1, 128, 7, 128, 128], P(None, ('gx', 'gy'))
Inputs may be any that keep to these rules, and one draw needn't show every extreme that they name: In the fine row order a_cols[u, 0] = u, and a_cols[u, 1], .., a_cols[u, 4] are (u + d) mod 2048 for four different d among -3 .. -1 and 1 .. 3, in rising order of d. p_cols[u, 0] = u // 4, and p_cols[u, 1] is (u // 4 + 1) mod 512 or (u // 4 - 1) mod 512. p2_cols[J, 0] = J // 4, and p2_cols[J, 1] is (J // 4 + 1) mod 128 or (J // 4 - 1) mod 128.
All inputs are finite; a program needn't handle non-finite values.
Results may differ from a plain program's by a relative error of at most 0.0095.
Values may be sent and summed in bfloat16 or wider, within the bound.
No kernel may reach another device: no remote copies, remote signals or barrier semaphores. Data moves between devices by JAX's collectives and lax.ppermute only.
A program may use at most 64 MiB of HBM per device.

v0:
```python
import jax
import jax.numpy as jnp
from jax import lax
from jax.sharding import PartitionSpec as P

KC = 7
HALF = 3
AGG = 4
AGG2 = 4


def with_halo(block, sides, width):
    for axis, dim in sides:
        count = lax.axis_size(axis)
        forward = [(i, i + 1) for i in range(count - 1)]
        forward.append((count - 1, 0))
        backward = [(target, source) for source, target in forward]
        low = lax.ppermute(
            lax.slice_in_dim(block, block.shape[dim] - width, None, axis=dim), axis, forward
        )
        high = lax.ppermute(lax.slice_in_dim(block, 0, width, axis=dim), axis, backward)
        block = jnp.concatenate([low, block, high], axis=dim)
    return block


def wrap_rims(extended, width):
    position = lax.axis_index(("gx", "gy"))
    final_dev = lax.axis_size(("gx", "gy")) - 1
    length = extended.shape[1]
    low_rim = extended[:, :width]
    high_rim = extended[:, length - width :]
    low_rim = jnp.where(position == 0, jnp.roll(low_rim, 1, axis=0), low_rim)
    high_rim = jnp.where(position == final_dev, jnp.roll(high_rim, -1, axis=0), high_rim)
    return jnp.concatenate([low_rim, extended[:, width : length - width], high_rim], axis=1)


def side_of(p_cols, ncoarse):
    return ((p_cols[:, :, 1] - p_cols[:, :, 0] + 1) % ncoarse - 1).astype(jnp.bfloat16)


def band_form(p_vals, side):
    second = p_vals[:, :, 1]
    lower_slot = jnp.where((side < 0)[:, :, None, None], second, jnp.zeros_like(second))
    upper_slot = jnp.where((side > 0)[:, :, None, None], second, jnp.zeros_like(second))
    return jnp.stack([lower_slot, p_vals[:, :, 0], upper_slot], axis=2)


def row_products(a_vals, offsets, extended, group_size):
    row_count = a_vals.shape[1]
    local_rows = jnp.arange(row_count, dtype=jnp.int32)
    accumulated = jnp.zeros(
        (a_vals.shape[0], row_count, 5, a_vals.shape[-2], extended.shape[-1]), jnp.float32
    )
    for column in range(a_vals.shape[2]):
        shifted = local_rows[None, :] + offsets[:, :, column]
        picked = jnp.take_along_axis(extended, (shifted + HALF)[:, :, None, None, None], axis=1)
        block_terms = jnp.einsum(
            "arij,arcjl->arcil", a_vals[:, :, column], picked, preferred_element_type=jnp.float32
        )
        coarse_step = shifted // group_size - (local_rows // group_size)[None, :]
        for offset in (-1, 0, 1):
            selected = jnp.where((coarse_step == offset)[:, :, None, None, None], block_terms, 0.0)
            accumulated = accumulated.at[:, :, offset + 1 : offset + 4].add(selected)
    return accumulated.astype(jnp.bfloat16)


def coarse_terms(products, bands, group_size):
    super_count, row_count = (products.shape[0], products.shape[1])
    groups = row_count // group_size
    prod_grouped = products.reshape(
        super_count, groups, group_size, 5, products.shape[-2], products.shape[-1]
    )
    band_grouped = bands.reshape(
        super_count, groups, group_size, 3, bands.shape[-2], bands.shape[-1]
    )
    pair_terms = jnp.einsum(
        "agmcij,agmsil->agcsjl", band_grouped, prod_grouped, preferred_element_type=jnp.float32
    )
    accumulated = jnp.zeros(
        (super_count, groups + 2, KC, products.shape[-1], products.shape[-1]), jnp.float32
    )
    for column in range(3):
        accumulated = accumulated.at[:, column : column + groups, 2 - column : 7 - column].add(
            pair_terms[:, :, column]
        )
    return accumulated


def body(a_vals, a_cols, p_vals, p_cols, p2_vals, p2_cols):
    devices = lax.axis_size(("gx", "gy"))
    position = lax.axis_index(("gx", "gy"))
    super_count, fine_rows = (a_vals.shape[0], a_vals.shape[1])
    nfine = super_count * fine_rows * devices
    ncoarse = nfine // AGG
    fine_side = side_of(p_cols, ncoarse)
    bands = band_form(p_vals, fine_side)
    fine_ext = wrap_rims(with_halo(bands, ((("gx", "gy"), 1),), HALF), HALF)
    global_rows = (
        jnp.arange(super_count, dtype=jnp.int32)[:, None] * devices + position
    ) * fine_rows + jnp.arange(fine_rows, dtype=jnp.int32)[None, :]
    offsets = (a_cols - global_rows[:, :, None] + HALF) % nfine - HALF
    products = row_products(a_vals, offsets, fine_ext, AGG)
    combined = jnp.concatenate([products, bands], axis=2)
    neighbour_rows = wrap_rims(with_halo(combined, ((("gx", "gy"), 1),), AGG), AGG)
    neighbour_bands = neighbour_rows[:, :, 5:]
    partial_sums = coarse_terms(neighbour_rows[:, :, :5], neighbour_bands, AGG)
    coarse_sum = partial_sums[:, 2 : partial_sums.shape[1] - 2]
    coarse = coarse_sum.astype(jnp.bfloat16)
    ncoarsest = ncoarse // AGG2
    coarse_side = side_of(p2_cols, ncoarsest)
    coarse_bands = band_form(p2_vals, coarse_side)
    coarse_ext = wrap_rims(with_halo(coarse_bands, ((("gx", "gy"), 1),), HALF), HALF)
    band_offsets = jnp.broadcast_to(
        jnp.arange(KC, dtype=jnp.int32) - HALF, (super_count, coarse.shape[1], KC)
    )
    coarse_products = row_products(coarse, band_offsets, coarse_ext, AGG2)
    final_sums = coarse_terms(coarse_products, coarse_bands, AGG2)
    final_edges = wrap_rims(
        with_halo(final_sums.astype(jnp.bfloat16), ((("gx", "gy"), 1),), 1).astype(
            final_sums.dtype
        ),
        1,
    )
    coarsest = final_sums[:, 1:2] + final_edges[:, 0:1] + final_edges[:, final_edges.shape[1] - 1 :]
    return (coarse, coarsest.astype(jnp.bfloat16))


def solution(mesh):
    in_specs = (
        P(None, ("gx", "gy"), None, None, None),
        P(None, ("gx", "gy"), None),
        P(None, ("gx", "gy"), None, None, None),
        P(None, ("gx", "gy"), None),
        P(None, ("gx", "gy"), None, None, None),
        P(None, ("gx", "gy"), None),
    )
    out_specs = (P(None, ("gx", "gy"), None, None, None), P(None, ("gx", "gy"), None, None, None))
    return jax.shard_map(body, mesh=mesh, in_specs=in_specs, out_specs=out_specs, check_vma=False)
```

profile of v0, /device:TPU:0, one launch (start us, length us, event | category | flops | bytes accessed | tf_op | source)
XLA Modules:
  0.0 159.8 jit_solution(13083015939516802334)
XLA Ops:
  6.0 6.7 %collective-permute-start.1 = (bf16[1,3,3,128,128]{3,4,2,1,0:T(8,128)(2,1)S(1)}, bf16[1,3,3,128,128]{3,4,2,1,0:T(8,128)(2,1)S(1)}, u32[]{:S(2)}, u32[]{:S(2)}) collective-permute-start(bf16[1,3,3,128,128]{3,4,2,1,0:T(8,128)(2,1)S(1)} %get-tuple-element.527), channel_id=1, source_target_pairs={{1,0},{2,1},{3,2},{4,3},{5,4},{6,5},{7,6},{8,7},{9,8},{10,9},{11,1... | collective-permute-start | bytes 884744 | tf_op jit(solution)/shard_map/ppermute | solution.py:21
  13.8 7.2 %collective-permute-start.5 = (bf16[1,3,3,128,128]{4,3,1,2,0:T(8,128)(2,1)}, bf16[1,3,3,128,128]{4,3,1,2,0:T(8,128)(2,1)}, u32[]{:S(2)}, u32[]{:S(2)}) collective-permute-start(bf16[1,3,3,128,128]{4,3,1,2,0:T(8,128)(2,1)} %get-tuple-element.535), channel_id=1, source_target_pairs={{1,0},{2,1},{3,2},{4,3},{5,4},{6,5},{7,6},{8,7},{9,8},{10,9},{11,1... | collective-permute-start | bytes 884744 | tf_op jit(solution)/shard_map/ppermute | solution.py:21
  23.1 1.9 %broadcast_compare_fusion.6 = (pred[4]{0:T(512)(128)(4,1)}, pred[4]{0:T(512)(128)(4,1)}) fusion(s32[]{:T(128)} %bitcast.110, s32[]{:T(128)} %bitcast.98), kind=kLoop, calls=%fused_computation.372 | loop fusion | flops 176 | bytes 16 | tf_op jit(solution)/shard_map/eq | solution.py:62
  25.0 1.9 %and_bitcast_fusion.4 = (pred[4]{0:T(512)(128)(4,1)}, pred[4]{0:T(512)(128)(4,1)}) fusion(s32[]{:T(128)} %bitcast.110, s32[]{:T(128)} %bitcast.98), kind=kLoop, calls=%fused_computation.261 | loop fusion | flops 64 | bytes 16 | tf_op jit(solution)/shard_map/jit(take_along_axis)/and | solution.py:56
  26.9 1.9 %broadcast_compare_fusion.20 = (pred[4]{0:T(512)(128)(4,1)}, pred[4]{0:T(512)(128)(4,1)}) fusion(s32[]{:T(128)} %bitcast.110, s32[]{:T(128)} %bitcast.98), kind=kLoop, calls=%fused_computation.386 | loop fusion | flops 176 | bytes 16 | tf_op jit(solution)/shard_map/eq | solution.py:62
  29.4 1.9 %broadcast_compare_fusion.14 = (pred[4]{0:T(512)(128)(4,1)}, pred[4]{0:T(512)(128)(4,1)}) fusion(s32[]{:T(128)} %bitcast.85, s32[]{:T(128)} %bitcast.146), kind=kLoop, calls=%fused_computation.380 | loop fusion | flops 176 | bytes 16 | tf_op jit(solution)/shard_map/eq | solution.py:62
  31.3 1.9 %broadcast_compare_fusion.10 = (pred[4]{0:T(512)(128)(4,1)}, pred[4]{0:T(512)(128)(4,1)}) fusion(s32[]{:T(128)} %bitcast.146, s32[]{:T(128)} %bitcast.110), kind=kLoop, calls=%fused_computation.376 | loop fusion | flops 176 | bytes 16 | tf_op jit(solution)/shard_map/eq | solution.py:62
  35.1 1.9 %broadcast_compare_fusion.12 = (pred[4]{0:T(512)(128)(4,1)}, pred[4]{0:T(512)(128)(4,1)}) fusion(s32[]{:T(128)} %bitcast.134, s32[]{:T(128)} %bitcast.98), kind=kLoop, calls=%fused_computation.378 | loop fusion | flops 176 | bytes 16 | tf_op jit(solution)/shard_map/eq | solution.py:62
  37.0 1.9 %fusion.132 = (s32[4]{0:T(128)}, s32[4]{0:T(128)}) fusion(s32[]{:T(128)} %bitcast.122, s32[]{:T(128)} %bitcast.134), kind=kLoop, calls=%fused_computation.361 | loop fusion | flops 40 | bytes 40 | tf_op jit(solution)/shard_map/jit(take_along_axis)/reshape | solution.py:56
  44.4 1.9 %fusion.134 = (s32[4]{0:T(128)}, s32[4]{0:T(128)}) fusion(s32[]{:T(128)} %bitcast.146, s32[]{:T(128)} %bitcast.158), kind=kLoop, calls=%fused_computation.363 | loop fusion | flops 40 | bytes 40 | tf_op jit(solution)/shard_map/jit(take_along_axis)/reshape | solution.py:56
  46.4 1.9 %broadcast_compare_fusion.2 = (pred[4]{0:T(512)(128)(4,1)}, pred[4]{0:T(512)(128)(4,1)}) fusion(s32[]{:T(128)} %bitcast.158, s32[]{:T(128)} %bitcast.146), kind=kLoop, calls=%fused_computation.368 | loop fusion | flops 176 | bytes 16 | tf_op jit(solution)/shard_map/eq | solution.py:62
  48.3 1.9 %and_bitcast_fusion = (pred[4]{0:T(512)(128)(4,1)}, pred[4]{0:T(512)(128)(4,1)}) fusion(s32[]{:T(128)} %bitcast.158, s32[]{:T(128)} %bitcast.146), kind=kLoop, calls=%fused_computation.257 | loop fusion | flops 64 | bytes 16 | tf_op jit(solution)/shard_map/jit(take_along_axis)/and | solution.py:56
  52.7 1.9 %gather_fusion = bf16[16,3,128,128]{2,3,1,0:T(8,128)(2,1)} fusion(bf16[22,3,128,128]{2,3,1,0:T(8,128)(2,1)S(1)} %maximum_bitcast_fusion, s32[1024]{0:T(1024)S(1)} %pad_clamp_fusion.11), kind=kCustom, calls=%fused_computation.clone | custom fusion | bytes 3145792 | tf_op jit(solution)/shard_map/jit(take_along_axis)/gather | solution.py:56
  54.6 1.9 %gather_fusion.1 = bf16[16,3,128,128]{2,3,1,0:T(8,128)(2,1)} fusion(bf16[22,3,128,128]{2,3,1,0:T(8,128)(2,1)S(1)} %maximum_bitcast_fusion, s32[1024]{0:T(1024)S(1)} %get-tuple-element.634), kind=kCustom, calls=%fused_computation.2.clone | custom fusion | bytes 3145792 | tf_op jit(solution)/shard_map/jit(take_along_axis)/gather | solution.py:56
  56.5 1.9 %gather_fusion.2 = bf16[16,3,128,128]{2,3,1,0:T(8,128)(2,1)} fusion(bf16[22,3,128,128]{2,3,1,0:T(8,128)(2,1)S(1)} %maximum_bitcast_fusion, s32[1024]{0:T(1024)S(1)} %get-tuple-element.633), kind=kCustom, calls=%fused_computation.3.clone | custom fusion | bytes 3145792 | tf_op jit(solution)/shard_map/jit(take_along_axis)/gather | solution.py:56
  60.3 2.0 %gather_fusion.4 = bf16[16,3,128,128]{2,3,1,0:T(8,128)(2,1)} fusion(bf16[22,3,128,128]{2,3,1,0:T(8,128)(2,1)S(1)} %maximum_bitcast_fusion, s32[1024]{0:T(1024)S(1)} %get-tuple-element.631), kind=kCustom, calls=%fused_computation.5.clone | custom fusion | bytes 3145792 | tf_op jit(solution)/shard_map/jit(take_along_axis)/gather | solution.py:56
  62.3 2.1 %fusion.36 = f32[16,3,128,128]{3,2,1,0:T(8,128)S(1)} fusion(bf16[16,3,128,128]{2,3,1,0:T(8,128)(2,1)} %gather_fusion, pred[16]{0:T(512)(128)(4,1)S(1)} %get-tuple-element.550, bf16[1,16,5,128,128]{4,3,2,1,0:T(8,128)(2,1)} %param.94), kind=kOutput, calls=%fused_computation.85 | convolution fusion | flops 202113024 | bytes 5242896 | tf_op jit(solution)/shard_map/arij,arcjl->arcil/dot_general | solution.py:57
  86.6 7.2 %collective-permute-start.3 = (bf16[1,4,8,128,128]{3,4,2,1,0:T(8,128)(2,1)}, bf16[1,4,8,128,128]{3,4,2,1,0:T(8,128)(2,1)}, u32[]{:S(2)}, u32[]{:S(2)}) collective-permute-start(bf16[1,4,8,128,128]{3,4,2,1,0:T(8,128)(2,1)} %get-tuple-element.525), channel_id=1, source_target_pairs={{1,0},{2,1},{3,2},{4,3},{5,4},{6,5},{7,6},{8,7},{9,8},{10,9},{11,1... | collective-permute-start | bytes 3145736 | tf_op jit(solution)/shard_map/ppermute | solution.py:21
  99.3 2.2 %maximum_bitcast_fusion.1 = bf16[10,3,128,128]{3,2,0,1:T(8,128)(2,1)} fusion(bf16[1,3,3,128,128]{4,3,1,2,0:T(8,128)(2,1)} %collective-permute-done.5, bf16[1,4,1,128,128]{4,3,1,2,0:T(8,128)(2,1)S(1)} %get-tuple-element.537, bf16[1,4,1,128,128]{4,3,1,2,0:T(8,128)(2,1)S(1)} %slice_bitcast_fusion.20, bf16[1,4,1,128,128]{4,3,1,2,0:T(8,128)(2,1)S(1)} %get-tuple-element.536, ...), kind=kLoop, calls=%fused_computation.105 | loop fusion | flops 1966080 | bytes 1966080 | tf_op jit(solution)/shard_map/jit(take_along_axis)/Arg_0.37 | solution.py:56
  101.5 2.5 %gather_fusion.5 = bf16[4,3,128,128]{3,2,1,0:T(8,128)(2,1)} fusion(bf16[10,3,128,128]{3,2,0,1:T(8,128)(2,1)} %maximum_bitcast_fusion.1, s32[1024]{0:T(1024)S(1)} %pad_clamp_fusion.6), kind=kCustom, calls=%fused_computation.1.clone | custom fusion | bytes 786448 | tf_op jit(solution)/shard_map/jit(take_along_axis)/gather | solution.py:56
  104.0 2.6 %gather_fusion.6 = bf16[4,3,128,128]{3,2,1,0:T(8,128)(2,1)} fusion(bf16[10,3,128,128]{3,2,0,1:T(8,128)(2,1)} %maximum_bitcast_fusion.1, s32[1024]{0:T(1024)S(1)} %pad_clamp_fusion.5), kind=kCustom, calls=%fused_computation.6.clone | custom fusion | bytes 786448 | tf_op jit(solution)/shard_map/jit(take_along_axis)/gather | solution.py:56
  106.6 2.6 %gather_fusion.7 = bf16[4,3,128,128]{3,2,1,0:T(8,128)(2,1)} fusion(bf16[10,3,128,128]{3,2,0,1:T(8,128)(2,1)} %maximum_bitcast_fusion.1, s32[1024]{0:T(1024)S(1)} %pad_clamp_fusion.4), kind=kCustom, calls=%fused_computation.7.clone | custom fusion | bytes 786448 | tf_op jit(solution)/shard_map/jit(take_along_axis)/gather | solution.py:56
  109.3 2.6 %gather_fusion.8 = bf16[4,3,128,128]{3,2,1,0:T(8,128)(2,1)} fusion(bf16[10,3,128,128]{3,2,0,1:T(8,128)(2,1)} %maximum_bitcast_fusion.1, s32[1024]{0:T(1024)S(1)} %pad_clamp_fusion.3), kind=kCustom, calls=%fused_computation.8.clone | custom fusion | bytes 786448 | tf_op jit(solution)/shard_map/jit(take_along_axis)/gather | solution.py:56
  111.8 2.7 %gather_fusion.9 = bf16[4,3,128,128]{3,2,1,0:T(8,128)(2,1)} fusion(bf16[10,3,128,128]{3,2,0,1:T(8,128)(2,1)} %maximum_bitcast_fusion.1, s32[1024]{0:T(1024)} %pad_clamp_fusion.2), kind=kCustom, calls=%fused_computation.9.clone | custom fusion | bytes 786448 | tf_op jit(solution)/shard_map/jit(take_along_axis)/gather | solution.py:56
  114.5 2.7 %gather_fusion.10 = bf16[4,3,128,128]{3,2,1,0:T(8,128)(2,1)} fusion(bf16[10,3,128,128]{3,2,0,1:T(8,128)(2,1)} %maximum_bitcast_fusion.1, s32[1024]{0:T(1024)} %pad_clamp_fusion.1), kind=kCustom, calls=%fused_computation.10.clone | custom fusion | bytes 786448 | tf_op jit(solution)/shard_map/jit(take_along_axis)/gather | solution.py:56
  117.2 2.7 %gather_fusion.11 = bf16[4,3,128,128]{3,2,1,0:T(8,128)(2,1)} fusion(bf16[10,3,128,128]{3,2,0,1:T(8,128)(2,1)} %maximum_bitcast_fusion.1, s32[1024]{0:T(1024)} %pad_clamp_fusion), kind=kCustom, calls=%fused_computation.11.clone | custom fusion | bytes 786448 | tf_op jit(solution)/shard_map/jit(take_along_axis)/gather | solution.py:56
  119.9 3.5 %pad_maximum_fusion = bf16[1,24,8,128,128]{3,4,2,1,0:T(8,128)(2,1)S(1)} fusion(bf16[1,4,8,128,128]{3,4,2,1,0:T(8,128)(2,1)} %collective-permute-done.3, bf16[1,16,1,128,128]{3,4,2,1,0:T(8,128)(2,1)} %copy-done.3, bf16[1,16,1,128,128]{3,4,2,1,0:T(8,128)(2,1)S(1)} %copy.85, bf16[1,16,1,128,128]{3,4,2,1,0:T(8,128)(2,1)} %copy-done, ...), kind=kLoop, calls=%fused_computation.12 | loop fusion | flops 15728640 | bytes 12582912 | tf_op jit(solution)/shard_map/concatenate | solution.py:34
  126.1 2.2 %fusion.17 = f32[1,6,3,5,128,128]{4,5,2,3,1,0:T(8,128)S(1)} fusion(bf16[6,4,5,128,128,1]{3,4,2,1,0,5:T(8,128)(2,1)S(1)} %bitcast.618, bf16[6,4,3,128,128,1]{3,4,2,1,0,5:T(8,128)(2,1)S(1)} %bitcast.619), kind=kOutput, calls=%fused_computation.59 | convolution fusion | flops 1509949440 | bytes 12189696 | tf_op jit(solution)/shard_map/agmcij,agmsil->agcsjl/dot_general | solution.py:76
  128.7 2.2 %fusion.27 = f32[1,8,7,128,128]{3,4,2,1,0:T(8,128)S(1)} fusion(f32[1,8,7,128,128]{3,4,2,1,0:T(8,128)S(1)} %broadcast_in_dim.381, s32[]{:T(128)} %bitcast.80, s32[]{:T(128)} %bitcast.81, f32[1,6,3,5,128,128]{4,5,2,3,1,0:T(8,128)S(1)} %fusion.17, pred[]{:T(512)} %and_reduce_fusion), kind=kLoop, calls=%fused_computation.72 | loop fusion | flops 491520 | bytes 3932169 | tf_op jit(solution)/shard_map/scatter-add | solution.py:83
  143.9 1.9 %fusion.102 = f32[1,3,7,128,128]{3,4,2,1,0:T(8,128)S(1)} fusion(f32[1,3,7,128,128]{3,4,2,1,0:T(8,128)S(1)} %broadcast_in_dim.400, s32[]{:T(128)} %bitcast.80, s32[]{:T(128)} %bitcast.81, f32[1,1,3,5,128,128]{4,5,2,3,1,0:T(8,128)S(1)} %convolution_bitcast_fusion, pred[]{:T(512)} %and_reduce_fusion), kind=kLoop, calls=%fused_computation.201 | loop fusion | flops 81920 | bytes 655369 | tf_op jit(solution)/shard_map/scatter-add | solution.py:83
  146.9 7.2 %collective-permute-start.7 = (bf16[1,1,7,128,128]{3,4,2,1,0:T(8,128)(2,1)S(1)}, bf16[1,1,7,128,128]{3,4,2,1,0:T(8,128)(2,1)}, u32[]{:S(2)}, u32[]{:S(2)}) collective-permute-start(bf16[1,1,7,128,128]{3,4,2,1,0:T(8,128)(2,1)S(1)} %get-tuple-element.531), channel_id=1, source_target_pairs={{1,0},{2,1},{3,2},{4,3},{5,4},{6,5},{7,6},{8,7},{9,8},{10,9},{11,1... | collective-permute-start | bytes 688136 | tf_op jit(solution)/shard_map/ppermute | solution.py:21
  155.4 2.6 %collective-permute-done.6 = bf16[1,1,7,128,128]{3,4,2,1,0:T(8,128)(2,1)S(1)} collective-permute-done((bf16[1,1,7,128,128]{3,4,2,1,0:T(8,128)(2,1)}, bf16[1,1,7,128,128]{3,4,2,1,0:T(8,128)(2,1)S(1)}, u32[]{:S(2)}, u32[]{:S(2)}) %collective-permute-start.6) | collective-permute-done | bytes 229408 | tf_op jit(solution)/shard_map/ppermute | solution.py:18
  (223 shorter events, 68.0 us)
Async XLA Ops:
  3.8 8.9 %copy-start.48 = (s32[1,4,2]{1,2,0:T(2,128)S(1)}, s32[1,4,2]{1,2,0:T(2,128)}, u32[]{:S(2)}) copy-start(s32[1,4,2]{1,2,0:T(2,128)} %param.99) | copy-start | bytes 100
  3.8 9.0 %copy-start.18 = (bf16[1,4,2,128,128]{4,3,2,1,0:T(8,128)(2,1)S(1)}, bf16[1,4,2,128,128]{4,3,2,1,0:T(8,128)(2,1)}, u32[]{:S(2)}) copy-start(bf16[1,4,2,128,128]{4,3,2,1,0:T(8,128)(2,1)} %param.98) | copy-start | bytes 786436
  4.2 47.9 %copy-start = (bf16[1,16,1,128,128]{3,4,2,1,0:T(8,128)(2,1)}, bf16[1,16,1,128,128]{3,4,2,1,0:T(8,128)(2,1)S(1)}, u32[]{:S(2)}) copy-start(bf16[1,16,1,128,128]{3,4,2,1,0:T(8,128)(2,1)S(1)} %get-tuple-element.532) | copy-start | bytes 1572868
  4.2 47.9 %copy-start.3 = (bf16[1,16,1,128,128]{3,4,2,1,0:T(8,128)(2,1)}, bf16[1,16,1,128,128]{3,4,2,1,0:T(8,128)(2,1)S(1)}, u32[]{:S(2)}) copy-start(bf16[1,16,1,128,128]{3,4,2,1,0:T(8,128)(2,1)S(1)} %get-tuple-element.533) | copy-start | bytes 1572868
  4.3 47.8 %collective-permute-start = (bf16[1,3,3,128,128]{3,4,2,1,0:T(8,128)(2,1)S(1)}, bf16[1,3,3,128,128]{3,4,2,1,0:T(8,128)(2,1)S(1)}, u32[]{:S(2)}, u32[]{:S(2)}) collective-permute-start(bf16[1,3,3,128,128]{3,4,2,1,0:T(8,128)(2,1)S(1)} %get-tuple-element.526), channel_id=1, source_target_pairs={{0,1},{1,2},{2,3},{3,4},{4,5},{5,6},{6,7},{7,8},{8,9},{9,10},{10,1... | collective-permute-start | bytes 884744 | tf_op jit(solution)/shard_map/ppermute | solution.py:18
  6.0 46.1 %collective-permute-start.1 = (bf16[1,3,3,128,128]{3,4,2,1,0:T(8,128)(2,1)S(1)}, bf16[1,3,3,128,128]{3,4,2,1,0:T(8,128)(2,1)S(1)}, u32[]{:S(2)}, u32[]{:S(2)}) collective-permute-start(bf16[1,3,3,128,128]{3,4,2,1,0:T(8,128)(2,1)S(1)} %get-tuple-element.527), channel_id=1, source_target_pairs={{1,0},{2,1},{3,2},{4,3},{5,4},{6,5},{7,6},{8,7},{9,8},{10,9},{11,1... | collective-permute-start | bytes 884744 | tf_op jit(solution)/shard_map/ppermute | solution.py:21
  13.8 85.5 %collective-permute-start.4 = (bf16[1,3,3,128,128]{4,3,1,2,0:T(8,128)(2,1)}, bf16[1,3,3,128,128]{4,3,1,2,0:T(8,128)(2,1)}, u32[]{:S(2)}, u32[]{:S(2)}) collective-permute-start(bf16[1,3,3,128,128]{4,3,1,2,0:T(8,128)(2,1)} %get-tuple-element.534), channel_id=1, source_target_pairs={{0,1},{1,2},{2,3},{3,4},{4,5},{5,6},{6,7},{7,8},{8,9},{9,10},{10,1... | collective-permute-start | bytes 884744 | tf_op jit(solution)/shard_map/ppermute | solution.py:18
  13.8 85.5 %collective-permute-start.5 = (bf16[1,3,3,128,128]{4,3,1,2,0:T(8,128)(2,1)}, bf16[1,3,3,128,128]{4,3,1,2,0:T(8,128)(2,1)}, u32[]{:S(2)}, u32[]{:S(2)}) collective-permute-start(bf16[1,3,3,128,128]{4,3,1,2,0:T(8,128)(2,1)} %get-tuple-element.535), channel_id=1, source_target_pairs={{1,0},{2,1},{3,2},{4,3},{5,4},{6,5},{7,6},{8,7},{9,8},{10,9},{11,1... | collective-permute-start | bytes 884744 | tf_op jit(solution)/shard_map/ppermute | solution.py:21
  66.4 1.4 copy-start.9
  66.4 2.2 %copy-start.10 = (bf16[1,16,5,128,128]{4,3,2,1,0:T(8,128)(2,1)S(1)}, bf16[1,16,5,128,128]{4,3,2,1,0:T(8,128)(2,1)}, u32[]{:S(2)}) copy-start(bf16[1,16,5,128,128]{4,3,2,1,0:T(8,128)(2,1)} %param.94) | copy-start | bytes 7864324
  71.1 1.4 copy-start.8
  74.9 1.4 copy-start.7
  79.0 1.4 copy-start.6
  83.7 1.0 copy-start.1
  83.7 1.2 copy-start.4
  84.9 10.0 %copy-start.33 = (s32[4]{0:T(128)S(1)}, s32[4]{0:T(128)}, u32[]{:S(2)}) copy-start(s32[4]{0:T(128)} %get-tuple-element.623) | copy-start | bytes 52
  84.9 10.0 %copy-start.32 = (s32[4]{0:T(128)S(1)}, s32[4]{0:T(128)}, u32[]{:S(2)}) copy-start(s32[4]{0:T(128)} %get-tuple-element.624) | copy-start | bytes 52
  84.9 10.6 %copy-start.35 = (s32[4]{0:T(128)S(1)}, s32[4]{0:T(128)}, u32[]{:S(2)}) copy-start(s32[4]{0:T(128)} %get-tuple-element.625) | copy-start | bytes 52
  84.9 11.2 %copy-start.34 = (s32[4]{0:T(128)S(1)}, s32[4]{0:T(128)}, u32[]{:S(2)}) copy-start(s32[4]{0:T(128)} %get-tuple-element.626) | copy-start | bytes 52
  85.0 13.0 %copy-start.19 = (s32[2]{0:T(128)S(1)}, s32[2]{0:T(128)}, u32[]{:S(2)}) copy-start(s32[2]{0:T(128)} %iota_multiply_fusion) | copy-start | bytes 28
  85.0 13.6 %copy-start.53 = (s32[5]{0:T(128)S(1)}, s32[5]{0:T(128)}, u32[]{:S(2)}) copy-start(s32[5]{0:T(128)} %constant.1176.clone.1) | copy-start | bytes 64
  86.6 33.3 %collective-permute-start.2 = (bf16[1,4,8,128,128]{3,4,2,1,0:T(8,128)(2,1)}, bf16[1,4,8,128,128]{3,4,2,1,0:T(8,128)(2,1)}, u32[]{:S(2)}, u32[]{:S(2)}) collective-permute-start(bf16[1,4,8,128,128]{3,4,2,1,0:T(8,128)(2,1)} %get-tuple-element.524), channel_id=1, source_target_pairs={{0,1},{1,2},{2,3},{3,4},{4,5},{5,6},{6,7},{7,8},{8,9},{9,10},{10,1... | collective-permute-start | bytes 3145736 | tf_op jit(solution)/shard_map/ppermute | solution.py:18
  86.6 33.3 %collective-permute-start.3 = (bf16[1,4,8,128,128]{3,4,2,1,0:T(8,128)(2,1)}, bf16[1,4,8,128,128]{3,4,2,1,0:T(8,128)(2,1)}, u32[]{:S(2)}, u32[]{:S(2)}) collective-permute-start(bf16[1,4,8,128,128]{3,4,2,1,0:T(8,128)(2,1)} %get-tuple-element.525), channel_id=1, source_target_pairs={{1,0},{2,1},{3,2},{4,3},{5,4},{6,5},{7,6},{8,7},{9,8},{10,9},{11,1... | collective-permute-start | bytes 3145736 | tf_op jit(solution)/shard_map/ppermute | solution.py:21
  123.4 1.2 copy-start.5
  131.9 1.4 copy-start.31
  135.4 1.3 copy-start.26
  136.9 1.3 copy-start.24
  138.5 1.3 copy-start.22
  140.0 1.3 copy-start.21
  141.5 1.3 copy-start.50
  146.9 11.1 %collective-permute-start.6 = (bf16[1,1,7,128,128]{3,4,2,1,0:T(8,128)(2,1)}, bf16[1,1,7,128,128]{3,4,2,1,0:T(8,128)(2,1)S(1)}, u32[]{:S(2)}, u32[]{:S(2)}) collective-permute-start(bf16[1,1,7,128,128]{3,4,2,1,0:T(8,128)(2,1)} %get-tuple-element.530), channel_id=1, source_target_pairs={{0,1},{1,2},{2,3},{3,4},{4,5},{5,6},{6,7},{7,8},{8,9},{9,10},{10,1... | collective-permute-start | bytes 688136 | tf_op jit(solution)/shard_map/ppermute | solution.py:18
  146.9 11.1 %collective-permute-start.7 = (bf16[1,1,7,128,128]{3,4,2,1,0:T(8,128)(2,1)S(1)}, bf16[1,1,7,128,128]{3,4,2,1,0:T(8,128)(2,1)}, u32[]{:S(2)}, u32[]{:S(2)}) collective-permute-start(bf16[1,1,7,128,128]{3,4,2,1,0:T(8,128)(2,1)S(1)} %get-tuple-element.531), channel_id=1, source_target_pairs={{1,0},{2,1},{3,2},{4,3},{5,4},{6,5},{7,6},{8,7},{9,8},{10,9},{11,1... | collective-permute-start | bytes 688136 | tf_op jit(solution)/shard_map/ppermute | solution.py:21
  (30 other events, 27.8 us)
where the time goes:
time: 161 us; the launch traced here: 160 us
  other arithmetic  65.9 us (41%)
  local copies, waits for them, and re-layouts  45 us (28%)
  starting transfers between devices  29.9 us (19%)
  matrix products  14.6 us (9%)
  waiting for transfers between devices  2.59 us (2%)
  between operations  1.72 us (1%)
    ppermute x4, starting transfers between devices, with_halo(): lax.ppermute(lax.slice_in_dim(block, 0, width, axis=dim), axis, backward)  28.2 us
    gather x12, local copies, waits for them, and re-layouts, row_products(): jnp.take_along_axis(extended, (shifted + HALF)[:, :, None, None, None], a...  28 us
    eq x15, other arithmetic, row_products(): coarse_step == offset  19.5 us
    dot_general x12, matrix products, row_products(): jnp.einsum('arij,arcjl->arcil', a_vals[:, :, column], picked, preferred_e...  11.9 us
    scatter-add x24, other arithmetic, row_products(): accumulated = accumulated.at[:, :, offset + 1:offset + 4].add(selected)  11.8 us
    unnamed x113, local copies, waits for them, and re-layouts  11.1 us
    and x5, other arithmetic, row_products(): jnp.take_along_axis(extended, (shifted + HALF)[:, :, None, None, None], a...  6.77 us
    reshape x5, other arithmetic, row_products(): jnp.take_along_axis(extended, (shifted + HALF)[:, :, None, None, None], a...  5.77 us
  transfers between devices with their start and end apart: 8, of which 1 were waited for; matrix products, arithmetic and copies ran while one was open for 56% of the time, Pallas kernels for 0%

commit v1 on v0

v1 whole, which is shorter than its diff:
```python
import jax
import jax.numpy as jnp
from jax import lax
from jax.experimental import pallas as pl
from jax.experimental.pallas import tpu as pltpu
from jax.sharding import PartitionSpec as P

B = 128
K = 5
KC = 7
ROWS = 16
CROWS = 4
BF = jnp.bfloat16
F32 = jnp.float32
PM = 6 * B + 16
QM = 4 * B + 16
AXES = ("gx", "gy")


def blk(i, n=1):
    return pl.ds(i * B, n * B)


def side_at(cols, r, ncoarse):
    return lax.rem(cols[r, 1] - cols[r, 0] + 1 + ncoarse, ncoarse) - 1


def dot(a, b):
    return jnp.dot(a, b, preferred_element_type=F32)


def dot_t(a, b):
    return lax.dot_general(a, b, (((0,), (0,)), ((), ())), preferred_element_type=F32)


def pack_kernel(ncoarse, ncoarsest, p_cols, p2_cols, p_hbm, p2_hbm, pa, pb, qa, qb, sems):
    odd = p2_cols[0, 0] % 2
    jobs = []
    for n, (dst, flip) in enumerate(((pa, 0), (pb, 1), (qa, 0), (qb, 1))):
        high = (odd == flip).astype(jnp.int32)
        if n < 2:
            start, rows, src, cols, ncols = high * (ROWS - 3), 3, p_hbm, p_cols, ncoarse
        else:
            start, rows, src, cols, ncols = high * (CROWS - 2), 2, p2_hbm, p2_cols, ncoarsest
        size = rows * 2 * B
        copy = pltpu.make_async_copy(
            src.at[pl.ds(pl.multiple_of(start * 2 * B, 2 * B), size)], dst.at[pl.ds(0, size)], sems.at[n]
        )
        copy.start()
        jobs.append((copy, dst, start, rows, cols, ncols, size))
    row = lax.broadcasted_iota(jnp.int32, (16, B), 0)
    for copy, dst, start, rows, cols, ncols, size in jobs:
        flags = jnp.zeros((16, B), F32)
        for r in range(rows):
            side = side_at(cols, start + r, ncols)
            flags = jnp.where(row == 2 * r, (side < 0).astype(F32), flags)
            flags = jnp.where(row == 2 * r + 1, (side > 0).astype(F32), flags)
        copy.wait()
        dst[pl.ds(size, 16), :] = flags.astype(BF)


def bands_of(p_ref, cols, rows, ncoarse):
    out = []
    for r in rows:
        side = side_at(cols, r, ncoarse)
        p0 = p_ref[blk(2 * r), :]
        p1 = p_ref[blk(2 * r + 1), :]
        zero = jnp.zeros_like(p1)
        out.append((jnp.where(side < 0, p1, zero), p0, jnp.where(side > 0, p1, zero)))
    return out


def halo_bands(low, high, is_low, rows, size):
    def pick(start, n):
        return jnp.where(is_low, low[pl.ds(start, n), :], high[pl.ds(start, n), :])

    flags = pick(size, 16).astype(F32)
    out = []
    for r in range(rows):
        p0 = pick(2 * r * B, B)
        p1 = pick((2 * r + 1) * B, B)
        lower = jnp.broadcast_to(flags[2 * r : 2 * r + 1, :], (B, B)).astype(BF)
        upper = jnp.broadcast_to(flags[2 * r + 1 : 2 * r + 2, :], (B, B)).astype(BF)
        out.append((p1 * lower, p0, p1 * upper))
    return out


def stack_bands(bands):
    return jnp.concatenate([jnp.concatenate(band, axis=1) for band in bands], axis=0)


def inner_kernel(nfine, ncoarse, a_cols, p_cols, a_ref, p_ref, acc_out, part_out, acc, prod):
    base = a_cols[0, 0]
    edge = {0: 0, 1: 1, 2: 2, 3: 3, 12: 4, 13: 5, 14: 6, 15: 7}
    for g in (0, 3, 1, 2):
        for r in range(4 * g, 4 * g + 4):
            acc[...] = jnp.zeros_like(acc)
            for k in range(K):
                shift = lax.rem(a_cols[r, k] - (base + r) + 3 + nfine, nfine) - 3
                v = r + shift
                inside = jnp.logical_and(v >= 0, v < ROWS)
                v = jnp.clip(v, 0, ROWS - 1)
                side = side_at(p_cols, v, ncoarse)
                slot0 = jnp.where(inside, v // 4 - g + 2, 6)
                slot1 = slot0 + side
                w0 = p_ref[pl.ds(pl.multiple_of(v * 2 * B, 2 * B), B), :]
                w1 = p_ref[pl.ds(pl.multiple_of(v * 2 * B + B, B), B), :]
                terms = dot(a_ref[blk(r * K + k), :], jnp.concatenate([w0, w1], axis=1))
                acc[slot0] += terms[:, :B]
                acc[slot1] += terms[:, B:]
            for s in range(5):
                if r in edge or r in (4, 5, 6, 7, 8, 9, 10, 11):
                    pass
                if g in (0, 3):
                    acc_out[4 * (g // 3) + r % 4, :, s * B : (s + 1) * B] = acc[s]
                else:
                    prod[blk(r - 4), s * B : (s + 1) * B] = acc[s].astype(BF)
    part_out[...] = jnp.zeros_like(part_out)
    for g in (1, 2):
        bands = stack_bands(bands_of(p_ref, p_cols, range(4 * g, 4 * g + 4), ncoarse))
        terms = dot_t(bands, prod[blk(4 * (g - 1), 4), :])
        for m in range(3):
            at = slice((g - 1) * B, (g + 4) * B)
            part_out[g - 1 + m, :, at] = part_out[g - 1 + m, :, at] + terms[m * B : (m + 1) * B, :]


def outer_kernel(
    nfine, ncoarse, ncoarsest, a_cols, p_cols, p2_cols, a_ref, p_ref, p2_ref, acc_in, part_in,
    pa, pb, qa, qb, coarse_out, rim_out, fine_out, ma, mb, na, nb, prod, part, cp,
):
    base = a_cols[0, 0]
    d = p2_cols[0, 0]
    even = d % 2 == 0
    for g in (0, 3):
        for m in range(4):
            for s in range(5):
                pass
    for side in (0, 1):
        first = 0 if side == 0 else ROWS - 3
        bands = stack_bands(
            halo_bands(pb, pa, even, 3, 6 * B) if side == 0 else halo_bands(pa, pb, even, 3, 6 * B)
        )
        rows = []
        for r in range(first, first + 3):
            line = []
            for h in range(3):
                v = h - 3 if side == 0 else ROWS + h
                want = v - r
                if abs(want) > 3:
                    line.append(jnp.zeros((B, B), BF))
                    continue
                at = jnp.int32(0)
                found = jnp.int32(0)
                for k in range(1, K):
                    shift = lax.rem(a_cols[r, k] - (base + r) + 3 + nfine, nfine) - 3
                    hit = (shift == want).astype(jnp.int32)
                    at = at + hit * k
                    found = found + hit
                block = a_ref[pl.ds(pl.multiple_of((r * K + at) * B, B), B), :]
                line.append(jnp.where(found > 0, block, jnp.zeros_like(block)))
            rows.append(jnp.concatenate(line, axis=1))
        terms = dot(jnp.concatenate(rows, axis=0), bands)
        for n in range(4):
            r = 4 * side + n
            q = n if side == 0 else n - 1
            for s in range(5):
                value = acc_in[r, :, s * B : (s + 1) * B]
                lane = s if side == 0 else s - 2
                if 0 <= lane < 3 and 0 <= q < 3:
                    value = value + terms[q * B : (q + 1) * B, lane * B : (lane + 1) * B]
                prod[blk(r), s * B : (s + 1) * B] = value.astype(BF)
    part[...] = jnp.zeros_like(part)
    for j in range(4):
        part[j + 1, :, B : 7 * B] = part_in[j]
    for g in (0, 3):
        bands = stack_bands(bands_of(p_ref, p_cols, range(4 * g, 4 * g + 4), ncoarse))
        terms = dot_t(bands, prod[blk(4 * (g // 3), 4), :])
        for m in range(3):
            at = slice(g * B, (g + 5) * B)
            part[g + m, :, at] = part[g + m, :, at] + terms[m * B : (m + 1) * B, :]
    for j in range(4):
        for t in range(KC):
            q = t + j - 1
            if 0 <= q < 8:
                coarse_out[blk(j * KC + t), :] = part[j + 1, :, q * B : (q + 1) * B].astype(BF)
            else:
                coarse_out[blk(j * KC + t), :] = jnp.zeros((B, B), BF)
    for t in range(5):
        rim_out[blk(t), :] = part[1, :, (t - 1) * B : t * B] if t > 0 else jnp.zeros((B, B), F32)
        q = t + 4
        rim_out[blk(5 + t), :] = part[4, :, q * B : (q + 1) * B] if q < 8 else jnp.zeros((B, B), F32)
    low = halo_bands(qb, qa, even, 2, 4 * B)
    high = halo_bands(qa, qb, even, 2, 4 * B)
    own = bands_of(p2_ref, p2_cols, range(4), ncoarsest)
    lines = part[...].astype(BF).reshape(6 * B, 8 * B)
    ta = dot(lines[0 : 4 * B, 0 : 2 * B], stack_bands(low))
    tb = dot(lines[:, 2 * B : 6 * B], stack_bands(own))
    tc = dot(lines[2 * B : 6 * B, 6 * B : 8 * B], stack_bands(high))
    for e in range(5):
        total = [None] * 6
        for i in range(6):
            pieces = []
            if e < 3 and i < 4:
                pieces.append(ta[i * B : (i + 1) * B, e * B : (e + 1) * B])
            if 1 <= e < 4:
                pieces.append(tb[i * B : (i + 1) * B, (e - 1) * B : e * B])
            if e >= 2 and i >= 2:
                pieces.append(tc[(i - 2) * B : (i - 1) * B, (e - 2) * B : (e - 1) * B])
            value = sum(pieces[1:], pieces[0]) if pieces else jnp.zeros((B, B), F32)
            cp[blk(i), e * B : (e + 1) * B] = value.astype(BF)
    gm = dot_t(stack_bands(low[1:2]), cp[blk(0), :])
    g0 = dot_t(stack_bands(own), cp[blk(1, 4), :])
    gp = dot_t(stack_bands(high[0:1]), cp[blk(5), :])

    def row(x, m):
        return x[m * B : (m + 1) * B, :]

    fine_out[...] = row(gm, 2) + row(g0, 1) + row(gp, 0)
    to_low = (row(gm, 1) + row(g0, 0)).astype(BF)
    to_high = (row(g0, 2) + row(gp, 1)).astype(BF)
    two_low = row(gm, 0).astype(BF)
    two_high = row(gp, 2).astype(BF)

    def put(dst, coarse_row, q0, fine):
        for t in range(5):
            dst[blk(t), :] = part[coarse_row, :, (q0 + t) * B : (q0 + t + 1) * B].astype(BF)
            dst[blk(5 + t), :] = fine[:, t * B : (t + 1) * B]

    def put2(dst, fine, e0):
        for t in range(4):
            dst[blk(t), :] = fine[:, (e0 + t) * B : (e0 + t + 1) * B]

    @pl.when(even)
    def _():
        put(mb, 0, 0, to_low)
        put(ma, 5, 3, to_high)

    @pl.when(jnp.logical_not(even))
    def _():
        put(ma, 0, 0, to_low)
        put(mb, 5, 3, to_high)

    even2 = (d // 2) % 2 == 0

    @pl.when(even2)
    def _():
        put2(nb, two_low, 0)
        put2(na, two_high, 1)

    @pl.when(jnp.logical_not(even2))
    def _():
        put2(na, two_low, 0)
        put2(nb, two_high, 1)


def last_kernel(p2_cols, coarse_in, rim, fine, ma, mb, na, nb, coarse_out, coarsest_out, rows, sems):
    d = p2_cols[0, 0]
    even = d % 2 == 0
    even2 = (d // 2) % 2 == 0

    def one(low, t):
        if low:
            return jnp.where(even, mb[blk(t), :], ma[blk(t), :]).astype(F32)
        return jnp.where(even, ma[blk(t), :], mb[blk(t), :]).astype(F32)

    def two(low, t):
        if low:
            return jnp.where(even2, nb[blk(t), :], na[blk(t), :]).astype(F32)
        return jnp.where(even2, na[blk(t), :], nb[blk(t), :]).astype(F32)

    for t in range(5):
        rows[blk(t), :] = (rim[blk(t), :] + one(True, t)).astype(BF)
        rows[blk(5 + t), :] = (rim[blk(5 + t), :] + one(False, t)).astype(BF)
    copies = [
        pltpu.make_async_copy(rows.at[blk(0, 5)], coarse_out.at[blk(0, 5)], sems.at[0]),
        pltpu.make_async_copy(rows.at[blk(5, 5)], coarse_out.at[blk(3 * KC + 2, 5)], sems.at[1]),
    ]
    for copy in copies:
        copy.start()
    for t in range(KC):
        value = jnp.zeros((B, B), F32)
        if 1 <= t < 6:
            value = value + fine[:, (t - 1) * B : t * B]
        if t < 5:
            value = value + one(True, 5 + t)
        if t >= 2:
            value = value + one(False, 5 + t - 2)
        if t < 4:
            value = value + two(True, t)
        if t >= 3:
            value = value + two(False, t - 3)
        coarsest_out[blk(t), :] = value.astype(BF)
    for copy in copies:
        copy.wait()


def call(kernel, ins, outs, args, scratch=(), cost=None, **kw):
    smem = pl.BlockSpec(memory_space=pltpu.SMEM)
    vmem = pl.BlockSpec(memory_space=pltpu.VMEM)
    anyspec = pl.BlockSpec(memory_space=pl.ANY)
    kinds = {"s": smem, "v": vmem, "a": anyspec}
    return pl.pallas_call(
        kernel,
        in_specs=[kinds[c] for c in ins],
        out_specs=tuple(kinds[c] for c, _, _ in outs),
        out_shape=tuple(jax.ShapeDtypeStruct(shape, dtype) for _, shape, dtype in outs),
        scratch_shapes=list(scratch),
        compiler_params=pltpu.CompilerParams(vmem_limit_bytes=40 * 1024 * 1024),
        cost_estimate=cost,
        **kw,
    )(*args)


def body(a_vals, a_cols, p_vals, p_cols, p2_vals, p2_cols):
    devices = lax.axis_size(AXES)
    nfine = ROWS * devices
    ncoarse = CROWS * devices
    a_cols = a_cols.reshape(ROWS, K)
    p_cols = p_cols.reshape(ROWS, 2)
    p2_cols = p2_cols.reshape(CROWS, 2)
    a = a_vals.reshape(ROWS * K * B, B)
    p = p_vals.reshape(ROWS * 2 * B, B)
    p2 = p2_vals.reshape(CROWS * 2 * B, B)
    swap_a = [(i, i ^ 1) for i in range(devices)]
    swap_b = [(i, (i + 1) % devices if i % 2 else (i - 1) % devices) for i in range(devices)]
    skip_a = [(i, i ^ 2) for i in range(devices)]
    skip_b = [(i, (i + 2) % devices if i & 2 else (i - 2) % devices) for i in range(devices)]

    def pack(*refs):
        pack_kernel(ncoarse, devices, *refs)

    pa, pb, qa, qb = call(
        pack,
        "ssaa",
        [("v", (PM, B), BF), ("v", (PM, B), BF), ("v", (QM, B), BF), ("v", (QM, B), BF)],
        (p_cols, p2_cols, p, p2),
        [pltpu.SemaphoreType.DMA((4,))],
    )
    pa = lax.ppermute(pa, AXES, swap_a)
    pb = lax.ppermute(pb, AXES, swap_b)
    qa = lax.ppermute(qa, AXES, swap_a)
    qb = lax.ppermute(qb, AXES, swap_b)

    def inner(*refs):
        inner_kernel(nfine, ncoarse, *refs)

    acc, part = call(
        inner,
        "ssvv",
        [("v", (8, B, 5 * B), F32), ("v", (4, B, 6 * B), F32)],
        (a_cols, p_cols, a, p),
        [pltpu.VMEM((8, B, B), F32), pltpu.VMEM((8 * B, 5 * B), BF)],
        pl.CostEstimate(flops=10**9, bytes_accessed=8 * 10**6, transcendentals=0),
    )

    def outer(*refs):
        outer_kernel(nfine, ncoarse, devices, *refs)

    coarse, rim, fine, ma, mb, na, nb = call(
        outer,
        "sssvvvvvvvvv",
        [
            ("v", (CROWS * KC * B, B), BF),
            ("v", (10 * B, B), F32),
            ("v", (B, 5 * B), F32),
            ("v", (10 * B, B), BF),
            ("v", (10 * B, B), BF),
            ("v", (4 * B, B), BF),
            ("v", (4 * B, B), BF),
        ],
        (a_cols, p_cols, p2_cols, a, p, p2, acc, part, pa, pb, qa, qb),
        [pltpu.VMEM((8 * B, 5 * B), BF), pltpu.VMEM((6, B, 8 * B), F32), pltpu.VMEM((6 * B, 5 * B), BF)],
        pl.CostEstimate(flops=2 * 10**9, bytes_accessed=8 * 10**6, transcendentals=0),
    )
    mb = lax.ppermute(mb, AXES, swap_b)
    nb = lax.ppermute(nb, AXES, skip_b)
    ma = lax.ppermute(ma, AXES, swap_a)
    na = lax.ppermute(na, AXES, skip_a)
    coarse, coarsest = call(
        last_kernel,
        "savvvvvv",
        [("a", (CROWS * KC * B, B), BF), ("v", (KC * B, B), BF)],
        (p2_cols, coarse, rim, fine, ma, mb, na, nb),
        [pltpu.VMEM((10 * B, B), BF), pltpu.SemaphoreType.DMA((2,))],
        input_output_aliases={1: 0},
    )
    return coarse.reshape(1, CROWS, KC, B, B), coarsest.reshape(1, 1, KC, B, B)


def solution(mesh):
    blocks = P(None, AXES, None, None, None)
    cols = P(None, AXES, None)
    return jax.shard_map(
        body,
        mesh=mesh,
        in_specs=(blocks, cols, blocks, cols, blocks, cols),
        out_specs=(blocks, blocks),
        check_vma=False,
    )
```

time: 161 us -> 51.5 us (0.32)
  other arithmetic: 65.9 us -> 0 us
  local copies, waits for them, and re-layouts: 45 us -> 7.42 us
  matrix products: 14.6 us -> 0 us
  starting transfers between devices: 29.9 us -> 16 us
  Pallas kernels: 0 us -> 12.6 us
  waiting for transfers between devices: 2.59 us -> 14.5 us
    gather x12 -> x0, local copies, waits for them, and re-layouts: 28 us -> none  [row_products(): jnp.take_along_axis(extended, (shifted + HALF)[:, :, None, None, None], a...]
    eq x15 -> x0, other arithmetic: 19.5 us -> none  [row_products(): coarse_step == offset]
    scatter-add x30 -> x0, other arithmetic: 17.1 us -> none  [the longest x24 11.8 us: row_products(): accumulated = accumulated.at[:, :, offset + 1:offset + 4].add(selected)]
    dot_general x14 -> x0, matrix products: 14.6 us -> none  [the longest x12 11.9 us: row_products(): jnp.einsum('arij,arcjl->arcil', a_vals[:, :, column], picked, preferred_e...]
    ppermute x8, starting transfers between devices: 29.9 us -> 16 us  [the longest x1 7.18 us: body(): pb = lax.ppermute(pb, AXES, swap_b)]
    pallas_call x0 -> x4, Pallas kernels: none -> 12.6 us  [call(): pl.pallas_call(kernel, in_specs=[kinds[c] for c in ins], out_specs=tuple(...]
    ppermute x8, waiting for transfers between devices: 2.59 us -> 14.5 us  [the longest x1 7.9 us: body(): nb = lax.ppermute(nb, AXES, skip_b)]
    and x5 -> x0, other arithmetic: 6.77 us -> none  [row_products(): jnp.take_along_axis(extended, (shifted + HALF)[:, :, None, None, None], a...]
  transfers between devices with their start and end apart: 8 -> 8, of which waited for: 1 -> 3; matrix products, arithmetic and copies ran while one was open for 56% -> 1% of each run, Pallas kernels for 0% -> 9%
where the time goes in v1:
time: 51.5 us; the launch traced here: 51.2 us
  starting transfers between devices  16 us (31%)
  waiting for transfers between devices  14.5 us (28%)
  Pallas kernels  12.6 us (24%)
  local copies, waits for them, and re-layouts  7.42 us (14%)
  between operations  0.67 us (1%)
    pallas_call x4, Pallas kernels, call(): pl.pallas_call(kernel, in_specs=[kinds[c] for c in ins], out_specs=tuple(...  12.6 us
    ppermute x1, waiting for transfers between devices, body(): nb = lax.ppermute(nb, AXES, skip_b)  7.9 us
    ppermute x1, starting transfers between devices, body(): pb = lax.ppermute(pb, AXES, swap_b)  7.18 us
    ppermute x1, waiting for transfers between devices, body(): na = lax.ppermute(na, AXES, skip_a)  5.29 us
    unnamed x10, local copies, waits for them, and re-layouts  5.14 us
    ppermute x1, starting transfers between devices, body(): mb = lax.ppermute(mb, AXES, swap_b)  5.02 us
    ppermute x1, starting transfers between devices, body(): pa = lax.ppermute(pa, AXES, swap_a)  1.68 us
    ppermute x1, waiting for transfers between devices, body(): qb = lax.ppermute(qb, AXES, swap_b)  1.27 us
  transfers between devices with their start and end apart: 8, of which 3 were waited for; matrix products, arithmetic and copies ran while one was open for 1% of the time, Pallas kernels for 9%

profile of v1, /device:TPU:0, one launch (start us, length us, event | category | flops | bytes accessed | tf_op | source)
XLA Modules:
  0.0 51.2 jit_solution(8862346870963521533)
XLA Ops:
  0.6 0.8 %copy.16.refs_1_.refs_2_.p2_cols = s32[4,2]{1,0:T(4,128)S(1)} copy(s32[4,2]{0,1:T(2,128)} %bitcast.18) | data formatting | bytes 64 | tf_op jit(solution)/shard_map/reshape | solution.py:320
  1.4 0.8 %copy.14.refs_1_.refs_0_ = s32[16,2]{1,0:T(8,128)S(1)} copy(s32[16,2]{0,1:T(2,128)} %bitcast.19) | data formatting | bytes 256 | tf_op jit(solution)/shard_map/reshape | solution.py:319
  2.2 0.0 copy-start
  2.2 1.2 %copy-done = bf16[1,16,2,128,128]{4,3,2,1,0:T(8,128)(2,1)S(1)} copy-done((bf16[1,16,2,128,128]{4,3,2,1,0:T(8,128)(2,1)S(1)}, bf16[1,16,2,128,128]{4,3,2,1,0:T(8,128)(2,1)}, u32[]{:S(2)}) %copy-start) | copy-done | bytes 1048600
  3.4 0.0 copy-start.3
  3.4 0.9 %copy-done.3 = bf16[1,4,2,128,128]{4,3,2,1,0:T(8,128)(2,1)S(1)} copy-done((bf16[1,4,2,128,128]{4,3,2,1,0:T(8,128)(2,1)S(1)}, bf16[1,4,2,128,128]{4,3,2,1,0:T(8,128)(2,1)}, u32[]{:S(2)}) %copy-start.3) | copy-done | bytes 262168
  4.3 0.0 copy-start.4
  4.3 1.7 %shard_map.78 = (bf16[784,128]{1,0:T(8,128)(2,1)S(1)}, bf16[784,128]{1,0:T(8,128)(2,1)S(1)}, bf16[528,128]{1,0:T(8,128)(2,1)S(1)}, bf16[528,128]{1,0:T(8,128)(2,1)S(1)}) custom-call(s32[16,2]{1,0:T(8,128)S(1)} %copy.14.refs_1_.refs_0_, s32[4,2]{1,0:T(4,128)S(1)} %copy.16.refs_1_.refs_2_.p2_cols, bf16[4096,128]{1,0:T(8,128)(2,1)S(1)} %bitcast.8, ...), custom_call_target="tpu_custom_call" | custom-call | tf_op jit(solution)/shard_map/pallas_call | solution.py:302
  6.0 1.7 %collective-permute-start = (bf16[784,128]{1,0:T(8,128)(2,1)S(1)}, bf16[784,128]{1,0:T(8,128)(2,1)S(1)}, u32[]{:S(2)}, u32[]{:S(2)}) collective-permute-start(bf16[784,128]{1,0:T(8,128)(2,1)S(1)} %get-tuple-element.19), channel_id=1, source_target_pairs={{0,1},{1,0},{2,3},{3,2},{4,5},{5,4},{6,7},{7,6},{8,9},{9,8},{10,11... | collective-permute-start | bytes 602120 | tf_op jit(solution)/shard_map/ppermute | solution.py:339
  7.7 7.2 %collective-permute-start.1 = (bf16[784,128]{1,0:T(8,128)(2,1)S(1)}, bf16[784,128]{1,0:T(8,128)(2,1)S(1)}, u32[]{:S(2)}, u32[]{:S(2)}) collective-permute-start(bf16[784,128]{1,0:T(8,128)(2,1)S(1)} %get-tuple-element.20), channel_id=1, source_target_pairs={{0,127},{1,2},{2,1},{3,4},{4,3},{5,6},{6,5},{7,8},{8,7},{9,10},{10... | collective-permute-start | bytes 602120 | tf_op jit(solution)/shard_map/ppermute | solution.py:340
  14.9 0.0 collective-permute-start.2
  14.9 0.9 %collective-permute-start.3 = (bf16[528,128]{1,0:T(8,128)(2,1)S(1)}, bf16[528,128]{1,0:T(8,128)(2,1)S(1)}, u32[]{:S(2)}, u32[]{:S(2)}) collective-permute-start(bf16[528,128]{1,0:T(8,128)(2,1)S(1)} %get-tuple-element.22), channel_id=1, source_target_pairs={{0,127},{1,2},{2,1},{3,4},{4,3},{5,6},{6,5},{7,8},{8,7},{9,10},{10... | collective-permute-start | bytes 405512 | tf_op jit(solution)/shard_map/ppermute | solution.py:342
  15.8 0.8 %copy.17 = s32[1,16,5]{2,1,0:T(8,128)S(1)} copy(s32[1,16,5]{1,0,2:T(1,128)} %param.7) | data formatting | bytes 640 | tf_op jit(solution)/shard_map/reshape | solution.py:318
  16.5 0.0 copy-start.1
  16.6 1.2 %copy-done.1 = bf16[1,16,2,128,128]{4,3,2,1,0:T(8,128)(2,1)S(1)} copy-done((bf16[1,16,2,128,128]{4,3,2,1,0:T(8,128)(2,1)S(1)}, bf16[1,16,2,128,128]{4,3,2,1,0:T(8,128)(2,1)}, u32[]{:S(2)}) %copy-start.1) | copy-done | bytes 1048600
  17.8 1.7 %copy-done.2 = bf16[1,16,5,128,128]{4,3,2,1,0:T(8,128)(2,1)S(1)} copy-done((bf16[1,16,5,128,128]{4,3,2,1,0:T(8,128)(2,1)S(1)}, bf16[1,16,5,128,128]{4,3,2,1,0:T(8,128)(2,1)}, u32[]{:S(2)}) %copy-start.2) | copy-done | bytes 2621464
  19.5 4.4 %shard_map.77 = (f32[8,128,640]{2,1,0:T(8,128)S(1)}, f32[4,128,768]{2,1,0:T(8,128)S(1)}) custom-call(s32[16,5]{1,0:T(8,128)S(1)} %bitcast.15, s32[16,2]{1,0:T(8,128)S(1)} %copy.14.refs_1_.refs_0_, bf16[10240,128]{1,0:T(8,128)(2,1)S(1)} %bitcast.11, bf16[4096,128]{1,0:T(8,128)(2,1)S(1)} %bitcast.9), custom_call_target="tpu_custom_call" | custom-call | flops 1000000000 | bytes 8000000 | tf_op jit(solution)/shard_map/pallas_call | solution.py:302
  23.9 0.0 collective-permute-done.2.refs_10_
  23.9 1.3 %collective-permute-done.3.refs_11_ = bf16[528,128]{1,0:T(8,128)(2,1)S(1)} collective-permute-done((bf16[528,128]{1,0:T(8,128)(2,1)S(1)}, bf16[528,128]{1,0:T(8,128)(2,1)S(1)}, u32[]{:S(2)}, u32[]{:S(2)}) %collective-permute-start.3) | collective-permute-done | bytes 135200 | tf_op jit(solution)/shard_map/ppermute | solution.py:342
  25.2 0.0 collective-permute-done.refs_8_
  25.2 0.0 collective-permute-done.1.refs_9_
  25.2 0.0 copy-done.4
  25.2 4.5 %shard_map.79 = (bf16[3584,128]{1,0:T(8,128)(2,1)}, f32[1280,128]{1,0:T(8,128)S(1)}, f32[128,640]{1,0:T(8,128)S(1)}, bf16[1280,128]{1,0:T(8,128)(2,1)S(1)}, bf16...) custom-call(s32[16,5]{1,0:T(8,128)S(1)} %bitcast.16, ...), custom_call_target="tpu_custom_call" | custom-call | flops 2000000000 | bytes 8000000 | tf_op jit(solution)/shard_map/pallas_call | solution.py:302
  29.7 0.0 collective-permute-start.4
  29.7 5.0 %collective-permute-start.5 = (bf16[1280,128]{1,0:T(8,128)(2,1)S(1)}, bf16[1280,128]{1,0:T(8,128)(2,1)S(1)}, u32[]{:S(2)}, u32[]{:S(2)}) collective-permute-start(bf16[1280,128]{1,0:T(8,128)(2,1)S(1)} %get-tuple-element.27), channel_id=1, source_target_pairs={{0,127},{1,2},{2,1},{3,4},{4,3},{5,6},{6,5},{7,8},{8,7},{9,10},{10... | collective-permute-start | bytes 983048 | tf_op jit(solution)/shard_map/ppermute | solution.py:375
  34.7 0.0 collective-permute-start.6
  34.7 1.2 %collective-permute-start.7 = (bf16[512,128]{1,0:T(8,128)(2,1)S(1)}, bf16[512,128]{1,0:T(8,128)(2,1)S(1)}, u32[]{:S(2)}, u32[]{:S(2)}) collective-permute-start(bf16[512,128]{1,0:T(8,128)(2,1)S(1)} %get-tuple-element.29), channel_id=1, source_target_pairs={{0,126},{1,127},{2,4},{3,5},{4,2},{5,3},{6,8},{7,9},{8,6},{9,7},{1... | collective-permute-start | bytes 393224 | tf_op jit(solution)/shard_map/ppermute | solution.py:376
  35.9 5.3 %collective-permute-done.6.na = bf16[512,128]{1,0:T(8,128)(2,1)S(1)} collective-permute-done((bf16[512,128]{1,0:T(8,128)(2,1)S(1)}, bf16[512,128]{1,0:T(8,128)(2,1)S(1)}, u32[]{:S(2)}, u32[]{:S(2)}) %collective-permute-start.6) | collective-permute-done | bytes 131104 | tf_op jit(solution)/shard_map/ppermute | solution.py:378
  41.2 7.9 %collective-permute-done.7.nb = bf16[512,128]{1,0:T(8,128)(2,1)S(1)} collective-permute-done((bf16[512,128]{1,0:T(8,128)(2,1)S(1)}, bf16[512,128]{1,0:T(8,128)(2,1)S(1)}, u32[]{:S(2)}, u32[]{:S(2)}) %collective-permute-start.7) | collective-permute-done | bytes 131104 | tf_op jit(solution)/shard_map/ppermute | solution.py:376
  49.1 0.0 collective-permute-done.4.ma
  49.1 0.0 collective-permute-done.5.mb
  49.1 2.1 %shard_map.80 = (bf16[3584,128]{1,0:T(8,128)(2,1)}, bf16[896,128]{1,0:T(8,128)(2,1)}) custom-call(s32[4,2]{1,0:T(4,128)S(1)} %copy.16.refs_1_.refs_2_.p2_cols, bf16[3584,128]{1,0:T(8,128)(2,1)} %get-tuple-element.23.coarse_in, f32[1280,128]{1,0:T(8,128)S(1)} %get-tuple-element.24.rim, ...), custom_call_target="tpu_custom_call", output_to_operand_aliasing={{0}: (1, {})} | custom-call | tf_op jit(solution)/shard_map/pallas_call | solution.py:302
  (1 shorter events, 0.0 us)
Async XLA Ops:
  2.2 1.2 %copy-start = (bf16[1,16,2,128,128]{4,3,2,1,0:T(8,128)(2,1)S(1)}, bf16[1,16,2,128,128]{4,3,2,1,0:T(8,128)(2,1)}, u32[]{:S(2)}) copy-start(bf16[1,16,2,128,128]{4,3,2,1,0:T(8,128)(2,1)} %param.8) | copy-start | bytes 3145732
  3.4 0.9 %copy-start.3 = (bf16[1,4,2,128,128]{4,3,2,1,0:T(8,128)(2,1)S(1)}, bf16[1,4,2,128,128]{4,3,2,1,0:T(8,128)(2,1)}, u32[]{:S(2)}) copy-start(bf16[1,4,2,128,128]{4,3,2,1,0:T(8,128)(2,1)} %param.10) | copy-start | bytes 786436
  4.3 20.9 %copy-start.4 = (bf16[1,4,2,128,128]{4,3,2,1,0:T(8,128)(2,1)S(1)}, bf16[1,4,2,128,128]{4,3,2,1,0:T(8,128)(2,1)}, u32[]{:S(2)}) copy-start(bf16[1,4,2,128,128]{4,3,2,1,0:T(8,128)(2,1)} %param.10) | copy-start | bytes 786436
  6.0 19.2 %collective-permute-start = (bf16[784,128]{1,0:T(8,128)(2,1)S(1)}, bf16[784,128]{1,0:T(8,128)(2,1)S(1)}, u32[]{:S(2)}, u32[]{:S(2)}) collective-permute-start(bf16[784,128]{1,0:T(8,128)(2,1)S(1)} %get-tuple-element.19), channel_id=1, source_target_pairs={{0,1},{1,0},{2,3},{3,2},{4,5},{5,4},{6,7},{7,6},{8,9},{9,8},{10,11... | collective-permute-start | bytes 602120 | tf_op jit(solution)/shard_map/ppermute | solution.py:339
  7.7 17.5 %collective-permute-start.1 = (bf16[784,128]{1,0:T(8,128)(2,1)S(1)}, bf16[784,128]{1,0:T(8,128)(2,1)S(1)}, u32[]{:S(2)}, u32[]{:S(2)}) collective-permute-start(bf16[784,128]{1,0:T(8,128)(2,1)S(1)} %get-tuple-element.20), channel_id=1, source_target_pairs={{0,127},{1,2},{2,1},{3,4},{4,3},{5,6},{6,5},{7,8},{8,7},{9,10},{10... | collective-permute-start | bytes 602120 | tf_op jit(solution)/shard_map/ppermute | solution.py:340
  14.9 9.1 %collective-permute-start.2 = (bf16[528,128]{1,0:T(8,128)(2,1)S(1)}, bf16[528,128]{1,0:T(8,128)(2,1)S(1)}, u32[]{:S(2)}, u32[]{:S(2)}) collective-permute-start(bf16[528,128]{1,0:T(8,128)(2,1)S(1)} %get-tuple-element.21), channel_id=1, source_target_pairs={{0,1},{1,0},{2,3},{3,2},{4,5},{5,4},{6,7},{7,6},{8,9},{9,8},{10,11... | collective-permute-start | bytes 405512 | tf_op jit(solution)/shard_map/ppermute | solution.py:341
  14.9 10.3 %collective-permute-start.3 = (bf16[528,128]{1,0:T(8,128)(2,1)S(1)}, bf16[528,128]{1,0:T(8,128)(2,1)S(1)}, u32[]{:S(2)}, u32[]{:S(2)}) collective-permute-start(bf16[528,128]{1,0:T(8,128)(2,1)S(1)} %get-tuple-element.22), channel_id=1, source_target_pairs={{0,127},{1,2},{2,1},{3,4},{4,3},{5,6},{6,5},{7,8},{8,7},{9,10},{10... | collective-permute-start | bytes 405512 | tf_op jit(solution)/shard_map/ppermute | solution.py:342
  16.5 1.2 %copy-start.1 = (bf16[1,16,2,128,128]{4,3,2,1,0:T(8,128)(2,1)S(1)}, bf16[1,16,2,128,128]{4,3,2,1,0:T(8,128)(2,1)}, u32[]{:S(2)}) copy-start(bf16[1,16,2,128,128]{4,3,2,1,0:T(8,128)(2,1)} %param.8) | copy-start | bytes 3145732
  17.8 1.7 %copy-start.2 = (bf16[1,16,5,128,128]{4,3,2,1,0:T(8,128)(2,1)S(1)}, bf16[1,16,5,128,128]{4,3,2,1,0:T(8,128)(2,1)}, u32[]{:S(2)}) copy-start(bf16[1,16,5,128,128]{4,3,2,1,0:T(8,128)(2,1)} %param.6) | copy-start | bytes 7864324
  29.7 19.4 %collective-permute-start.4 = (bf16[1280,128]{1,0:T(8,128)(2,1)S(1)}, bf16[1280,128]{1,0:T(8,128)(2,1)S(1)}, u32[]{:S(2)}, u32[]{:S(2)}) collective-permute-start(bf16[1280,128]{1,0:T(8,128)(2,1)S(1)} %get-tuple-element.26), channel_id=1, source_target_pairs={{0,1},{1,0},{2,3},{3,2},{4,5},{5,4},{6,7},{7,6},{8,9},{9,8},{10,11... | collective-permute-start | bytes 983048 | tf_op jit(solution)/shard_map/ppermute | solution.py:377
  29.7 19.4 %collective-permute-start.5 = (bf16[1280,128]{1,0:T(8,128)(2,1)S(1)}, bf16[1280,128]{1,0:T(8,128)(2,1)S(1)}, u32[]{:S(2)}, u32[]{:S(2)}) collective-permute-start(bf16[1280,128]{1,0:T(8,128)(2,1)S(1)} %get-tuple-element.27), channel_id=1, source_target_pairs={{0,127},{1,2},{2,1},{3,4},{4,3},{5,6},{6,5},{7,8},{8,7},{9,10},{10... | collective-permute-start | bytes 983048 | tf_op jit(solution)/shard_map/ppermute | solution.py:375
  34.7 6.5 %collective-permute-start.6 = (bf16[512,128]{1,0:T(8,128)(2,1)S(1)}, bf16[512,128]{1,0:T(8,128)(2,1)S(1)}, u32[]{:S(2)}, u32[]{:S(2)}) collective-permute-start(bf16[512,128]{1,0:T(8,128)(2,1)S(1)} %get-tuple-element.28), channel_id=1, source_target_pairs={{0,2},{1,3},{2,0},{3,1},{4,6},{5,7},{6,4},{7,5},{8,10},{9,11},{10,... | collective-permute-start | bytes 393224 | tf_op jit(solution)/shard_map/ppermute | solution.py:378
  34.7 14.4 %collective-permute-start.7 = (bf16[512,128]{1,0:T(8,128)(2,1)S(1)}, bf16[512,128]{1,0:T(8,128)(2,1)S(1)}, u32[]{:S(2)}, u32[]{:S(2)}) collective-permute-start(bf16[512,128]{1,0:T(8,128)(2,1)S(1)} %get-tuple-element.29), channel_id=1, source_target_pairs={{0,126},{1,127},{2,4},{3,5},{4,2},{5,3},{6,8},{7,9},{8,6},{9,7},{1... | collective-permute-start | bytes 393224 | tf_op jit(solution)/shard_map/ppermute | solution.py:376

commit v2 on v1

--- a/solution.py
+++ b/solution.py
@@ -22,7 +22,11 @@
 
 
 def side_at(cols, r, ncoarse):
-    return lax.rem(cols[r, 1] - cols[r, 0] + 1 + ncoarse, ncoarse) - 1
+    return lax.rem(cols[1, r] - cols[0, r] + 1 + ncoarse, ncoarse) - 1
+
+
+def place():
+    return lax.axis_index(AXES)
 
 
 def dot(a, b):
@@ -33,8 +37,11 @@
     return lax.dot_general(a, b, (((0,), (0,)), ((), ())), preferred_element_type=F32)
 
 
-def pack_kernel(ncoarse, ncoarsest, p_cols, p2_cols, p_hbm, p2_hbm, pa, pb, qa, qb, sems):
-    odd = p2_cols[0, 0] % 2
+def pack_kernel(ncoarse, ncoarsest, pc_hbm, qc_hbm, p_hbm, p2_hbm, pa, pb, qa, qb, p_cols, p2_cols, sems):
+    odd = place() % 2
+    cols_in = [pltpu.make_async_copy(x, y, sems.at[4 + n]) for n, (x, y) in enumerate(((pc_hbm, p_cols), (qc_hbm, p2_cols)))]
+    for copy in cols_in:
+        copy.start()
     jobs = []
     for n, (dst, flip) in enumerate(((pa, 0), (pb, 1), (qa, 0), (qb, 1))):
         high = (odd == flip).astype(jnp.int32)
@@ -49,6 +56,8 @@
         copy.start()
         jobs.append((copy, dst, start, rows, cols, ncols, size))
     row = lax.broadcasted_iota(jnp.int32, (16, B), 0)
+    for copy in cols_in:
+        copy.wait()
     for copy, dst, start, rows, cols, ncols, size in jobs:
         flags = jnp.zeros((16, B), F32)
         for r in range(rows):
@@ -89,15 +98,44 @@
     return jnp.concatenate([jnp.concatenate(band, axis=1) for band in bands], axis=0)
 
 
-def inner_kernel(nfine, ncoarse, a_cols, p_cols, a_ref, p_ref, acc_out, part_out, acc, prod):
-    base = a_cols[0, 0]
-    edge = {0: 0, 1: 1, 2: 2, 3: 3, 12: 4, 13: 5, 14: 6, 15: 7}
-    for g in (0, 3, 1, 2):
+def shift_at(a_cols, r, k, nfine):
+    return lax.rem(a_cols[k, 0, r] - (a_cols[0, 0, 0] + r) + 3 + nfine, nfine) - 3
+
+
+def flip(x):
+    return jnp.transpose(x, (1, 0))
+
+
+def inner_kernel(
+    nfine, ncoarse, ncoarsest, ac_hbm, pc_hbm, qc_hbm, a_hbm, p_hbm, p2_hbm,
+    acc_out, part_out, edge_out, wt_out, own_out, ownt_out,
+    a_cols, p_cols, p2_cols, a_ref, p_ref, p2_ref, acc, prod, sems,
+):
+    order = (0, 3, 1, 2)
+    cols_in = [
+        pltpu.make_async_copy(x, y, sems.at[6 + n])
+        for n, (x, y) in enumerate(((ac_hbm, a_cols), (pc_hbm, p_cols), (qc_hbm, p2_cols)))
+    ]
+    for copy in cols_in:
+        copy.start()
+    copies = [pltpu.make_async_copy(p_hbm, p_ref, sems.at[4])]
+    for g in range(4):
+        rows = pl.ds(4 * g * K * B, 4 * K * B)
+        copies.append(pltpu.make_async_copy(a_hbm.at[rows], a_ref.at[rows], sems.at[g]))
+    copies.append(pltpu.make_async_copy(p2_hbm, p2_ref, sems.at[5]))
+    copies[0].start()
+    for g in order:
+        copies[1 + g].start()
+    copies[5].start()
+    for copy in cols_in:
+        copy.wait()
+    copies[0].wait()
+    for g in order:
+        copies[1 + g].wait()
         for r in range(4 * g, 4 * g + 4):
             acc[...] = jnp.zeros_like(acc)
             for k in range(K):
-                shift = lax.rem(a_cols[r, k] - (base + r) + 3 + nfine, nfine) - 3
-                v = r + shift
+                v = r + shift_at(a_cols, r, k, nfine)
                 inside = jnp.logical_and(v >= 0, v < ROWS)
                 v = jnp.clip(v, 0, ROWS - 1)
                 side = side_at(p_cols, v, ncoarse)
@@ -109,57 +147,55 @@
                 acc[slot0] += terms[:, :B]
                 acc[slot1] += terms[:, B:]
             for s in range(5):
-                if r in edge or r in (4, 5, 6, 7, 8, 9, 10, 11):
-                    pass
                 if g in (0, 3):
                     acc_out[4 * (g // 3) + r % 4, :, s * B : (s + 1) * B] = acc[s]
                 else:
                     prod[blk(r - 4), s * B : (s + 1) * B] = acc[s].astype(BF)
+    for side in (0, 1):
+        first = 0 if side == 0 else ROWS - 3
+        for n in range(3):
+            r = first + n
+            for h in range(3):
+                want = (h - 3 if side == 0 else ROWS + h) - r
+                at = jnp.int32(0)
+                found = jnp.int32(0)
+                for k in range(1, K):
+                    hit = (shift_at(a_cols, r, k, nfine) == want).astype(jnp.int32)
+                    at = at + hit * k
+                    found = found + hit
+                block = a_ref[pl.ds(pl.multiple_of((r * K + at) * B, B), B), :]
+                keep = jnp.where(found > 0, block, jnp.zeros_like(block))
+                edge_out[blk(3 * side + n), h * B : (h + 1) * B] = keep if abs(want) <= 3 else jnp.zeros((B, B), BF)
+        bands = bands_of(p_ref, p_cols, range(12 * side, 12 * side + 4), ncoarse)
+        for n in range(4):
+            for m in range(3):
+                wt_out[blk(3 * side + m), n * B : (n + 1) * B] = flip(bands[n][m])
+    copies[5].wait()
+    own = bands_of(p2_ref, p2_cols, range(CROWS), ncoarsest)
+    for n in range(4):
+        for m in range(3):
+            own_out[blk(n), m * B : (m + 1) * B] = own[n][m]
+            ownt_out[blk(m), n * B : (n + 1) * B] = flip(own[n][m])
     part_out[...] = jnp.zeros_like(part_out)
     for g in (1, 2):
         bands = stack_bands(bands_of(p_ref, p_cols, range(4 * g, 4 * g + 4), ncoarse))
         terms = dot_t(bands, prod[blk(4 * (g - 1), 4), :])
         for m in range(3):
-            at = slice((g - 1) * B, (g + 4) * B)
-            part_out[g - 1 + m, :, at] = part_out[g - 1 + m, :, at] + terms[m * B : (m + 1) * B, :]
+            at = slice(g * B, (g + 5) * B)
+            part_out[g + m, :, at] = part_out[g + m, :, at] + terms[m * B : (m + 1) * B, :]
 
 
 def outer_kernel(
-    nfine, ncoarse, ncoarsest, a_cols, p_cols, p2_cols, a_ref, p_ref, p2_ref, acc_in, part_in,
-    pa, pb, qa, qb, coarse_out, rim_out, fine_out, ma, mb, na, nb, prod, part, cp,
+    acc_in, part_in, edge, wt, own, ownt, pa, pb, qa, qb, part, fine_out, ma, mb, na, nb, prod, cp
 ):
-    base = a_cols[0, 0]
-    d = p2_cols[0, 0]
+    d = place()
     even = d % 2 == 0
-    for g in (0, 3):
-        for m in range(4):
-            for s in range(5):
-                pass
+    part[...] = part_in[...]
     for side in (0, 1):
-        first = 0 if side == 0 else ROWS - 3
         bands = stack_bands(
             halo_bands(pb, pa, even, 3, 6 * B) if side == 0 else halo_bands(pa, pb, even, 3, 6 * B)
         )
-        rows = []
-        for r in range(first, first + 3):
-            line = []
-            for h in range(3):
-                v = h - 3 if side == 0 else ROWS + h
-                want = v - r
-                if abs(want) > 3:
-                    line.append(jnp.zeros((B, B), BF))
-                    continue
-                at = jnp.int32(0)
-                found = jnp.int32(0)
-                for k in range(1, K):
-                    shift = lax.rem(a_cols[r, k] - (base + r) + 3 + nfine, nfine) - 3
-                    hit = (shift == want).astype(jnp.int32)
-                    at = at + hit * k
-                    found = found + hit
-                block = a_ref[pl.ds(pl.multiple_of((r * K + at) * B, B), B), :]
-                line.append(jnp.where(found > 0, block, jnp.zeros_like(block)))
-            rows.append(jnp.concatenate(line, axis=1))
-        terms = dot(jnp.concatenate(rows, axis=0), bands)
+        terms = dot(edge[blk(3 * side, 3), :], bands)
         for n in range(4):
             r = 4 * side + n
             q = n if side == 0 else n - 1
@@ -169,35 +205,19 @@
                 if 0 <= lane < 3 and 0 <= q < 3:
                     value = value + terms[q * B : (q + 1) * B, lane * B : (lane + 1) * B]
                 prod[blk(r), s * B : (s + 1) * B] = value.astype(BF)
-    part[...] = jnp.zeros_like(part)
-    for j in range(4):
-        part[j + 1, :, B : 7 * B] = part_in[j]
-    for g in (0, 3):
-        bands = stack_bands(bands_of(p_ref, p_cols, range(4 * g, 4 * g + 4), ncoarse))
-        terms = dot_t(bands, prod[blk(4 * (g // 3), 4), :])
+    for side in (0, 1):
+        g = 3 * side
+        terms = dot(wt[blk(3 * side, 3), :], prod[blk(4 * side, 4), :])
         for m in range(3):
             at = slice(g * B, (g + 5) * B)
             part[g + m, :, at] = part[g + m, :, at] + terms[m * B : (m + 1) * B, :]
-    for j in range(4):
-        for t in range(KC):
-            q = t + j - 1
-            if 0 <= q < 8:
-                coarse_out[blk(j * KC + t), :] = part[j + 1, :, q * B : (q + 1) * B].astype(BF)
-            else:
-                coarse_out[blk(j * KC + t), :] = jnp.zeros((B, B), BF)
-    for t in range(5):
-        rim_out[blk(t), :] = part[1, :, (t - 1) * B : t * B] if t > 0 else jnp.zeros((B, B), F32)
-        q = t + 4
-        rim_out[blk(5 + t), :] = part[4, :, q * B : (q + 1) * B] if q < 8 else jnp.zeros((B, B), F32)
     low = halo_bands(qb, qa, even, 2, 4 * B)
     high = halo_bands(qa, qb, even, 2, 4 * B)
-    own = bands_of(p2_ref, p2_cols, range(4), ncoarsest)
     lines = part[...].astype(BF).reshape(6 * B, 8 * B)
     ta = dot(lines[0 : 4 * B, 0 : 2 * B], stack_bands(low))
-    tb = dot(lines[:, 2 * B : 6 * B], stack_bands(own))
+    tb = dot(lines[:, 2 * B : 6 * B], own[...])
     tc = dot(lines[2 * B : 6 * B, 6 * B : 8 * B], stack_bands(high))
     for e in range(5):
-        total = [None] * 6
         for i in range(6):
             pieces = []
             if e < 3 and i < 4:
@@ -209,7 +229,7 @@
             value = sum(pieces[1:], pieces[0]) if pieces else jnp.zeros((B, B), F32)
             cp[blk(i), e * B : (e + 1) * B] = value.astype(BF)
     gm = dot_t(stack_bands(low[1:2]), cp[blk(0), :])
-    g0 = dot_t(stack_bands(own), cp[blk(1, 4), :])
+    g0 = dot(ownt[...], cp[blk(1, 4), :])
     gp = dot_t(stack_bands(high[0:1]), cp[blk(5), :])
 
     def row(x, m):
@@ -253,8 +273,27 @@
         put2(nb, two_high, 1)
 
 
-def last_kernel(p2_cols, coarse_in, rim, fine, ma, mb, na, nb, coarse_out, coarsest_out, rows, sems):
-    d = p2_cols[0, 0]
+def column_block(part, j, t):
+    q = t + j - 1
+    if 0 <= q < 8:
+        return part[j + 1, :, q * B : (q + 1) * B]
+    return jnp.zeros((B, B), F32)
+
+
+def store_kernel(part, coarse_hbm, rows, sems):
+    copies = []
+    for j in range(CROWS):
+        for t in range(KC):
+            rows[blk(j * KC + t), :] = column_block(part, j, t).astype(BF)
+        at = blk(j * KC, KC)
+        copies.append(pltpu.make_async_copy(rows.at[at], coarse_hbm.at[at], sems.at[j]))
+        copies[-1].start()
+    for copy in copies:
+        copy.wait()
+
+
+def last_kernel(coarse_in, part, fine, ma, mb, na, nb, coarse_out, coarsest_out, rows, sems):
+    d = place()
     even = d % 2 == 0
     even2 = (d // 2) % 2 == 0
 
@@ -269,8 +308,8 @@
         return jnp.where(even2, na[blk(t), :], nb[blk(t), :]).astype(F32)
 
     for t in range(5):
-        rows[blk(t), :] = (rim[blk(t), :] + one(True, t)).astype(BF)
-        rows[blk(5 + t), :] = (rim[blk(5 + t), :] + one(False, t)).astype(BF)
+        rows[blk(t), :] = (column_block(part, 0, t) + one(True, t)).astype(BF)
+        rows[blk(5 + t), :] = (column_block(part, 3, t + 2) + one(False, t)).astype(BF)
     copies = [
         pltpu.make_async_copy(rows.at[blk(0, 5)], coarse_out.at[blk(0, 5)], sems.at[0]),
         pltpu.make_async_copy(rows.at[blk(5, 5)], coarse_out.at[blk(3 * KC + 2, 5)], sems.at[1]),
@@ -295,10 +334,11 @@
 
 
 def call(kernel, ins, outs, args, scratch=(), cost=None, **kw):
-    smem = pl.BlockSpec(memory_space=pltpu.SMEM)
     vmem = pl.BlockSpec(memory_space=pltpu.VMEM)
-    anyspec = pl.BlockSpec(memory_space=pl.ANY)
-    kinds = {"s": smem, "v": vmem, "a": anyspec}
+    hbm = pl.BlockSpec(memory_space=pltpu.HBM)
+    kinds = {"v": vmem, "h": hbm}
+    if not kw:
+        args = [pltpu.with_memory_space_constraint(x, pltpu.HBM) if c == "h" else x for c, x in zip(ins, args)]
     return pl.pallas_call(
         kernel,
         in_specs=[kinds[c] for c in ins],
@@ -315,9 +355,9 @@
     devices = lax.axis_size(AXES)
     nfine = ROWS * devices
     ncoarse = CROWS * devices
-    a_cols = a_cols.reshape(ROWS, K)
-    p_cols = p_cols.reshape(ROWS, 2)
-    p2_cols = p2_cols.reshape(CROWS, 2)
+    a_cols = jnp.transpose(a_cols, (2, 0, 1))
+    p_cols = p_cols.reshape(ROWS, 2).T
+    p2_cols = p2_cols.reshape(CROWS, 2).T
     a = a_vals.reshape(ROWS * K * B, B)
     p = p_vals.reshape(ROWS * 2 * B, B)
     p2 = p2_vals.reshape(CROWS * 2 * B, B)
@@ -331,10 +371,14 @@
 
     pa, pb, qa, qb = call(
         pack,
-        "ssaa",
+        "hhhh",
         [("v", (PM, B), BF), ("v", (PM, B), BF), ("v", (QM, B), BF), ("v", (QM, B), BF)],
         (p_cols, p2_cols, p, p2),
-        [pltpu.SemaphoreType.DMA((4,))],
+        [
+            pltpu.SMEM((2, ROWS), jnp.int32),
+            pltpu.SMEM((2, CROWS), jnp.int32),
+            pltpu.SemaphoreType.DMA((6,)),
+        ],
     )
     pa = lax.ppermute(pa, AXES, swap_a)
     pb = lax.ppermute(pb, AXES, swap_b)
@@ -342,47 +386,67 @@
     qb = lax.ppermute(qb, AXES, swap_b)
 
     def inner(*refs):
-        inner_kernel(nfine, ncoarse, *refs)
-
-    acc, part = call(
+        inner_kernel(nfine, ncoarse, devices, *refs)
+
+    ready = call(
         inner,
-        "ssvv",
-        [("v", (8, B, 5 * B), F32), ("v", (4, B, 6 * B), F32)],
-        (a_cols, p_cols, a, p),
-        [pltpu.VMEM((8, B, B), F32), pltpu.VMEM((8 * B, 5 * B), BF)],
+        "hhhhhh",
+        [
+            ("v", (8, B, 5 * B), F32),
+            ("v", (6, B, 8 * B), F32),
+            ("v", (6 * B, 3 * B), BF),
+            ("v", (6 * B, 4 * B), BF),
+            ("v", (4 * B, 3 * B), BF),
+            ("v", (3 * B, 4 * B), BF),
+        ],
+        (a_cols, p_cols, p2_cols, a, p, p2),
+        [
+            pltpu.SMEM((K, 1, ROWS), jnp.int32),
+            pltpu.SMEM((2, ROWS), jnp.int32),
+            pltpu.SMEM((2, CROWS), jnp.int32),
+            pltpu.VMEM((ROWS * K * B, B), BF),
+            pltpu.VMEM((ROWS * 2 * B, B), BF),
+            pltpu.VMEM((CROWS * 2 * B, B), BF),
+            pltpu.VMEM((8, B, B), F32),
+            pltpu.VMEM((8 * B, 5 * B), BF),
+            pltpu.SemaphoreType.DMA((9,)),
+        ],
         pl.CostEstimate(flops=10**9, bytes_accessed=8 * 10**6, transcendentals=0),
     )
-
-    def outer(*refs):
-        outer_kernel(nfine, ncoarse, devices, *refs)
-
-    coarse, rim, fine, ma, mb, na, nb = call(
-        outer,
-        "sssvvvvvvvvv",
+    part, fine, ma, mb, na, nb = call(
+        outer_kernel,
+        "vvvvvvvvvv",
         [
-            ("v", (CROWS * KC * B, B), BF),
-            ("v", (10 * B, B), F32),
+            ("v", (6, B, 8 * B), F32),
             ("v", (B, 5 * B), F32),
             ("v", (10 * B, B), BF),
             ("v", (10 * B, B), BF),
             ("v", (4 * B, B), BF),
             ("v", (4 * B, B), BF),
         ],
-        (a_cols, p_cols, p2_cols, a, p, p2, acc, part, pa, pb, qa, qb),
-        [pltpu.VMEM((8 * B, 5 * B), BF), pltpu.VMEM((6, B, 8 * B), F32), pltpu.VMEM((6 * B, 5 * B), BF)],
+        (*ready, pa, pb, qa, qb),
+        [pltpu.VMEM((8 * B, 5 * B), BF), pltpu.VMEM((6 * B, 5 * B), BF)],
         pl.CostEstimate(flops=2 * 10**9, bytes_accessed=8 * 10**6, transcendentals=0),
     )
     mb = lax.ppermute(mb, AXES, swap_b)
     nb = lax.ppermute(nb, AXES, skip_b)
     ma = lax.ppermute(ma, AXES, swap_a)
     na = lax.ppermute(na, AXES, skip_a)
+    (coarse,) = call(
+        store_kernel,
+        "v",
+        [("h", (CROWS * KC * B, B), BF)],
+        (part,),
+        [pltpu.VMEM((CROWS * KC * B, B), BF), pltpu.SemaphoreType.DMA((CROWS,))],
+        pl.CostEstimate(flops=10**6, bytes_accessed=3 * 10**6, transcendentals=0),
+    )
     coarse, coarsest = call(
         last_kernel,
-        "savvvvvv",
-        [("a", (CROWS * KC * B, B), BF), ("v", (KC * B, B), BF)],
-        (p2_cols, coarse, rim, fine, ma, mb, na, nb),
+        "hvvvvvv",
+        [("h", (CROWS * KC * B, B), BF), ("v", (KC * B, B), BF)],
+        (coarse, part, fine, ma, mb, na, nb),
         [pltpu.VMEM((10 * B, B), BF), pltpu.SemaphoreType.DMA((2,))],
-        input_output_aliases={1: 0},
+        input_output_aliases={0: 0},
     )
     return coarse.reshape(1, CROWS, KC, B, B), coarsest.reshape(1, 1, KC, B, B)
 

time: 51.5 us -> 43.9 us (0.85)
  local copies, waits for them, and re-layouts: 7.42 us -> 0 us
  waiting for transfers between devices: 14.5 us -> 16.9 us
  starting transfers between devices: 16 us -> 13.9 us
    unnamed x10 -> x0, local copies, waits for them, and re-layouts: 5.14 us -> none
    ppermute x1, waiting for transfers between devices: 1.27 us -> 3.6 us  [body(): qb = lax.ppermute(qb, AXES, swap_b)]
    reshape x3 -> x0, local copies, waits for them, and re-layouts: 2.28 us -> none  [the longest x1 0.77 us: body(): p2_cols = p2_cols.reshape(CROWS, 2)]
    ppermute x1, starting transfers between devices: 5.02 us -> 2.75 us  [body(): mb = lax.ppermute(mb, AXES, swap_b)]
    ppermute x1, waiting for transfers between devices: 0.01 us -> 2 us  [body(): mb = lax.ppermute(mb, AXES, swap_b)]
    ppermute x1, starting transfers between devices: 0.01 us -> 1.33 us  [body(): na = lax.ppermute(na, AXES, skip_a)]
    ppermute x1, starting transfers between devices: 1.18 us -> 0.01 us  [body(): nb = lax.ppermute(nb, AXES, skip_b)]
    ppermute x1, waiting for transfers between devices: 5.29 us -> 4.16 us  [body(): na = lax.ppermute(na, AXES, skip_a)]
  transfers between devices with their start and end apart: 8 -> 8, of which waited for: 3 -> 4; matrix products, arithmetic and copies ran while one was open for 1% -> 0% of each run, Pallas kernels for 9% -> 15%
where the time goes in v2:
time: 43.9 us; the launch traced here: 43.8 us
  waiting for transfers between devices  16.9 us (38%)
  starting transfers between devices  13.9 us (32%)
  Pallas kernels  12.2 us (28%)
  between operations  0.68 us (2%)
    pallas_call x5, Pallas kernels, call(): pl.pallas_call(kernel, in_specs=[kinds[c] for c in ins], out_specs=tuple(...  12.2 us
    ppermute x1, starting transfers between devices, body(): pb = lax.ppermute(pb, AXES, swap_b)  7.18 us
    ppermute x1, waiting for transfers between devices, body(): nb = lax.ppermute(nb, AXES, skip_b)  7.12 us
    ppermute x1, waiting for transfers between devices, body(): na = lax.ppermute(na, AXES, skip_a)  4.16 us
    ppermute x1, waiting for transfers between devices, body(): qb = lax.ppermute(qb, AXES, swap_b)  3.6 us
    ppermute x1, starting transfers between devices, body(): mb = lax.ppermute(mb, AXES, swap_b)  2.75 us
    ppermute x1, waiting for transfers between devices, body(): mb = lax.ppermute(mb, AXES, swap_b)  2 us
    ppermute x1, starting transfers between devices, body(): pa = lax.ppermute(pa, AXES, swap_a)  1.68 us
  transfers between devices with their start and end apart: 8, of which 4 were waited for; matrix products, arithmetic and copies ran while one was open for 0% of the time, Pallas kernels for 15%

profile of v2, /device:TPU:0, one launch (start us, length us, event | category | flops | bytes accessed | tf_op | source)
XLA Modules:
  0.0 43.8 jit_solution(8442945739096188495)
XLA Ops:
  0.6 1.2 %shard_map.78 = (bf16[784,128]{1,0:T(8,128)(2,1)S(1)}, bf16[784,128]{1,0:T(8,128)(2,1)S(1)}, bf16[528,128]{1,0:T(8,128)(2,1)S(1)}, bf16[528,128]{1,0:T(8,128)(2,1)S(1)}) custom-call(s32[2,16]{1,0:T(2,128)} %bitcast.18, s32[2,4]{1,0:T(2,128)} %bitcast.20, bf16[4096,128]{1,0:T(8,128)(2,1)} %bitcast.12, bf16[1024,128]{1,0:T(8,128)(2,1)} %bitcast.16), custom_call_target="tpu_custom_call" | custom-call | tf_op jit(solution)/shard_map/pallas_call | solution.py:342
  1.9 1.7 %collective-permute-start = (bf16[784,128]{1,0:T(8,128)(2,1)S(1)}, bf16[784,128]{1,0:T(8,128)(2,1)S(1)}, u32[]{:S(2)}, u32[]{:S(2)}) collective-permute-start(bf16[784,128]{1,0:T(8,128)(2,1)S(1)} %get-tuple-element.26), channel_id=1, source_target_pairs={{0,1},{1,0},{2,3},{3,2},{4,5},{5,4},{6,7},{7,6},{8,9},{9,8},{10,11... | collective-permute-start | bytes 602120 | tf_op jit(solution)/shard_map/ppermute | solution.py:383
  3.6 7.2 %collective-permute-start.1 = (bf16[784,128]{1,0:T(8,128)(2,1)S(1)}, bf16[784,128]{1,0:T(8,128)(2,1)S(1)}, u32[]{:S(2)}, u32[]{:S(2)}) collective-permute-start(bf16[784,128]{1,0:T(8,128)(2,1)S(1)} %get-tuple-element.27), channel_id=1, source_target_pairs={{0,127},{1,2},{2,1},{3,4},{4,3},{5,6},{6,5},{7,8},{8,7},{9,10},{10... | collective-permute-start | bytes 602120 | tf_op jit(solution)/shard_map/ppermute | solution.py:384
  10.7 0.0 collective-permute-start.2
  10.7 0.9 %collective-permute-start.3 = (bf16[528,128]{1,0:T(8,128)(2,1)S(1)}, bf16[528,128]{1,0:T(8,128)(2,1)S(1)}, u32[]{:S(2)}, u32[]{:S(2)}) collective-permute-start(bf16[528,128]{1,0:T(8,128)(2,1)S(1)} %get-tuple-element.29), channel_id=1, source_target_pairs={{0,127},{1,2},{2,1},{3,4},{4,3},{5,6},{6,5},{7,8},{8,7},{9,10},{10... | collective-permute-start | bytes 405512 | tf_op jit(solution)/shard_map/ppermute | solution.py:386
  11.7 5.8 %shard_map.77 = (f32[8,128,640]{2,1,0:T(8,128)S(1)}, f32[6,128,1024]{2,1,0:T(8,128)S(1)}, bf16[768,384]{1,0:T(8,128)(2,1)S(1)}, bf16[768,512]{1,0:T(8,128)(2,1)S...) custom-call(s32[5,1,16]{2,1,0:T(1,128)} %bitcast.22, s32[2,16]{1,0:T(2,128)} %bitcast.19, ...), custom_call_target="tpu_custom_call" | custom-call | flops 1000000000 | bytes 8000000 | tf_op jit(solution)/shard_map/pallas_call | solution.py:342
  17.5 0.0 collective-permute-done.2.qa
  17.5 3.6 %collective-permute-done.3.qb = bf16[528,128]{1,0:T(8,128)(2,1)S(1)} collective-permute-done((bf16[528,128]{1,0:T(8,128)(2,1)S(1)}, bf16[528,128]{1,0:T(8,128)(2,1)S(1)}, u32[]{:S(2)}, u32[]{:S(2)}) %collective-permute-start.3) | collective-permute-done | bytes 135200 | tf_op jit(solution)/shard_map/ppermute | solution.py:386
  21.1 0.0 collective-permute-done.pa
  21.1 0.0 collective-permute-done.1.pb
  21.1 2.7 %shard_map.79 = (f32[6,128,1024]{2,1,0:T(8,128)S(1)}, f32[128,640]{1,0:T(8,128)S(1)}, bf16[1280,128]{1,0:T(8,128)(2,1)S(1)}, bf16[1280,128]{1,0:T(8,128)(2,1)S(1...) custom-call(f32[8,128,640]{2,1,0:T(8,128)S(1)} %get-tuple-element.20.acc_in, ...), custom_call_target="tpu_custom_call" | custom-call | flops 2000000000 | bytes 8000000 | tf_op jit(solution)/shard_map/pallas_call | solution.py:342
  23.8 0.1 collective-permute-start.4
  23.9 2.8 %collective-permute-start.5 = (bf16[1280,128]{1,0:T(8,128)(2,1)S(1)}, bf16[1280,128]{1,0:T(8,128)(2,1)S(1)}, u32[]{:S(2)}, u32[]{:S(2)}) collective-permute-start(bf16[1280,128]{1,0:T(8,128)(2,1)S(1)} %get-tuple-element.33), channel_id=1, source_target_pairs={{0,127},{1,2},{2,1},{3,4},{4,3},{5,6},{6,5},{7,8},{8,7},{9,10},{10... | collective-permute-start | bytes 983048 | tf_op jit(solution)/shard_map/ppermute | solution.py:431
  26.6 1.3 %collective-permute-start.6 = (bf16[512,128]{1,0:T(8,128)(2,1)S(1)}, bf16[512,128]{1,0:T(8,128)(2,1)S(1)}, u32[]{:S(2)}, u32[]{:S(2)}) collective-permute-start(bf16[512,128]{1,0:T(8,128)(2,1)S(1)} %get-tuple-element.34), channel_id=1, source_target_pairs={{0,2},{1,3},{2,0},{3,1},{4,6},{5,7},{6,4},{7,5},{8,10},{9,11},{10,... | collective-permute-start | bytes 393224 | tf_op jit(solution)/shard_map/ppermute | solution.py:434
  28.0 0.0 collective-permute-start.7
  28.0 1.0 %shard_map.80.coarse_in = bf16[3584,128]{1,0:T(8,128)(2,1)} custom-call(f32[6,128,1024]{2,1,0:T(8,128)S(1)} %get-tuple-element.30.part), custom_call_target="tpu_custom_call" | custom-call | flops 1000000 | bytes 3000000 | tf_op jit(solution)/shard_map/pallas_call | solution.py:342
  29.0 4.2 %collective-permute-done.6.na = bf16[512,128]{1,0:T(8,128)(2,1)S(1)} collective-permute-done((bf16[512,128]{1,0:T(8,128)(2,1)S(1)}, bf16[512,128]{1,0:T(8,128)(2,1)S(1)}, u32[]{:S(2)}, u32[]{:S(2)}) %collective-permute-start.6) | collective-permute-done | bytes 131104 | tf_op jit(solution)/shard_map/ppermute | solution.py:434
  33.1 7.1 %collective-permute-done.7.nb = bf16[512,128]{1,0:T(8,128)(2,1)S(1)} collective-permute-done((bf16[512,128]{1,0:T(8,128)(2,1)S(1)}, bf16[512,128]{1,0:T(8,128)(2,1)S(1)}, u32[]{:S(2)}, u32[]{:S(2)}) %collective-permute-start.7) | collective-permute-done | bytes 131104 | tf_op jit(solution)/shard_map/ppermute | solution.py:432
  40.2 0.0 collective-permute-done.4.ma
  40.2 2.0 %collective-permute-done.5.mb = bf16[1280,128]{1,0:T(8,128)(2,1)S(1)} collective-permute-done((bf16[1280,128]{1,0:T(8,128)(2,1)S(1)}, bf16[1280,128]{1,0:T(8,128)(2,1)S(1)}, u32[]{:S(2)}, u32[]{:S(2)}) %collective-permute-start.5) | collective-permute-done | bytes 327712 | tf_op jit(solution)/shard_map/ppermute | solution.py:431
  42.2 1.5 %shard_map.81 = (bf16[3584,128]{1,0:T(8,128)(2,1)}, bf16[896,128]{1,0:T(8,128)(2,1)}) custom-call(bf16[3584,128]{1,0:T(8,128)(2,1)} %shard_map.80.coarse_in, f32[6,128,1024]{2,1,0:T(8,128)S(1)} %get-tuple-element.30.part, f32[128,640]{1,0:T(8,128)S(1)} %get-tuple-element.31.fine, ...), custom_call_target="tpu_custom_call", output_to_operand_aliasing={{0}: (0, {})} | custom-call | tf_op jit(solution)/shard_map/pallas_call | solution.py:342
Async XLA Ops:
  1.9 19.2 %collective-permute-start = (bf16[784,128]{1,0:T(8,128)(2,1)S(1)}, bf16[784,128]{1,0:T(8,128)(2,1)S(1)}, u32[]{:S(2)}, u32[]{:S(2)}) collective-permute-start(bf16[784,128]{1,0:T(8,128)(2,1)S(1)} %get-tuple-element.26), channel_id=1, source_target_pairs={{0,1},{1,0},{2,3},{3,2},{4,5},{5,4},{6,7},{7,6},{8,9},{9,8},{10,11... | collective-permute-start | bytes 602120 | tf_op jit(solution)/shard_map/ppermute | solution.py:383
  3.6 17.5 %collective-permute-start.1 = (bf16[784,128]{1,0:T(8,128)(2,1)S(1)}, bf16[784,128]{1,0:T(8,128)(2,1)S(1)}, u32[]{:S(2)}, u32[]{:S(2)}) collective-permute-start(bf16[784,128]{1,0:T(8,128)(2,1)S(1)} %get-tuple-element.27), channel_id=1, source_target_pairs={{0,127},{1,2},{2,1},{3,4},{4,3},{5,6},{6,5},{7,8},{8,7},{9,10},{10... | collective-permute-start | bytes 602120 | tf_op jit(solution)/shard_map/ppermute | solution.py:384
  10.7 6.7 %collective-permute-start.2 = (bf16[528,128]{1,0:T(8,128)(2,1)S(1)}, bf16[528,128]{1,0:T(8,128)(2,1)S(1)}, u32[]{:S(2)}, u32[]{:S(2)}) collective-permute-start(bf16[528,128]{1,0:T(8,128)(2,1)S(1)} %get-tuple-element.28), channel_id=1, source_target_pairs={{0,1},{1,0},{2,3},{3,2},{4,5},{5,4},{6,7},{7,6},{8,9},{9,8},{10,11... | collective-permute-start | bytes 405512 | tf_op jit(solution)/shard_map/ppermute | solution.py:385
  10.7 10.3 %collective-permute-start.3 = (bf16[528,128]{1,0:T(8,128)(2,1)S(1)}, bf16[528,128]{1,0:T(8,128)(2,1)S(1)}, u32[]{:S(2)}, u32[]{:S(2)}) collective-permute-start(bf16[528,128]{1,0:T(8,128)(2,1)S(1)} %get-tuple-element.29), channel_id=1, source_target_pairs={{0,127},{1,2},{2,1},{3,4},{4,3},{5,6},{6,5},{7,8},{8,7},{9,10},{10... | collective-permute-start | bytes 405512 | tf_op jit(solution)/shard_map/ppermute | solution.py:386
  23.8 16.4 %collective-permute-start.4 = (bf16[1280,128]{1,0:T(8,128)(2,1)S(1)}, bf16[1280,128]{1,0:T(8,128)(2,1)S(1)}, u32[]{:S(2)}, u32[]{:S(2)}) collective-permute-start(bf16[1280,128]{1,0:T(8,128)(2,1)S(1)} %get-tuple-element.32), channel_id=1, source_target_pairs={{0,1},{1,0},{2,3},{3,2},{4,5},{5,4},{6,7},{7,6},{8,9},{9,8},{10,11... | collective-permute-start | bytes 983048 | tf_op jit(solution)/shard_map/ppermute | solution.py:433
  23.9 18.3 %collective-permute-start.5 = (bf16[1280,128]{1,0:T(8,128)(2,1)S(1)}, bf16[1280,128]{1,0:T(8,128)(2,1)S(1)}, u32[]{:S(2)}, u32[]{:S(2)}) collective-permute-start(bf16[1280,128]{1,0:T(8,128)(2,1)S(1)} %get-tuple-element.33), channel_id=1, source_target_pairs={{0,127},{1,2},{2,1},{3,4},{4,3},{5,6},{6,5},{7,8},{8,7},{9,10},{10... | collective-permute-start | bytes 983048 | tf_op jit(solution)/shard_map/ppermute | solution.py:431
  26.6 6.5 %collective-permute-start.6 = (bf16[512,128]{1,0:T(8,128)(2,1)S(1)}, bf16[512,128]{1,0:T(8,128)(2,1)S(1)}, u32[]{:S(2)}, u32[]{:S(2)}) collective-permute-start(bf16[512,128]{1,0:T(8,128)(2,1)S(1)} %get-tuple-element.34), channel_id=1, source_target_pairs={{0,2},{1,3},{2,0},{3,1},{4,6},{5,7},{6,4},{7,5},{8,10},{9,11},{10,... | collective-permute-start | bytes 393224 | tf_op jit(solution)/shard_map/ppermute | solution.py:434
  28.0 12.3 %collective-permute-start.7 = (bf16[512,128]{1,0:T(8,128)(2,1)S(1)}, bf16[512,128]{1,0:T(8,128)(2,1)S(1)}, u32[]{:S(2)}, u32[]{:S(2)}) collective-permute-start(bf16[512,128]{1,0:T(8,128)(2,1)S(1)} %get-tuple-element.35), channel_id=1, source_target_pairs={{0,126},{1,127},{2,4},{3,5},{4,2},{5,3},{6,8},{7,9},{8,6},{9,7},{1... | collective-permute-start | bytes 393224 | tf_op jit(solution)/shard_map/ppermute | solution.py:432

commit v3 on v2

--- a/solution.py
+++ b/solution.py
@@ -4,6 +4,7 @@
 from jax.experimental import pallas as pl
 from jax.experimental.pallas import tpu as pltpu
 from jax.sharding import PartitionSpec as P
+
 
 B = 128
 K = 5
@@ -12,8 +13,7 @@
 CROWS = 4
 BF = jnp.bfloat16
 F32 = jnp.float32
-PM = 6 * B + 16
-QM = 4 * B + 16
+PM = 10 * B + 16
 AXES = ("gx", "gy")
 
 
@@ -37,35 +37,29 @@
     return lax.dot_general(a, b, (((0,), (0,)), ((), ())), preferred_element_type=F32)
 
 
-def pack_kernel(ncoarse, ncoarsest, pc_hbm, qc_hbm, p_hbm, p2_hbm, pa, pb, qa, qb, p_cols, p2_cols, sems):
-    odd = place() % 2
+def pack_kernel(ncoarse, ncoarsest, pc_hbm, qc_hbm, p_hbm, p2_hbm, up, down, p_cols, p2_cols, sems):
     cols_in = [pltpu.make_async_copy(x, y, sems.at[4 + n]) for n, (x, y) in enumerate(((pc_hbm, p_cols), (qc_hbm, p2_cols)))]
     for copy in cols_in:
         copy.start()
-    jobs = []
-    for n, (dst, flip) in enumerate(((pa, 0), (pb, 1), (qa, 0), (qb, 1))):
-        high = (odd == flip).astype(jnp.int32)
-        if n < 2:
-            start, rows, src, cols, ncols = high * (ROWS - 3), 3, p_hbm, p_cols, ncoarse
-        else:
-            start, rows, src, cols, ncols = high * (CROWS - 2), 2, p2_hbm, p2_cols, ncoarsest
-        size = rows * 2 * B
-        copy = pltpu.make_async_copy(
-            src.at[pl.ds(pl.multiple_of(start * 2 * B, 2 * B), size)], dst.at[pl.ds(0, size)], sems.at[n]
-        )
+    copies = []
+    for n, (dst, fine, coarse) in enumerate(((up, ROWS - 3, CROWS - 2), (down, 0, 0))):
+        copies.append(pltpu.make_async_copy(p_hbm.at[blk(2 * fine, 6)], dst.at[blk(0, 6)], sems.at[2 * n]))
+        copies.append(pltpu.make_async_copy(p2_hbm.at[blk(2 * coarse, 4)], dst.at[blk(6, 4)], sems.at[2 * n + 1]))
+    for copy in copies:
         copy.start()
-        jobs.append((copy, dst, start, rows, cols, ncols, size))
     row = lax.broadcasted_iota(jnp.int32, (16, B), 0)
     for copy in cols_in:
         copy.wait()
-    for copy, dst, start, rows, cols, ncols, size in jobs:
+    for dst, fine, coarse in ((up, ROWS - 3, CROWS - 2), (down, 0, 0)):
         flags = jnp.zeros((16, B), F32)
-        for r in range(rows):
-            side = side_at(cols, start + r, ncols)
+        sides = [side_at(p_cols, fine + r, ncoarse) for r in range(3)]
+        sides += [side_at(p2_cols, coarse + r, ncoarsest) for r in range(2)]
+        for r, side in enumerate(sides):
             flags = jnp.where(row == 2 * r, (side < 0).astype(F32), flags)
             flags = jnp.where(row == 2 * r + 1, (side > 0).astype(F32), flags)
+        dst[pl.ds(10 * B, 16), :] = flags.astype(BF)
+    for copy in copies:
         copy.wait()
-        dst[pl.ds(size, 16), :] = flags.astype(BF)
 
 
 def bands_of(p_ref, cols, rows, ncoarse):
@@ -79,15 +73,12 @@
     return out
 
 
-def halo_bands(low, high, is_low, rows, size):
-    def pick(start, n):
-        return jnp.where(is_low, low[pl.ds(start, n), :], high[pl.ds(start, n), :])
-
-    flags = pick(size, 16).astype(F32)
+def halo_bands(message, rows):
+    flags = message[pl.ds(10 * B, 16), :].astype(F32)
     out = []
-    for r in range(rows):
-        p0 = pick(2 * r * B, B)
-        p1 = pick((2 * r + 1) * B, B)
+    for r in rows:
+        p0 = message[blk(2 * r), :]
+        p1 = message[blk(2 * r + 1), :]
         lower = jnp.broadcast_to(flags[2 * r : 2 * r + 1, :], (B, B)).astype(BF)
         upper = jnp.broadcast_to(flags[2 * r + 1 : 2 * r + 2, :], (B, B)).astype(BF)
         out.append((p1 * lower, p0, p1 * upper))
@@ -186,15 +177,13 @@
 
 
 def outer_kernel(
-    acc_in, part_in, edge, wt, own, ownt, pa, pb, qa, qb, part, fine_out, ma, mb, na, nb, prod, cp
+    acc_in, part_in, edge, wt, own, ownt, from_low, from_high, part, fine_out, ma, mb, na, nb, prod, cp
 ):
     d = place()
     even = d % 2 == 0
     part[...] = part_in[...]
     for side in (0, 1):
-        bands = stack_bands(
-            halo_bands(pb, pa, even, 3, 6 * B) if side == 0 else halo_bands(pa, pb, even, 3, 6 * B)
-        )
+        bands = stack_bands(halo_bands(from_low if side == 0 else from_high, range(3)))
         terms = dot(edge[blk(3 * side, 3), :], bands)
         for n in range(4):
             r = 4 * side + n
@@ -211,8 +200,8 @@
         for m in range(3):
             at = slice(g * B, (g + 5) * B)
             part[g + m, :, at] = part[g + m, :, at] + terms[m * B : (m + 1) * B, :]
-    low = halo_bands(qb, qa, even, 2, 4 * B)
-    high = halo_bands(qa, qb, even, 2, 4 * B)
+    low = halo_bands(from_low, (3, 4))
+    high = halo_bands(from_high, (3, 4))
     lines = part[...].astype(BF).reshape(6 * B, 8 * B)
     ta = dot(lines[0 : 4 * B, 0 : 2 * B], stack_bands(low))
     tb = dot(lines[:, 2 * B : 6 * B], own[...])
@@ -369,10 +358,10 @@
     def pack(*refs):
         pack_kernel(ncoarse, devices, *refs)
 
-    pa, pb, qa, qb = call(
+    up, down = call(
         pack,
         "hhhh",
-        [("v", (PM, B), BF), ("v", (PM, B), BF), ("v", (QM, B), BF), ("v", (QM, B), BF)],
+        [("v", (PM, B), BF), ("v", (PM, B), BF)],
         (p_cols, p2_cols, p, p2),
         [
             pltpu.SMEM((2, ROWS), jnp.int32),
@@ -380,10 +369,8 @@
             pltpu.SemaphoreType.DMA((6,)),
         ],
     )
-    pa = lax.ppermute(pa, AXES, swap_a)
-    pb = lax.ppermute(pb, AXES, swap_b)
-    qa = lax.ppermute(qa, AXES, swap_a)
-    qb = lax.ppermute(qb, AXES, swap_b)
+    from_low = lax.ppermute(up, AXES, [(i, (i + 1) % devices) for i in range(devices)])
+    from_high = lax.ppermute(down, AXES, [((i + 1) % devices, i) for i in range(devices)])
 
     def inner(*refs):
         inner_kernel(nfine, ncoarse, devices, *refs)
@@ -415,7 +402,7 @@
     )
     part, fine, ma, mb, na, nb = call(
         outer_kernel,
-        "vvvvvvvvvv",
+        "vvvvvvvv",
         [
             ("v", (6, B, 8 * B), F32),
             ("v", (B, 5 * B), F32),
@@ -424,7 +411,7 @@
             ("v", (4 * B, B), BF),
             ("v", (4 * B, B), BF),
         ],
-        (*ready, pa, pb, qa, qb),
+        (*ready, from_low, from_high),
         [pltpu.VMEM((8 * B, 5 * B), BF), pltpu.VMEM((6 * B, 5 * B), BF)],
         pl.CostEstimate(flops=2 * 10**9, bytes_accessed=8 * 10**6, transcendentals=0),
     )
@@ -454,6 +441,7 @@
 def solution(mesh):
     blocks = P(None, AXES, None, None, None)
     cols = P(None, AXES, None)
+
     return jax.shard_map(
         body,
         mesh=mesh,

time: 43.9 us -> 42.3 us (0.964)
  waiting for transfers between devices: 16.9 us -> 13.7 us
  starting transfers between devices: 13.9 us -> 15.6 us
    ppermute x1, starting transfers between devices: 0.01 us -> 2.46 us  [body(): nb = lax.ppermute(nb, AXES, skip_b)]
    ppermute x4 -> x2, waiting for transfers between devices: 3.61 us -> 1.62 us  [the longest x1 1.62 us: body(): lax.ppermute(up, AXES, [(i, (i + 1) % devices) for i in range(devices)])]
    ppermute x1, starting transfers between devices: 2.75 us -> 4.69 us  [body(): mb = lax.ppermute(mb, AXES, swap_b)]
    ppermute x4 -> x2, starting transfers between devices: 9.78 us -> 8.39 us  [the longest x1 6.71 us: body(): lax.ppermute(down, AXES, [((i + 1) % devices, i) for i in range(devices)])]
    ppermute x1, starting transfers between devices: 1.33 us -> 0.01 us  [body(): na = lax.ppermute(na, AXES, skip_a)]
    ppermute x1, waiting for transfers between devices: 7.12 us -> 6.56 us  [body(): nb = lax.ppermute(nb, AXES, skip_b)]
  transfers between devices with their start and end apart: 8 -> 6, of which waited for: 4 -> 4; matrix products, arithmetic and copies ran while one was open for 0% -> 0% of each run, Pallas kernels for 15% -> 16%
where the time goes in v3:
time: 42.3 us; the launch traced here: 42.2 us
  starting transfers between devices  15.6 us (37%)
  waiting for transfers between devices  13.7 us (32%)
  Pallas kernels  12.2 us (29%)
  between operations  0.67 us (2%)
    pallas_call x5, Pallas kernels, call(): pl.pallas_call(kernel, in_specs=[kinds[c] for c in ins], out_specs=tuple(...  12.2 us
    ppermute x1, starting transfers between devices, body(): lax.ppermute(down, AXES, [((i + 1) % devices, i) for i in range(devices)])  6.71 us
    ppermute x1, waiting for transfers between devices, body(): nb = lax.ppermute(nb, AXES, skip_b)  6.56 us
    ppermute x1, starting transfers between devices, body(): mb = lax.ppermute(mb, AXES, swap_b)  4.69 us
    ppermute x1, waiting for transfers between devices, body(): na = lax.ppermute(na, AXES, skip_a)  3.8 us
    ppermute x1, starting transfers between devices, body(): nb = lax.ppermute(nb, AXES, skip_b)  2.46 us
    ppermute x1, starting transfers between devices, body(): lax.ppermute(up, AXES, [(i, (i + 1) % devices) for i in range(devices)])  1.68 us
    ppermute x1, waiting for transfers between devices, body(): mb = lax.ppermute(mb, AXES, swap_b)  1.67 us
  transfers between devices with their start and end apart: 6, of which 4 were waited for; matrix products, arithmetic and copies ran while one was open for 0% of the time, Pallas kernels for 16%

profile of v3, /device:TPU:0, one launch (start us, length us, event | category | flops | bytes accessed | tf_op | source)
XLA Modules:
  0.0 42.2 jit_solution(4270057430254854507)
XLA Ops:
  0.6 1.2 %shard_map.78 = (bf16[1296,128]{1,0:T(8,128)(2,1)S(1)}, bf16[1296,128]{1,0:T(8,128)(2,1)S(1)}) custom-call(s32[2,16]{1,0:T(2,128)} %bitcast.18, s32[2,4]{1,0:T(2,128)} %bitcast.20, bf16[4096,128]{1,0:T(8,128)(2,1)} %bitcast.12, bf16[1024,128]{1,0:T(8,128)(2,1)} %bitcast.16), custom_call_target="tpu_custom_call" | custom-call | tf_op jit(solution)/shard_map/pallas_call | solution.py:331
  1.9 1.7 %collective-permute-start = (bf16[1296,128]{1,0:T(8,128)(2,1)S(1)}, bf16[1296,128]{1,0:T(8,128)(2,1)S(1)}, u32[]{:S(2)}, u32[]{:S(2)}) collective-permute-start(bf16[1296,128]{1,0:T(8,128)(2,1)S(1)} %get-tuple-element.24), channel_id=1, source_target_pairs={{0,1},{1,2},{2,3},{3,4},{4,5},{5,6},{6,7},{7,8},{8,9},{9,10},{10,1... | collective-permute-start | bytes 995336 | tf_op jit(solution)/shard_map/ppermute | solution.py:372
  3.5 6.7 %collective-permute-start.1 = (bf16[1296,128]{1,0:T(8,128)(2,1)S(1)}, bf16[1296,128]{1,0:T(8,128)(2,1)S(1)}, u32[]{:S(2)}, u32[]{:S(2)}) collective-permute-start(bf16[1296,128]{1,0:T(8,128)(2,1)S(1)} %get-tuple-element.25), channel_id=1, source_target_pairs={{1,0},{2,1},{3,2},{4,3},{5,4},{6,5},{7,6},{8,7},{9,8},{10,9},{11,1... | collective-permute-start | bytes 995336 | tf_op jit(solution)/shard_map/ppermute | solution.py:373
  10.2 5.8 %shard_map.77 = (f32[8,128,640]{2,1,0:T(8,128)S(1)}, f32[6,128,1024]{2,1,0:T(8,128)S(1)}, bf16[768,384]{1,0:T(8,128)(2,1)S(1)}, bf16[768,512]{1,0:T(8,128)(2,1)S...) custom-call(s32[5,1,16]{2,1,0:T(1,128)} %bitcast.22, s32[2,16]{1,0:T(2,128)} %bitcast.19, ...), custom_call_target="tpu_custom_call" | custom-call | flops 1000000000 | bytes 8000000 | tf_op jit(solution)/shard_map/pallas_call | solution.py:331
  16.0 1.6 %collective-permute-done.from_low = bf16[1296,128]{1,0:T(8,128)(2,1)S(1)} collective-permute-done((bf16[1296,128]{1,0:T(8,128)(2,1)S(1)}, bf16[1296,128]{1,0:T(8,128)(2,1)S(1)}, u32[]{:S(2)}, u32[]{:S(2)}) %collective-permute-start) | collective-permute-done | bytes 331808 | tf_op jit(solution)/shard_map/ppermute | solution.py:372
  17.7 0.0 collective-permute-done.1.from_high
  17.7 2.7 %shard_map.79 = (f32[6,128,1024]{2,1,0:T(8,128)S(1)}, f32[128,640]{1,0:T(8,128)S(1)}, bf16[1280,128]{1,0:T(8,128)(2,1)S(1)}, bf16[1280,128]{1,0:T(8,128)(2,1)S(1...) custom-call(f32[8,128,640]{2,1,0:T(8,128)S(1)} %get-tuple-element.18.acc_in, ...), custom_call_target="tpu_custom_call" | custom-call | flops 2000000000 | bytes 8000000 | tf_op jit(solution)/shard_map/pallas_call | solution.py:331
  20.4 0.1 collective-permute-start.2
  20.5 4.7 %collective-permute-start.3 = (bf16[1280,128]{1,0:T(8,128)(2,1)S(1)}, bf16[1280,128]{1,0:T(8,128)(2,1)S(1)}, u32[]{:S(2)}, u32[]{:S(2)}) collective-permute-start(bf16[1280,128]{1,0:T(8,128)(2,1)S(1)} %get-tuple-element.29), channel_id=1, source_target_pairs={{0,127},{1,2},{2,1},{3,4},{4,3},{5,6},{6,5},{7,8},{8,7},{9,10},{10... | collective-permute-start | bytes 983048 | tf_op jit(solution)/shard_map/ppermute | solution.py:418
  25.2 0.0 collective-permute-start.4
  25.2 2.5 %collective-permute-start.5 = (bf16[512,128]{1,0:T(8,128)(2,1)S(1)}, bf16[512,128]{1,0:T(8,128)(2,1)S(1)}, u32[]{:S(2)}, u32[]{:S(2)}) collective-permute-start(bf16[512,128]{1,0:T(8,128)(2,1)S(1)} %get-tuple-element.31), channel_id=1, source_target_pairs={{0,126},{1,127},{2,4},{3,5},{4,2},{5,3},{6,8},{7,9},{8,6},{9,7},{1... | collective-permute-start | bytes 393224 | tf_op jit(solution)/shard_map/ppermute | solution.py:419
  27.6 1.0 %shard_map.80.coarse_in = bf16[3584,128]{1,0:T(8,128)(2,1)} custom-call(f32[6,128,1024]{2,1,0:T(8,128)S(1)} %get-tuple-element.26.part), custom_call_target="tpu_custom_call" | custom-call | flops 1000000 | bytes 3000000 | tf_op jit(solution)/shard_map/pallas_call | solution.py:331
  28.6 3.8 %collective-permute-done.4.na = bf16[512,128]{1,0:T(8,128)(2,1)S(1)} collective-permute-done((bf16[512,128]{1,0:T(8,128)(2,1)S(1)}, bf16[512,128]{1,0:T(8,128)(2,1)S(1)}, u32[]{:S(2)}, u32[]{:S(2)}) %collective-permute-start.4) | collective-permute-done | bytes 131104 | tf_op jit(solution)/shard_map/ppermute | solution.py:421
  32.4 6.6 %collective-permute-done.5.nb = bf16[512,128]{1,0:T(8,128)(2,1)S(1)} collective-permute-done((bf16[512,128]{1,0:T(8,128)(2,1)S(1)}, bf16[512,128]{1,0:T(8,128)(2,1)S(1)}, u32[]{:S(2)}, u32[]{:S(2)}) %collective-permute-start.5) | collective-permute-done | bytes 131104 | tf_op jit(solution)/shard_map/ppermute | solution.py:419
  39.0 0.0 collective-permute-done.2.ma
  39.0 1.7 %collective-permute-done.3.mb = bf16[1280,128]{1,0:T(8,128)(2,1)S(1)} collective-permute-done((bf16[1280,128]{1,0:T(8,128)(2,1)S(1)}, bf16[1280,128]{1,0:T(8,128)(2,1)S(1)}, u32[]{:S(2)}, u32[]{:S(2)}) %collective-permute-start.3) | collective-permute-done | bytes 327712 | tf_op jit(solution)/shard_map/ppermute | solution.py:418
  40.7 1.5 %shard_map.81 = (bf16[3584,128]{1,0:T(8,128)(2,1)}, bf16[896,128]{1,0:T(8,128)(2,1)}) custom-call(bf16[3584,128]{1,0:T(8,128)(2,1)} %shard_map.80.coarse_in, f32[6,128,1024]{2,1,0:T(8,128)S(1)} %get-tuple-element.26.part, f32[128,640]{1,0:T(8,128)S(1)} %get-tuple-element.27.fine, ...), custom_call_target="tpu_custom_call", output_to_operand_aliasing={{0}: (0, {})} | custom-call | tf_op jit(solution)/shard_map/pallas_call | solution.py:331
Async XLA Ops:
  1.9 15.8 %collective-permute-start = (bf16[1296,128]{1,0:T(8,128)(2,1)S(1)}, bf16[1296,128]{1,0:T(8,128)(2,1)S(1)}, u32[]{:S(2)}, u32[]{:S(2)}) collective-permute-start(bf16[1296,128]{1,0:T(8,128)(2,1)S(1)} %get-tuple-element.24), channel_id=1, source_target_pairs={{0,1},{1,2},{2,3},{3,4},{4,5},{5,6},{6,7},{7,8},{8,9},{9,10},{10,1... | collective-permute-start | bytes 995336 | tf_op jit(solution)/shard_map/ppermute | solution.py:372
  3.5 14.1 %collective-permute-start.1 = (bf16[1296,128]{1,0:T(8,128)(2,1)S(1)}, bf16[1296,128]{1,0:T(8,128)(2,1)S(1)}, u32[]{:S(2)}, u32[]{:S(2)}) collective-permute-start(bf16[1296,128]{1,0:T(8,128)(2,1)S(1)} %get-tuple-element.25), channel_id=1, source_target_pairs={{1,0},{2,1},{3,2},{4,3},{5,4},{6,5},{7,6},{8,7},{9,8},{10,9},{11,1... | collective-permute-start | bytes 995336 | tf_op jit(solution)/shard_map/ppermute | solution.py:373
  20.4 18.6 %collective-permute-start.2 = (bf16[1280,128]{1,0:T(8,128)(2,1)S(1)}, bf16[1280,128]{1,0:T(8,128)(2,1)S(1)}, u32[]{:S(2)}, u32[]{:S(2)}) collective-permute-start(bf16[1280,128]{1,0:T(8,128)(2,1)S(1)} %get-tuple-element.28), channel_id=1, source_target_pairs={{0,1},{1,0},{2,3},{3,2},{4,5},{5,4},{6,7},{7,6},{8,9},{9,8},{10,11... | collective-permute-start | bytes 983048 | tf_op jit(solution)/shard_map/ppermute | solution.py:420
  20.5 20.2 %collective-permute-start.3 = (bf16[1280,128]{1,0:T(8,128)(2,1)S(1)}, bf16[1280,128]{1,0:T(8,128)(2,1)S(1)}, u32[]{:S(2)}, u32[]{:S(2)}) collective-permute-start(bf16[1280,128]{1,0:T(8,128)(2,1)S(1)} %get-tuple-element.29), channel_id=1, source_target_pairs={{0,127},{1,2},{2,1},{3,4},{4,3},{5,6},{6,5},{7,8},{8,7},{9,10},{10... | collective-permute-start | bytes 983048 | tf_op jit(solution)/shard_map/ppermute | solution.py:418
  25.2 7.2 %collective-permute-start.4 = (bf16[512,128]{1,0:T(8,128)(2,1)S(1)}, bf16[512,128]{1,0:T(8,128)(2,1)S(1)}, u32[]{:S(2)}, u32[]{:S(2)}) collective-permute-start(bf16[512,128]{1,0:T(8,128)(2,1)S(1)} %get-tuple-element.30), channel_id=1, source_target_pairs={{0,2},{1,3},{2,0},{3,1},{4,6},{5,7},{6,4},{7,5},{8,10},{9,11},{10,... | collective-permute-start | bytes 393224 | tf_op jit(solution)/shard_map/ppermute | solution.py:421
  25.2 13.8 %collective-permute-start.5 = (bf16[512,128]{1,0:T(8,128)(2,1)S(1)}, bf16[512,128]{1,0:T(8,128)(2,1)S(1)}, u32[]{:S(2)}, u32[]{:S(2)}) collective-permute-start(bf16[512,128]{1,0:T(8,128)(2,1)S(1)} %get-tuple-element.31), channel_id=1, source_target_pairs={{0,126},{1,127},{2,4},{3,5},{4,2},{5,3},{6,8},{7,9},{8,6},{9,7},{1... | collective-permute-start | bytes 393224 | tf_op jit(solution)/shard_map/ppermute | solution.py:419

commit v4 on v3

v4 whole, which is shorter than its diff:
```python
import jax
import jax.numpy as jnp
from jax import lax
from jax.experimental import pallas as pl
from jax.experimental.pallas import tpu as pltpu
from jax.sharding import PartitionSpec as P


B = 128
K = 5
KC = 7
ROWS = 16
CROWS = 4
BF = jnp.bfloat16
F32 = jnp.float32
PM = 6 * B + 16
QM = 4 * B + 16
NACC = 8
AXES = ("gx", "gy")


def blk(i, n=1):
    return pl.ds(i * B, n * B)


def side_at(cols, r, ncoarse):
    step = cols[1, r] - cols[0, r]
    return jnp.where(jnp.logical_or(step == 1, step == 1 - ncoarse), 1, -1)


def place():
    return lax.axis_index(AXES)


def dot(a, b):
    return jnp.dot(a, b, preferred_element_type=F32)


def dot_t(a, b):
    return lax.dot_general(a, b, (((0,), (0,)), ((), ())), preferred_element_type=F32)


def pack_kernel(ncoarse, ncoarsest, pc_hbm, qc_hbm, p_hbm, p2_hbm, pu, qu, pd, qd, p_cols, p2_cols, sems):
    cols_in = [pltpu.make_async_copy(x, y, sems.at[4 + n]) for n, (x, y) in enumerate(((pc_hbm, p_cols), (qc_hbm, p2_cols)))]
    for copy in cols_in:
        copy.start()
    jobs = (
        (pu, p_hbm, p_cols, ncoarse, ROWS - 3, 3),
        (qu, p2_hbm, p2_cols, ncoarsest, CROWS - 2, 2),
        (pd, p_hbm, p_cols, ncoarse, 0, 3),
        (qd, p2_hbm, p2_cols, ncoarsest, 0, 2),
    )
    copies = [
        pltpu.make_async_copy(src.at[blk(2 * first, 2 * rows)], dst.at[blk(0, 2 * rows)], sems.at[n])
        for n, (dst, src, cols, ncols, first, rows) in enumerate(jobs)
    ]
    for copy in copies:
        copy.start()
    row = lax.broadcasted_iota(jnp.int32, (16, B), 0)
    for copy in cols_in:
        copy.wait()
    for dst, src, cols, ncols, first, rows in jobs:
        flags = jnp.zeros((16, B), F32)
        for r in range(rows):
            side = side_at(cols, first + r, ncols)
            flags = jnp.where(row == 2 * r, (side < 0).astype(F32), flags)
            flags = jnp.where(row == 2 * r + 1, (side > 0).astype(F32), flags)
        dst[pl.ds(2 * rows * B, 16), :] = flags.astype(BF)
    for copy in copies:
        copy.wait()


def bands_of(p_ref, cols, rows, ncoarse):
    out = []
    for r in rows:
        side = side_at(cols, r, ncoarse)
        p0 = p_ref[blk(2 * r), :]
        p1 = p_ref[blk(2 * r + 1), :]
        zero = jnp.zeros_like(p1)
        out.append((jnp.where(side < 0, p1, zero), p0, jnp.where(side > 0, p1, zero)))
    return out


def halo_bands(message, rows):
    flags = message[pl.ds(2 * rows * B, 16), :].astype(F32)
    out = []
    for r in range(rows):
        p0 = message[blk(2 * r), :]
        p1 = message[blk(2 * r + 1), :]
        lower = jnp.broadcast_to(flags[2 * r : 2 * r + 1, :], (B, B)).astype(BF)
        upper = jnp.broadcast_to(flags[2 * r + 1 : 2 * r + 2, :], (B, B)).astype(BF)
        out.append((p1 * lower, p0, p1 * upper))
    return out


def stack_bands(bands):
    return jnp.concatenate([jnp.concatenate(band, axis=1) for band in bands], axis=0)


def shift_at(a_cols, r, k, nfine):
    step = a_cols[k, 0, r] - a_cols[0, 0, r]
    return jnp.where(step > 3, step - nfine, jnp.where(step < -3, step + nfine, step))


def flip(x):
    return jnp.transpose(x, (1, 0))


def is_early():
    return lax.axis_index("gy") % 4 == 0


def group_products(g, a_cols, p_cols, a_ref, p_ref, accs, nfine, ncoarse, store):
    for r in range(4 * g, 4 * g + 4):
        acc = accs[r % len(accs)]
        for s in range(5):
            acc[s] = jnp.zeros((B, B), F32)
        for k in range(K):
            if k == 0:
                v, side, slot0 = r, side_at(p_cols, r, ncoarse), 2
                w0, w1 = p_ref[blk(2 * r), :], p_ref[blk(2 * r + 1), :]
            else:
                v = r + shift_at(a_cols, r, k, nfine)
                inside = jnp.logical_and(v >= 0, v < ROWS)
                v = jnp.clip(v, 0, ROWS - 1)
                side = side_at(p_cols, v, ncoarse)
                slot0 = jnp.where(inside, lax.shift_right_logical(v, 2) - g + 2, 6)
                w0 = p_ref[pl.ds(pl.multiple_of(v * 2 * B, 2 * B), B), :]
                w1 = p_ref[pl.ds(pl.multiple_of(v * 2 * B + B, B), B), :]
            terms = dot(a_ref[blk(r * K + k), :], jnp.concatenate([w0, w1], axis=1))
            acc[slot0] += terms[:, :B]
            acc[slot0 + side] += terms[:, B:]
        for s in range(5):
            store(r, s, acc[s])


def group_rows(g):
    return pl.ds(4 * g * K * B, 4 * K * B)


def start_all(pairs, sems):
    copies = [pltpu.make_async_copy(src, dst, sems.at[n]) for n, (src, dst) in enumerate(pairs)]
    for copy in copies:
        copy.start()
    return copies


def early_kernel(nfine, ncoarse, ac_hbm, pc_hbm, a_hbm, p_hbm, prod, a_cols, p_cols, a_ref, p_ref, sems, *accs):
    @pl.when(is_early())
    def _():
        pairs = [(ac_hbm, a_cols), (pc_hbm, p_cols), (p_hbm, p_ref)]
        pairs += [(a_hbm.at[group_rows(g)], a_ref.at[group_rows(g)]) for g in (0, 3)]
        for copy in start_all(pairs, sems):
            copy.wait()

        def store(r, s, value):
            prod[blk(4 * (r // 12) + r % 4), s * B : (s + 1) * B] = value.astype(BF)

        for g in (0, 3):
            group_products(g, a_cols, p_cols, a_ref, p_ref, accs, nfine, ncoarse, store)


def inner_kernel(
    nfine, ncoarse, ncoarsest, prod_in, ac_hbm, pc_hbm, qc_hbm, a_hbm, p_hbm, p2_hbm,
    prod, part_out, edge_out, wt_out, own_out, ownt_out,
    a_cols, p_cols, p2_cols, a_ref, p_ref, p2_ref, middle, sems, *accs,
):
    pairs = [(ac_hbm, a_cols), (pc_hbm, p_cols), (qc_hbm, p2_cols), (p_hbm, p_ref)]
    pairs += [(a_hbm.at[group_rows(g)], a_ref.at[group_rows(g)]) for g in (0, 3, 1, 2)]
    pairs += [(p2_hbm, p2_ref)]
    copies = start_all(pairs, sems)
    for copy in copies[:6]:
        copy.wait()

    @pl.when(jnp.logical_not(is_early()))
    def _():
        def store(r, s, value):
            prod[blk(4 * (r // 12) + r % 4), s * B : (s + 1) * B] = value.astype(BF)

        for g in (0, 3):
            group_products(g, a_cols, p_cols, a_ref, p_ref, accs, nfine, ncoarse, store)

    for copy in copies[6:]:
        copy.wait()

    def store_middle(r, s, value):
        middle[blk(r - 4), s * B : (s + 1) * B] = value.astype(BF)

    for g in (1, 2):
        group_products(g, a_cols, p_cols, a_ref, p_ref, accs, nfine, ncoarse, store_middle)
    for side in (0, 1):
        first = 0 if side == 0 else ROWS - 3
        for n in range(3):
            r = first + n
            for h in range(3):
                want = (h - 3 if side == 0 else ROWS + h) - r
                at = jnp.int32(0)
                found = jnp.int32(0)
                for k in range(1, K):
                    hit = (shift_at(a_cols, r, k, nfine) == want).astype(jnp.int32)
                    at = at + hit * k
                    found = found + hit
                block = a_ref[pl.ds(pl.multiple_of((r * K + at) * B, B), B), :]
                keep = jnp.where(found > 0, block, jnp.zeros_like(block))
                edge_out[blk(3 * side + n), h * B : (h + 1) * B] = keep if abs(want) <= 3 else jnp.zeros((B, B), BF)
        bands = bands_of(p_ref, p_cols, range(first, first + 3), ncoarse)
        for n in range(3):
            for m in range(3):
                wt_out[blk(3 * side + m), n * B : (n + 1) * B] = flip(bands[n][m])
    own = bands_of(p2_ref, p2_cols, range(CROWS), ncoarsest)
    for n in range(4):
        for m in range(3):
            own_out[blk(n), m * B : (m + 1) * B] = own[n][m]
            ownt_out[blk(m), n * B : (n + 1) * B] = flip(own[n][m])
    part_out[...] = jnp.zeros_like(part_out)
    for g in (1, 2, 0, 3):
        bands = stack_bands(bands_of(p_ref, p_cols, range(4 * g, 4 * g + 4), ncoarse))
        rows = middle[blk(4 * (g - 1), 4), :] if g in (1, 2) else prod[blk(4 * (g // 3), 4), :]
        terms = dot_t(bands, rows)
        for m in range(3):
            at = slice(g * B, (g + 5) * B)
            part_out[g + m, :, at] = part_out[g + m, :, at] + terms[m * B : (m + 1) * B, :]


def middle_kernel(part_in, edge, wt, p_low, p_high, part):
    for side in (0, 1):
        halo = stack_bands(halo_bands(p_high if side else p_low, 3))
        extra = dot(edge[blk(3 * side, 3), :], halo).astype(BF)
        terms = dot(wt[blk(3 * side, 3), :], extra)
        for m in range(3):
            j = 3 * side + m
            at = slice(5 * side * B, (5 * side + 3) * B)
            part[j, :, at] = part_in[j, :, at] + terms[m * B : (m + 1) * B, :]


def outer_kernel(part, own, ownt, q_low, q_high, fine_out, ma, mb, na, nb, cp):
    d = place()
    even = d % 2 == 0
    low = halo_bands(q_low, 2)
    high = halo_bands(q_high, 2)
    lines = part[...].astype(BF).reshape(6 * B, 8 * B)
    ta = dot(lines[0 : 4 * B, 0 : 2 * B], stack_bands(low))
    tb = dot(lines[:, 2 * B : 6 * B], own[...])
    tc = dot(lines[2 * B : 6 * B, 6 * B : 8 * B], stack_bands(high))
    for e in range(5):
        for i in range(6):
            pieces = []
            if e < 3 and i < 4:
                pieces.append(ta[i * B : (i + 1) * B, e * B : (e + 1) * B])
            if 1 <= e < 4:
                pieces.append(tb[i * B : (i + 1) * B, (e - 1) * B : e * B])
            if e >= 2 and i >= 2:
                pieces.append(tc[(i - 2) * B : (i - 1) * B, (e - 2) * B : (e - 1) * B])
            value = sum(pieces[1:], pieces[0]) if pieces else jnp.zeros((B, B), F32)
            cp[blk(i), e * B : (e + 1) * B] = value.astype(BF)
    gm = dot_t(stack_bands(low[1:2]), cp[blk(0), 0 : 4 * B])
    g0 = dot(ownt[...], cp[blk(1, 4), :])
    gp = dot_t(stack_bands(high[0:1]), cp[blk(5), B : 5 * B])

    def low_at(m, e):
        return gm[m * B : (m + 1) * B, e * B : (e + 1) * B] if e < 4 else 0.0

    def own_at(m, e):
        return g0[m * B : (m + 1) * B, e * B : (e + 1) * B]

    def high_at(m, e):
        return gp[m * B : (m + 1) * B, (e - 1) * B : e * B] if e > 0 else 0.0

    for e in range(5):
        fine_out[:, e * B : (e + 1) * B] = low_at(2, e) + own_at(1, e) + high_at(0, e)
    to_low = [(low_at(1, e) + own_at(0, e)).astype(BF) for e in range(5)]
    to_high = [(own_at(2, e) + high_at(1, e)).astype(BF) for e in range(5)]
    two_low = [low_at(0, e).astype(BF) for e in range(4)]
    two_high = [high_at(2, e).astype(BF) for e in range(1, 5)]

    def put(dst, coarse_row, q0, fine):
        for t in range(5):
            dst[blk(t), :] = part[coarse_row, :, (q0 + t) * B : (q0 + t + 1) * B].astype(BF)
            dst[blk(5 + t), :] = fine[t]

    def put2(dst, fine):
        for t in range(4):
            dst[blk(t), :] = fine[t]

    @pl.when(even)
    def _():
        put(mb, 0, 0, to_low)
        put(ma, 5, 3, to_high)

    @pl.when(jnp.logical_not(even))
    def _():
        put(ma, 0, 0, to_low)
        put(mb, 5, 3, to_high)

    even2 = (d // 2) % 2 == 0

    @pl.when(even2)
    def _():
        put2(nb, two_low)
        put2(na, two_high)

    @pl.when(jnp.logical_not(even2))
    def _():
        put2(na, two_low)
        put2(nb, two_high)


def column_block(part, j, t):
    q = t + j - 1
    if 0 <= q < 8:
        return part[j + 1, :, q * B : (q + 1) * B]
    return jnp.zeros((B, B), F32)


def store_kernel(part, coarse_hbm, rows, sems):
    copies = []
    for j in range(CROWS):
        for t in range(KC):
            rows[blk(j * KC + t), :] = column_block(part, j, t).astype(BF)
        at = blk(j * KC, KC)
        copies.append(pltpu.make_async_copy(rows.at[at], coarse_hbm.at[at], sems.at[j]))
        copies[-1].start()
    for copy in copies:
        copy.wait()


def last_kernel(coarse_in, part, fine, ma, mb, na, nb, coarse_out, coarsest_out, rows, sems):
    d = place()
    even = d % 2 == 0
    even2 = (d // 2) % 2 == 0

    def one(low, t):
        if low:
            return jnp.where(even, mb[blk(t), :], ma[blk(t), :]).astype(F32)
        return jnp.where(even, ma[blk(t), :], mb[blk(t), :]).astype(F32)

    def two(low, t):
        if low:
            return jnp.where(even2, nb[blk(t), :], na[blk(t), :]).astype(F32)
        return jnp.where(even2, na[blk(t), :], nb[blk(t), :]).astype(F32)

    for t in range(KC):
        value = jnp.zeros((B, B), F32)
        if 1 <= t < 6:
            value = value + fine[:, (t - 1) * B : t * B]
        if t < 5:
            value = value + one(True, 5 + t)
        if t >= 2:
            value = value + one(False, 5 + t - 2)
        if t < 4:
            value = value + two(True, t)
        if t >= 3:
            value = value + two(False, t - 3)
        rows[blk(10 + t), :] = value.astype(BF)
    copies = [pltpu.make_async_copy(rows.at[blk(10, KC)], coarsest_out, sems.at[2])]
    copies[0].start()
    for n, j in enumerate((0, 3)):
        for t in range(5):
            rows[blk(5 * n + t), :] = (column_block(part, j, t + 2 * n) + one(n == 0, t)).astype(BF)
        at = blk(j * KC + 2 * n, 5)
        copies.append(pltpu.make_async_copy(rows.at[blk(5 * n, 5)], coarse_out.at[at], sems.at[n]))
        copies[-1].start()
    for copy in copies:
        copy.wait()


def call(kernel, ins, outs, args, scratch=(), cost=None, **kw):
    vmem = pl.BlockSpec(memory_space=pltpu.VMEM)
    hbm = pl.BlockSpec(memory_space=pltpu.HBM)
    kinds = {"v": vmem, "h": hbm}
    aliased = kw.get("input_output_aliases", {})
    args = [
        pltpu.with_memory_space_constraint(x, pltpu.HBM) if c == "h" and n not in aliased else x
        for n, (c, x) in enumerate(zip(ins, args))
    ]
    return pl.pallas_call(
        kernel,
        in_specs=[kinds[c] for c in ins],
        out_specs=tuple(kinds[c] for c, _, _ in outs),
        out_shape=tuple(jax.ShapeDtypeStruct(shape, dtype) for _, shape, dtype in outs),
        scratch_shapes=list(scratch),
        compiler_params=pltpu.CompilerParams(vmem_limit_bytes=40 * 1024 * 1024),
        cost_estimate=cost,
        **kw,
    )(*args)


def body(a_vals, a_cols, p_vals, p_cols, p2_vals, p2_cols):
    devices = lax.axis_size(AXES)
    nfine = ROWS * devices
    ncoarse = CROWS * devices
    a_cols = jnp.transpose(a_cols, (2, 0, 1))
    p_cols = p_cols.reshape(ROWS, 2).T
    p2_cols = p2_cols.reshape(CROWS, 2).T
    a = a_vals.reshape(ROWS * K * B, B)
    p = p_vals.reshape(ROWS * 2 * B, B)
    p2 = p2_vals.reshape(CROWS * 2 * B, B)
    swap_a = [(i, i ^ 1) for i in range(devices)]
    swap_b = [(i, (i + 1) % devices if i % 2 else (i - 1) % devices) for i in range(devices)]
    skip_a = [(i, i ^ 2) for i in range(devices)]
    skip_b = [(i, (i + 2) % devices if i & 2 else (i - 2) % devices) for i in range(devices)]

    def pack(*refs):
        pack_kernel(ncoarse, devices, *refs)

    pu, qu, pd, qd = call(
        pack,
        "hhhh",
        [("v", (PM, B), BF), ("v", (QM, B), BF), ("v", (PM, B), BF), ("v", (QM, B), BF)],
        (p_cols, p2_cols, p, p2),
        [
            pltpu.SMEM((2, ROWS), jnp.int32),
            pltpu.SMEM((2, CROWS), jnp.int32),
            pltpu.SemaphoreType.DMA((6,)),
        ],
    )
    up = [(i, (i + 1) % devices) for i in range(devices)]
    down = [((i + 1) % devices, i) for i in range(devices)]
    p_low = lax.ppermute(pu, AXES, up)
    q_low = lax.ppermute(qu, AXES, up)

    def early(*refs):
        early_kernel(nfine, ncoarse, *refs)

    (prod,) = call(
        early,
        "hhhh",
        [("v", (8 * B, 5 * B), BF)],
        (a_cols, p_cols, a, p),
        [
            pltpu.SMEM((K, 1, ROWS), jnp.int32),
            pltpu.SMEM((2, ROWS), jnp.int32),
            pltpu.VMEM((ROWS * K * B, B), BF),
            pltpu.VMEM((ROWS * 2 * B, B), BF),
            pltpu.SemaphoreType.DMA((5,)),
            *[pltpu.VMEM((8, B, B), F32) for _ in range(NACC)],
        ],
        pl.CostEstimate(flops=10**6, bytes_accessed=10**6, transcendentals=0),
    )
    p_high = lax.ppermute(pd, AXES, down)
    q_high = lax.ppermute(qd, AXES, down)

    def inner(*refs):
        inner_kernel(nfine, ncoarse, devices, *refs)

    prod, part, edge, wt, own, ownt = call(
        inner,
        "vhhhhhh",
        [
            ("v", (8 * B, 5 * B), BF),
            ("v", (6, B, 8 * B), F32),
            ("v", (6 * B, 3 * B), BF),
            ("v", (6 * B, 3 * B), BF),
            ("v", (4 * B, 3 * B), BF),
            ("v", (3 * B, 4 * B), BF),
        ],
        (prod, a_cols, p_cols, p2_cols, a, p, p2),
        [
            pltpu.SMEM((K, 1, ROWS), jnp.int32),
            pltpu.SMEM((2, ROWS), jnp.int32),
            pltpu.SMEM((2, CROWS), jnp.int32),
            pltpu.VMEM((ROWS * K * B, B), BF),
            pltpu.VMEM((ROWS * 2 * B, B), BF),
            pltpu.VMEM((CROWS * 2 * B, B), BF),
            pltpu.VMEM((8 * B, 5 * B), BF),
            pltpu.SemaphoreType.DMA((9,)),
            *[pltpu.VMEM((8, B, B), F32) for _ in range(NACC)],
        ],
        pl.CostEstimate(flops=10**9, bytes_accessed=8 * 10**6, transcendentals=0),
        input_output_aliases={0: 0},
    )
    (part,) = call(
        middle_kernel,
        "vvvvv",
        [("v", (6, B, 8 * B), F32)],
        (part, edge, wt, p_low, p_high),
        cost=pl.CostEstimate(flops=10**9, bytes_accessed=4 * 10**6, transcendentals=0),
        input_output_aliases={0: 0},
    )
    fine, ma, mb, na, nb = call(
        outer_kernel,
        "vvvvv",
        [
            ("v", (B, 5 * B), F32),
            ("v", (10 * B, B), BF),
            ("v", (10 * B, B), BF),
            ("v", (4 * B, B), BF),
            ("v", (4 * B, B), BF),
        ],
        (part, own, ownt, q_low, q_high),
        [pltpu.VMEM((6 * B, 5 * B), BF)],
        pl.CostEstimate(flops=10**9, bytes_accessed=4 * 10**6, transcendentals=0),
    )
    mb = lax.ppermute(mb, AXES, swap_b)
    nb = lax.ppermute(nb, AXES, skip_b)
    ma = lax.ppermute(ma, AXES, swap_a)
    na = lax.ppermute(na, AXES, skip_a)
    (coarse,) = call(
        store_kernel,
        "v",
        [("h", (CROWS * KC * B, B), BF)],
        (part,),
        [pltpu.VMEM((CROWS * KC * B, B), BF), pltpu.SemaphoreType.DMA((CROWS,))],
        pl.CostEstimate(flops=10**6, bytes_accessed=3 * 10**6, transcendentals=0),
    )
    coarse, coarsest = call(
        last_kernel,
        "hvvvvvv",
        [("h", (CROWS * KC * B, B), BF), ("h", (KC * B, B), BF)],
        (coarse, part, fine, ma, mb, na, nb),
        [pltpu.VMEM(((10 + KC) * B, B), BF), pltpu.SemaphoreType.DMA((3,))],
        input_output_aliases={0: 0},
    )
    return coarse.reshape(1, CROWS, KC, B, B), coarsest.reshape(1, 1, KC, B, B)


def solution(mesh):
    blocks = P(None, AXES, None, None, None)
    cols = P(None, AXES, None)

    return jax.shard_map(
        body,
        mesh=mesh,
        in_specs=(blocks, cols, blocks, cols, blocks, cols),
        out_specs=(blocks, blocks),
        check_vma=False,
    )
```

time: 42.3 us -> 46.5 us (1.099)
  starting transfers between devices: 15.6 us -> 19.7 us
  Pallas kernels: 12.2 us -> 13.5 us
  waiting for transfers between devices: 13.7 us -> 12.4 us
    ppermute x2 -> x4, starting transfers between devices: 8.39 us -> 15.6 us  [the longest x1 7.17 us: body(): q_high = lax.ppermute(qd, AXES, down)]
    ppermute x1, starting transfers between devices: 4.69 us -> 1.02 us  [body(): mb = lax.ppermute(mb, AXES, swap_b)]
    ppermute x1, starting transfers between devices: 0.01 us -> 3.06 us  [body(): na = lax.ppermute(na, AXES, skip_a)]
    ppermute x1, starting transfers between devices: 2.46 us -> 0.01 us  [body(): nb = lax.ppermute(nb, AXES, skip_b)]
    ppermute x2 -> x4, waiting for transfers between devices: 1.62 us -> 0.01 us  [the longest x1 0.01 us: body(): p_high = lax.ppermute(pd, AXES, down)]
    ppermute x1, waiting for transfers between devices: 1.67 us -> 3.12 us  [body(): mb = lax.ppermute(mb, AXES, swap_b)]
    ppermute x1, waiting for transfers between devices: 3.8 us -> 2.52 us  [body(): na = lax.ppermute(na, AXES, skip_a)]
    pallas_call x5 -> x7, Pallas kernels: 12.2 us -> 13.5 us  [call(): pl.pallas_call(kernel, in_specs=[kinds[c] for c in ins], out_specs=tuple(...]
  transfers between devices with their start and end apart: 6 -> 8, of which waited for: 4 -> 3; matrix products, arithmetic and copies ran while one was open for 0% -> 0% of each run, Pallas kernels for 16% -> 21%
where the time goes in v4:
time: 46.5 us; the launch traced here: 46.3 us
  starting transfers between devices  19.7 us (42%)
  Pallas kernels  13.5 us (29%)
  waiting for transfers between devices  12.4 us (27%)
  between operations  0.72 us (2%)
    pallas_call x7, Pallas kernels, call(): pl.pallas_call(kernel, in_specs=[kinds[c] for c in ins], out_specs=tuple(...  13.5 us
    ppermute x1, starting transfers between devices, body(): q_high = lax.ppermute(qd, AXES, down)  7.17 us
    ppermute x1, starting transfers between devices, body(): p_high = lax.ppermute(pd, AXES, down)  6.71 us
    ppermute x1, waiting for transfers between devices, body(): nb = lax.ppermute(nb, AXES, skip_b)  6.71 us
    ppermute x1, waiting for transfers between devices, body(): mb = lax.ppermute(mb, AXES, swap_b)  3.12 us
    ppermute x1, starting transfers between devices, body(): na = lax.ppermute(na, AXES, skip_a)  3.06 us
    ppermute x1, waiting for transfers between devices, body(): na = lax.ppermute(na, AXES, skip_a)  2.52 us
    ppermute x1, starting transfers between devices, body(): p_low = lax.ppermute(pu, AXES, up)  1.68 us
  transfers between devices with their start and end apart: 8, of which 3 were waited for; matrix products, arithmetic and copies ran while one was open for 0% of the time, Pallas kernels for 21%

profile of v4, /device:TPU:0, one launch (start us, length us, event | category | flops | bytes accessed | tf_op | source)
XLA Modules:
  0.0 46.3 jit_solution(1804779746216659782)
XLA Ops:
  0.6 1.2 %shard_map.79 = (bf16[784,128]{1,0:T(8,128)(2,1)S(1)}, bf16[528,128]{1,0:T(8,128)(2,1)S(1)}, bf16[784,128]{1,0:T(8,128)(2,1)S(1)}, bf16[528,128]{1,0:T(8,128)(2,1)S(1)}) custom-call(s32[2,16]{1,0:T(2,128)} %bitcast.22, s32[2,4]{1,0:T(2,128)} %bitcast.25, bf16[4096,128]{1,0:T(8,128)(2,1)} %bitcast.14, bf16[1024,128]{1,0:T(8,128)(2,1)} %bitcast.18), custom_call_target="tpu_custom_call" | custom-call | tf_op jit(solution)/shard_map/pallas_call | solution.py:376
  1.9 1.7 %collective-permute-start = (bf16[784,128]{1,0:T(8,128)(2,1)S(1)}, bf16[784,128]{1,0:T(8,128)(2,1)S(1)}, u32[]{:S(2)}, u32[]{:S(2)}) collective-permute-start(bf16[784,128]{1,0:T(8,128)(2,1)S(1)} %get-tuple-element.21), channel_id=1, source_target_pairs={{0,1},{1,2},{2,3},{3,4},{4,5},{5,6},{6,7},{7,8},{8,9},{9,10},{10,1... | collective-permute-start | bytes 602120 | tf_op jit(solution)/shard_map/ppermute | solution.py:419
  3.5 6.7 %collective-permute-start.1 = (bf16[784,128]{1,0:T(8,128)(2,1)S(1)}, bf16[784,128]{1,0:T(8,128)(2,1)S(1)}, u32[]{:S(2)}, u32[]{:S(2)}) collective-permute-start(bf16[784,128]{1,0:T(8,128)(2,1)S(1)} %get-tuple-element.22), channel_id=1, source_target_pairs={{1,0},{2,1},{3,2},{4,3},{5,4},{6,5},{7,6},{8,7},{9,8},{10,9},{11,1... | collective-permute-start | bytes 602120 | tf_op jit(solution)/shard_map/ppermute | solution.py:440
  10.2 0.0 collective-permute-start.2
  10.3 7.2 %collective-permute-start.3 = (bf16[528,128]{1,0:T(8,128)(2,1)S(1)}, bf16[528,128]{1,0:T(8,128)(2,1)S(1)}, u32[]{:S(2)}, u32[]{:S(2)}) collective-permute-start(bf16[528,128]{1,0:T(8,128)(2,1)S(1)} %get-tuple-element.26), channel_id=1, source_target_pairs={{1,0},{2,1},{3,2},{4,3},{5,4},{6,5},{7,6},{8,7},{9,8},{10,9},{11,1... | collective-permute-start | bytes 405512 | tf_op jit(solution)/shard_map/ppermute | solution.py:441
  17.4 2.9 %shard_map.77.refs_0_ = bf16[1024,640]{1,0:T(8,128)(2,1)S(1)} custom-call(s32[5,1,16]{2,1,0:T(1,128)} %bitcast.20, s32[2,16]{1,0:T(2,128)} %bitcast.23, bf16[10240,128]{1,0:T(8,128)(2,1)} %bitcast.12, bf16[4096,128]{1,0:T(8,128)(2,1)} %bitcast.15), custom_call_target="tpu_custom_call" | custom-call | flops 1000000 | bytes 1000000 | tf_op jit(solution)/shard_map/pallas_call | solution.py:376
  20.3 4.8 %shard_map.78 = (bf16[1024,640]{1,0:T(8,128)(2,1)S(1)}, f32[6,128,1024]{2,1,0:T(8,128)S(1)}, bf16[768,384]{1,0:T(8,128)(2,1)S(1)}, bf16[768,384]{1,0:T(8,128)(2,...) custom-call(bf16[1024,640]{1,0:T(8,128)(2,1)S(1)} %shard_map.77.refs_0_, ...), custom_call_target="tpu_custom_call", output_to_operand_aliasing={{0}: (0, {})} | custom-call | flops 1000000000 | bytes 8000000 | tf_op jit(solution)/shard_map/pallas_call | solution.py:376
  25.2 0.0 collective-permute-done.p_low
  25.2 0.0 collective-permute-done.1.p_high
  25.2 1.1 %shard_map.80.part = f32[6,128,1024]{2,1,0:T(8,128)S(1)} custom-call(f32[6,128,1024]{2,1,0:T(8,128)S(1)} %get-tuple-element.18.part_in, bf16[768,384]{1,0:T(8,128)(2,1)S(1)} %get-tuple-element.19.edge, bf16[768,384]{1,0:T(8,128)(2,1)S(1)} %get-tuple-element.20.wt, bf16[784,128]{1,0:T(8,128)(2,1)S(1)} %collective-permute-done.p_low, ...), custom_call_target="tpu_custom_call", output_to_operand_aliasing={{}: (0, {})} | custom-call | flops 1000000000 | bytes 4000000 | tf_op jit(solution)/shard_map/pallas_call | solution.py:376
  26.3 0.0 collective-permute-done.2.q_low
  26.3 0.0 collective-permute-done.3.q_high
  26.4 1.5 %shard_map.82 = (f32[128,640]{1,0:T(8,128)S(1)}, bf16[1280,128]{1,0:T(8,128)(2,1)S(1)}, bf16[1280,128]{1,0:T(8,128)(2,1)S(1)}, bf16[512,128]{1,0:T(8,128)(2,1)S(1)}, bf16[512,128]{1,0:T(8,128)(2,1)S(1)}) custom-call(f32[6,128,1024]{2,1,0:T(8,128)S(1)} %shard_map.80.part, bf16[512,384]{1,0:T(8,128)(2,1)S(1)} %get-tuple-element.23.own, ...), custom_call_target="tpu_custom_call" | custom-call | flops 1000000000 | bytes 4000000 | tf_op jit(solution)/shard_map/pallas_call | solution.py:376
  27.8 0.1 collective-permute-start.4
  27.9 1.0 %collective-permute-start.5 = (bf16[1280,128]{1,0:T(8,128)(2,1)S(1)}, bf16[1280,128]{1,0:T(8,128)(2,1)S(1)}, u32[]{:S(2)}, u32[]{:S(2)}) collective-permute-start(bf16[1280,128]{1,0:T(8,128)(2,1)S(1)} %get-tuple-element.29), channel_id=1, source_target_pairs={{0,127},{1,2},{2,1},{3,4},{4,3},{5,6},{6,5},{7,8},{8,7},{9,10},{10... | collective-permute-start | bytes 983048 | tf_op jit(solution)/shard_map/ppermute | solution.py:494
  28.9 3.1 %collective-permute-start.6 = (bf16[512,128]{1,0:T(8,128)(2,1)S(1)}, bf16[512,128]{1,0:T(8,128)(2,1)S(1)}, u32[]{:S(2)}, u32[]{:S(2)}) collective-permute-start(bf16[512,128]{1,0:T(8,128)(2,1)S(1)} %get-tuple-element.30), channel_id=1, source_target_pairs={{0,2},{1,3},{2,0},{3,1},{4,6},{5,7},{6,4},{7,5},{8,10},{9,11},{10,... | collective-permute-start | bytes 393224 | tf_op jit(solution)/shard_map/ppermute | solution.py:497
  32.0 0.0 collective-permute-start.7
  32.0 1.0 %shard_map.81.coarse_in = bf16[3584,128]{1,0:T(8,128)(2,1)} custom-call(f32[6,128,1024]{2,1,0:T(8,128)S(1)} %shard_map.80.part), custom_call_target="tpu_custom_call" | custom-call | flops 1000000 | bytes 3000000 | tf_op jit(solution)/shard_map/pallas_call | solution.py:376
  33.0 2.5 %collective-permute-done.6.na = bf16[512,128]{1,0:T(8,128)(2,1)S(1)} collective-permute-done((bf16[512,128]{1,0:T(8,128)(2,1)S(1)}, bf16[512,128]{1,0:T(8,128)(2,1)S(1)}, u32[]{:S(2)}, u32[]{:S(2)}) %collective-permute-start.6) | collective-permute-done | bytes 131104 | tf_op jit(solution)/shard_map/ppermute | solution.py:497
  35.5 6.7 %collective-permute-done.7.nb = bf16[512,128]{1,0:T(8,128)(2,1)S(1)} collective-permute-done((bf16[512,128]{1,0:T(8,128)(2,1)S(1)}, bf16[512,128]{1,0:T(8,128)(2,1)S(1)}, u32[]{:S(2)}, u32[]{:S(2)}) %collective-permute-start.7) | collective-permute-done | bytes 131104 | tf_op jit(solution)/shard_map/ppermute | solution.py:495
  42.2 0.0 collective-permute-done.4.ma
  42.2 3.1 %collective-permute-done.5.mb = bf16[1280,128]{1,0:T(8,128)(2,1)S(1)} collective-permute-done((bf16[1280,128]{1,0:T(8,128)(2,1)S(1)}, bf16[1280,128]{1,0:T(8,128)(2,1)S(1)}, u32[]{:S(2)}, u32[]{:S(2)}) %collective-permute-start.5) | collective-permute-done | bytes 327712 | tf_op jit(solution)/shard_map/ppermute | solution.py:494
  45.4 1.0 %shard_map.83 = (bf16[3584,128]{1,0:T(8,128)(2,1)}, bf16[896,128]{1,0:T(8,128)(2,1)}) custom-call(bf16[3584,128]{1,0:T(8,128)(2,1)} %shard_map.81.coarse_in, f32[6,128,1024]{2,1,0:T(8,128)S(1)} %shard_map.80.part, f32[128,640]{1,0:T(8,128)S(1)} %get-tuple-element.27.fine, ...), custom_call_target="tpu_custom_call", output_to_operand_aliasing={{0}: (0, {})} | custom-call | tf_op jit(solution)/shard_map/pallas_call | solution.py:376
Async XLA Ops:
  1.9 23.3 %collective-permute-start = (bf16[784,128]{1,0:T(8,128)(2,1)S(1)}, bf16[784,128]{1,0:T(8,128)(2,1)S(1)}, u32[]{:S(2)}, u32[]{:S(2)}) collective-permute-start(bf16[784,128]{1,0:T(8,128)(2,1)S(1)} %get-tuple-element.21), channel_id=1, source_target_pairs={{0,1},{1,2},{2,3},{3,4},{4,5},{5,6},{6,7},{7,8},{8,9},{9,10},{10,1... | collective-permute-start | bytes 602120 | tf_op jit(solution)/shard_map/ppermute | solution.py:419
  3.5 21.6 %collective-permute-start.1 = (bf16[784,128]{1,0:T(8,128)(2,1)S(1)}, bf16[784,128]{1,0:T(8,128)(2,1)S(1)}, u32[]{:S(2)}, u32[]{:S(2)}) collective-permute-start(bf16[784,128]{1,0:T(8,128)(2,1)S(1)} %get-tuple-element.22), channel_id=1, source_target_pairs={{1,0},{2,1},{3,2},{4,3},{5,4},{6,5},{7,6},{8,7},{9,8},{10,9},{11,1... | collective-permute-start | bytes 602120 | tf_op jit(solution)/shard_map/ppermute | solution.py:440
  10.2 16.1 %collective-permute-start.2 = (bf16[528,128]{1,0:T(8,128)(2,1)S(1)}, bf16[528,128]{1,0:T(8,128)(2,1)S(1)}, u32[]{:S(2)}, u32[]{:S(2)}) collective-permute-start(bf16[528,128]{1,0:T(8,128)(2,1)S(1)} %get-tuple-element.25), channel_id=1, source_target_pairs={{0,1},{1,2},{2,3},{3,4},{4,5},{5,6},{6,7},{7,8},{8,9},{9,10},{10,1... | collective-permute-start | bytes 405512 | tf_op jit(solution)/shard_map/ppermute | solution.py:420
  10.3 16.1 %collective-permute-start.3 = (bf16[528,128]{1,0:T(8,128)(2,1)S(1)}, bf16[528,128]{1,0:T(8,128)(2,1)S(1)}, u32[]{:S(2)}, u32[]{:S(2)}) collective-permute-start(bf16[528,128]{1,0:T(8,128)(2,1)S(1)} %get-tuple-element.26), channel_id=1, source_target_pairs={{1,0},{2,1},{3,2},{4,3},{5,4},{6,5},{7,6},{8,7},{9,8},{10,9},{11,1... | collective-permute-start | bytes 405512 | tf_op jit(solution)/shard_map/ppermute | solution.py:441
  27.8 14.4 %collective-permute-start.4 = (bf16[1280,128]{1,0:T(8,128)(2,1)S(1)}, bf16[1280,128]{1,0:T(8,128)(2,1)S(1)}, u32[]{:S(2)}, u32[]{:S(2)}) collective-permute-start(bf16[1280,128]{1,0:T(8,128)(2,1)S(1)} %get-tuple-element.28), channel_id=1, source_target_pairs={{0,1},{1,0},{2,3},{3,2},{4,5},{5,4},{6,7},{7,6},{8,9},{9,8},{10,11... | collective-permute-start | bytes 983048 | tf_op jit(solution)/shard_map/ppermute | solution.py:496
  27.9 17.4 %collective-permute-start.5 = (bf16[1280,128]{1,0:T(8,128)(2,1)S(1)}, bf16[1280,128]{1,0:T(8,128)(2,1)S(1)}, u32[]{:S(2)}, u32[]{:S(2)}) collective-permute-start(bf16[1280,128]{1,0:T(8,128)(2,1)S(1)} %get-tuple-element.29), channel_id=1, source_target_pairs={{0,127},{1,2},{2,1},{3,4},{4,3},{5,6},{6,5},{7,8},{8,7},{9,10},{10... | collective-permute-start | bytes 983048 | tf_op jit(solution)/shard_map/ppermute | solution.py:494
  28.9 6.6 %collective-permute-start.6 = (bf16[512,128]{1,0:T(8,128)(2,1)S(1)}, bf16[512,128]{1,0:T(8,128)(2,1)S(1)}, u32[]{:S(2)}, u32[]{:S(2)}) collective-permute-start(bf16[512,128]{1,0:T(8,128)(2,1)S(1)} %get-tuple-element.30), channel_id=1, source_target_pairs={{0,2},{1,3},{2,0},{3,1},{4,6},{5,7},{6,4},{7,5},{8,10},{9,11},{10,... | collective-permute-start | bytes 393224 | tf_op jit(solution)/shard_map/ppermute | solution.py:497
  32.0 10.2 %collective-permute-start.7 = (bf16[512,128]{1,0:T(8,128)(2,1)S(1)}, bf16[512,128]{1,0:T(8,128)(2,1)S(1)}, u32[]{:S(2)}, u32[]{:S(2)}) collective-permute-start(bf16[512,128]{1,0:T(8,128)(2,1)S(1)} %get-tuple-element.31), channel_id=1, source_target_pairs={{0,126},{1,127},{2,4},{3,5},{4,2},{5,3},{6,8},{7,9},{8,6},{9,7},{1... | collective-permute-start | bytes 393224 | tf_op jit(solution)/shard_map/ppermute | solution.py:495

commit v5 on v4

--- a/solution.py
+++ b/solution.py
@@ -26,10 +26,6 @@
 def side_at(cols, r, ncoarse):
     step = cols[1, r] - cols[0, r]
     return jnp.where(jnp.logical_or(step == 1, step == 1 - ncoarse), 1, -1)
-
-
-def place():
-    return lax.axis_index(AXES)
 
 
 def dot(a, b):
@@ -224,8 +220,15 @@
 
 def middle_kernel(part_in, edge, wt, p_low, p_high, part):
     for side in (0, 1):
-        halo = stack_bands(halo_bands(p_high if side else p_low, 3))
-        extra = dot(edge[blk(3 * side, 3), :], halo).astype(BF)
+        halo = halo_bands(p_high if side else p_low, 3)
+        far, tall = (2, 2) if side else (0, 0)
+        near = [h for h in range(3) if h != far]
+        lanes = slice(0, 2 * B) if side else slice(B, 3 * B)
+        terms = dot(edge[blk(3 * side, 3), lanes], stack_bands([halo[h] for h in near]))
+        last = dot(edge[blk(3 * side + tall), far * B : (far + 1) * B], stack_bands([halo[far]]))
+        extra = jnp.concatenate(
+            [(terms[n * B : (n + 1) * B, :] + (last if n == tall else 0.0)).astype(BF) for n in range(3)], axis=0
+        )
         terms = dot(wt[blk(3 * side, 3), :], extra)
         for m in range(3):
             j = 3 * side + m
@@ -233,9 +236,7 @@
             part[j, :, at] = part_in[j, :, at] + terms[m * B : (m + 1) * B, :]
 
 
-def outer_kernel(part, own, ownt, q_low, q_high, fine_out, ma, mb, na, nb, cp):
-    d = place()
-    even = d % 2 == 0
+def outer_kernel(part, own, ownt, q_low, q_high, fine_out, mu, md, nu, nd, cp):
     low = halo_bands(q_low, 2)
     high = halo_bands(q_high, 2)
     lines = part[...].astype(BF).reshape(6 * B, 8 * B)
@@ -282,27 +283,10 @@
         for t in range(4):
             dst[blk(t), :] = fine[t]
 
-    @pl.when(even)
-    def _():
-        put(mb, 0, 0, to_low)
-        put(ma, 5, 3, to_high)
-
-    @pl.when(jnp.logical_not(even))
-    def _():
-        put(ma, 0, 0, to_low)
-        put(mb, 5, 3, to_high)
-
-    even2 = (d // 2) % 2 == 0
-
-    @pl.when(even2)
-    def _():
-        put2(nb, two_low)
-        put2(na, two_high)
-
-    @pl.when(jnp.logical_not(even2))
-    def _():
-        put2(na, two_low)
-        put2(nb, two_high)
+    put(mu, 5, 3, to_high)
+    put(md, 0, 0, to_low)
+    put2(nu, two_high)
+    put2(nd, two_low)
 
 
 def column_block(part, j, t):
@@ -324,20 +308,12 @@
         copy.wait()
 
 
-def last_kernel(coarse_in, part, fine, ma, mb, na, nb, coarse_out, coarsest_out, rows, sems):
-    d = place()
-    even = d % 2 == 0
-    even2 = (d // 2) % 2 == 0
-
+def last_kernel(coarse_in, part, fine, mu, md, nu, nd, coarse_out, coarsest_out, rows, sems):
     def one(low, t):
-        if low:
-            return jnp.where(even, mb[blk(t), :], ma[blk(t), :]).astype(F32)
-        return jnp.where(even, ma[blk(t), :], mb[blk(t), :]).astype(F32)
+        return (mu if low else md)[blk(t), :].astype(F32)
 
     def two(low, t):
-        if low:
-            return jnp.where(even2, nb[blk(t), :], na[blk(t), :]).astype(F32)
-        return jnp.where(even2, na[blk(t), :], nb[blk(t), :]).astype(F32)
+        return (nu if low else nd)[blk(t), :].astype(F32)
 
     for t in range(KC):
         value = jnp.zeros((B, B), F32)
@@ -395,10 +371,6 @@
     a = a_vals.reshape(ROWS * K * B, B)
     p = p_vals.reshape(ROWS * 2 * B, B)
     p2 = p2_vals.reshape(CROWS * 2 * B, B)
-    swap_a = [(i, i ^ 1) for i in range(devices)]
-    swap_b = [(i, (i + 1) % devices if i % 2 else (i - 1) % devices) for i in range(devices)]
-    skip_a = [(i, i ^ 2) for i in range(devices)]
-    skip_b = [(i, (i + 2) % devices if i & 2 else (i - 2) % devices) for i in range(devices)]
 
     def pack(*refs):
         pack_kernel(ncoarse, devices, *refs)
@@ -477,7 +449,7 @@
         cost=pl.CostEstimate(flops=10**9, bytes_accessed=4 * 10**6, transcendentals=0),
         input_output_aliases={0: 0},
     )
-    fine, ma, mb, na, nb = call(
+    fine, mu, md, nu, nd = call(
         outer_kernel,
         "vvvvv",
         [
@@ -491,10 +463,12 @@
         [pltpu.VMEM((6 * B, 5 * B), BF)],
         pl.CostEstimate(flops=10**9, bytes_accessed=4 * 10**6, transcendentals=0),
     )
-    mb = lax.ppermute(mb, AXES, swap_b)
-    nb = lax.ppermute(nb, AXES, skip_b)
-    ma = lax.ppermute(ma, AXES, swap_a)
-    na = lax.ppermute(na, AXES, skip_a)
+    up2 = [(i, (i + 2) % devices) for i in range(devices)]
+    down2 = [((i + 2) % devices, i) for i in range(devices)]
+    mu = lax.ppermute(mu, AXES, up)
+    nu = lax.ppermute(nu, AXES, up2)
+    md = lax.ppermute(md, AXES, down)
+    nd = lax.ppermute(nd, AXES, down2)
     (coarse,) = call(
         store_kernel,
         "v",
@@ -507,7 +481,7 @@
         last_kernel,
         "hvvvvvv",
         [("h", (CROWS * KC * B, B), BF), ("h", (KC * B, B), BF)],
-        (coarse, part, fine, ma, mb, na, nb),
+        (coarse, part, fine, mu, md, nu, nd),
         [pltpu.VMEM(((10 + KC) * B, B), BF), pltpu.SemaphoreType.DMA((3,))],
         input_output_aliases={0: 0},
     )

time: 46.5 us -> 46.1 us (level)
  waiting for transfers between devices: 12.4 us -> 1.68 us
  starting transfers between devices: 19.7 us -> 30.3 us
    ppermute x4, waiting for transfers between devices: 12.4 us -> 1.67 us  [the longest x1 1.66 us: body(): nu = lax.ppermute(nu, AXES, up2)]
    ppermute x4, starting transfers between devices: 4.17 us -> 14.7 us  [the longest x1 7.47 us: body(): nd = lax.ppermute(nd, AXES, down2)]
  transfers between devices with their start and end apart: 8 -> 8, of which waited for: 3 -> 1; matrix products, arithmetic and copies ran while one was open for 0% -> 0% of each run, Pallas kernels for 21% -> 21%
where the time goes in v5:
time: 46.1 us; the launch traced here: 46 us
  starting transfers between devices  30.3 us (66%)
  Pallas kernels  13.3 us (29%)
  waiting for transfers between devices  1.68 us (4%)
  between operations  0.72 us (2%)
    pallas_call x7, Pallas kernels, call(): pl.pallas_call(kernel, in_specs=[kinds[c] for c in ins], out_specs=tuple(...  13.3 us
    ppermute x1, starting transfers between devices, body(): nd = lax.ppermute(nd, AXES, down2)  7.47 us
    ppermute x1, starting transfers between devices, body(): q_high = lax.ppermute(qd, AXES, down)  7.17 us
    ppermute x1, starting transfers between devices, body(): md = lax.ppermute(md, AXES, down)  7.16 us
    ppermute x1, starting transfers between devices, body(): p_high = lax.ppermute(pd, AXES, down)  6.71 us
    ppermute x1, starting transfers between devices, body(): p_low = lax.ppermute(pu, AXES, up)  1.68 us
    ppermute x1, waiting for transfers between devices, body(): nu = lax.ppermute(nu, AXES, up2)  1.66 us
  transfers between devices with their start and end apart: 8, of which 1 were waited for; matrix products, arithmetic and copies ran while one was open for 0% of the time, Pallas kernels for 21%

profile of v5, /device:TPU:0, one launch (start us, length us, event | category | flops | bytes accessed | tf_op | source)
XLA Modules:
  0.0 46.0 jit_solution(15035355042119822537)
XLA Ops:
  0.6 1.2 %shard_map.79 = (bf16[784,128]{1,0:T(8,128)(2,1)S(1)}, bf16[528,128]{1,0:T(8,128)(2,1)S(1)}, bf16[784,128]{1,0:T(8,128)(2,1)S(1)}, bf16[528,128]{1,0:T(8,128)(2,1)S(1)}) custom-call(s32[2,16]{1,0:T(2,128)} %bitcast.22, s32[2,4]{1,0:T(2,128)} %bitcast.25, bf16[4096,128]{1,0:T(8,128)(2,1)} %bitcast.14, bf16[1024,128]{1,0:T(8,128)(2,1)} %bitcast.18), custom_call_target="tpu_custom_call" | custom-call | tf_op jit(solution)/shard_map/pallas_call | solution.py:352
  1.9 1.7 %collective-permute-start = (bf16[784,128]{1,0:T(8,128)(2,1)S(1)}, bf16[784,128]{1,0:T(8,128)(2,1)S(1)}, u32[]{:S(2)}, u32[]{:S(2)}) collective-permute-start(bf16[784,128]{1,0:T(8,128)(2,1)S(1)} %get-tuple-element.21), channel_id=1, source_target_pairs={{0,1},{1,2},{2,3},{3,4},{4,5},{5,6},{6,7},{7,8},{8,9},{9,10},{10,1... | collective-permute-start | bytes 602120 | tf_op jit(solution)/shard_map/ppermute | solution.py:391
  3.5 6.7 %collective-permute-start.1 = (bf16[784,128]{1,0:T(8,128)(2,1)S(1)}, bf16[784,128]{1,0:T(8,128)(2,1)S(1)}, u32[]{:S(2)}, u32[]{:S(2)}) collective-permute-start(bf16[784,128]{1,0:T(8,128)(2,1)S(1)} %get-tuple-element.22), channel_id=1, source_target_pairs={{1,0},{2,1},{3,2},{4,3},{5,4},{6,5},{7,6},{8,7},{9,8},{10,9},{11,1... | collective-permute-start | bytes 602120 | tf_op jit(solution)/shard_map/ppermute | solution.py:412
  10.2 0.0 collective-permute-start.2
  10.3 7.2 %collective-permute-start.3 = (bf16[528,128]{1,0:T(8,128)(2,1)S(1)}, bf16[528,128]{1,0:T(8,128)(2,1)S(1)}, u32[]{:S(2)}, u32[]{:S(2)}) collective-permute-start(bf16[528,128]{1,0:T(8,128)(2,1)S(1)} %get-tuple-element.26), channel_id=1, source_target_pairs={{1,0},{2,1},{3,2},{4,3},{5,4},{6,5},{7,6},{8,7},{9,8},{10,9},{11,1... | collective-permute-start | bytes 405512 | tf_op jit(solution)/shard_map/ppermute | solution.py:413
  17.4 2.9 %shard_map.77.refs_0_ = bf16[1024,640]{1,0:T(8,128)(2,1)S(1)} custom-call(s32[5,1,16]{2,1,0:T(1,128)} %bitcast.20, s32[2,16]{1,0:T(2,128)} %bitcast.23, bf16[10240,128]{1,0:T(8,128)(2,1)} %bitcast.12, bf16[4096,128]{1,0:T(8,128)(2,1)} %bitcast.15), custom_call_target="tpu_custom_call" | custom-call | flops 1000000 | bytes 1000000 | tf_op jit(solution)/shard_map/pallas_call | solution.py:352
  20.3 4.8 %shard_map.78 = (bf16[1024,640]{1,0:T(8,128)(2,1)S(1)}, f32[6,128,1024]{2,1,0:T(8,128)S(1)}, bf16[768,384]{1,0:T(8,128)(2,1)S(1)}, bf16[768,384]{1,0:T(8,128)(2,...) custom-call(bf16[1024,640]{1,0:T(8,128)(2,1)S(1)} %shard_map.77.refs_0_, ...), custom_call_target="tpu_custom_call", output_to_operand_aliasing={{0}: (0, {})} | custom-call | flops 1000000000 | bytes 8000000 | tf_op jit(solution)/shard_map/pallas_call | solution.py:352
  25.2 0.0 collective-permute-done.p_low
  25.2 0.0 collective-permute-done.1.p_high
  25.2 1.1 %shard_map.80.part = f32[6,128,1024]{2,1,0:T(8,128)S(1)} custom-call(f32[6,128,1024]{2,1,0:T(8,128)S(1)} %get-tuple-element.18.part_in, bf16[768,384]{1,0:T(8,128)(2,1)S(1)} %get-tuple-element.19.edge, bf16[768,384]{1,0:T(8,128)(2,1)S(1)} %get-tuple-element.20.wt, bf16[784,128]{1,0:T(8,128)(2,1)S(1)} %collective-permute-done.p_low, ...), custom_call_target="tpu_custom_call", output_to_operand_aliasing={{}: (0, {})} | custom-call | flops 1000000000 | bytes 4000000 | tf_op jit(solution)/shard_map/pallas_call | solution.py:352
  26.3 0.0 collective-permute-done.2.q_low
  26.3 0.0 collective-permute-done.3.q_high
  26.3 1.4 %shard_map.82 = (f32[128,640]{1,0:T(8,128)S(1)}, bf16[1280,128]{1,0:T(8,128)(2,1)S(1)}, bf16[1280,128]{1,0:T(8,128)(2,1)S(1)}, bf16[512,128]{1,0:T(8,128)(2,1)S(1)}, bf16[512,128]{1,0:T(8,128)(2,1)S(1)}) custom-call(f32[6,128,1024]{2,1,0:T(8,128)S(1)} %shard_map.80.part, bf16[512,384]{1,0:T(8,128)(2,1)S(1)} %get-tuple-element.23.own, ...), custom_call_target="tpu_custom_call" | custom-call | flops 1000000000 | bytes 4000000 | tf_op jit(solution)/shard_map/pallas_call | solution.py:352
  27.7 0.1 collective-permute-start.4
  27.8 7.2 %collective-permute-start.5 = (bf16[1280,128]{1,0:T(8,128)(2,1)S(1)}, bf16[1280,128]{1,0:T(8,128)(2,1)S(1)}, u32[]{:S(2)}, u32[]{:S(2)}) collective-permute-start(bf16[1280,128]{1,0:T(8,128)(2,1)S(1)} %get-tuple-element.29), channel_id=1, source_target_pairs={{1,0},{2,1},{3,2},{4,3},{5,4},{6,5},{7,6},{8,7},{9,8},{10,9},{11,1... | collective-permute-start | bytes 983048 | tf_op jit(solution)/shard_map/ppermute | solution.py:470
  34.9 0.0 collective-permute-start.6
  34.9 7.5 %collective-permute-start.7 = (bf16[512,128]{1,0:T(8,128)(2,1)S(1)}, bf16[512,128]{1,0:T(8,128)(2,1)S(1)}, u32[]{:S(2)}, u32[]{:S(2)}) collective-permute-start(bf16[512,128]{1,0:T(8,128)(2,1)S(1)} %get-tuple-element.31), channel_id=1, source_target_pairs={{2,0},{3,1},{4,2},{5,3},{6,4},{7,5},{8,6},{9,7},{10,8},{11,9},{12,... | collective-permute-start | bytes 393224 | tf_op jit(solution)/shard_map/ppermute | solution.py:471
  42.4 1.0 %shard_map.81.coarse_in = bf16[3584,128]{1,0:T(8,128)(2,1)} custom-call(f32[6,128,1024]{2,1,0:T(8,128)S(1)} %shard_map.80.part), custom_call_target="tpu_custom_call" | custom-call | flops 1000000 | bytes 3000000 | tf_op jit(solution)/shard_map/pallas_call | solution.py:352
  43.4 1.7 %collective-permute-done.6.nu = bf16[512,128]{1,0:T(8,128)(2,1)S(1)} collective-permute-done((bf16[512,128]{1,0:T(8,128)(2,1)S(1)}, bf16[512,128]{1,0:T(8,128)(2,1)S(1)}, u32[]{:S(2)}, u32[]{:S(2)}) %collective-permute-start.6) | collective-permute-done | bytes 131104 | tf_op jit(solution)/shard_map/ppermute | solution.py:469
  45.0 0.0 collective-permute-done.7.nd
  45.0 0.0 collective-permute-done.4.mu
  45.0 0.0 collective-permute-done.5.md
  45.1 0.9 %shard_map.83 = (bf16[3584,128]{1,0:T(8,128)(2,1)}, bf16[896,128]{1,0:T(8,128)(2,1)}) custom-call(bf16[3584,128]{1,0:T(8,128)(2,1)} %shard_map.81.coarse_in, f32[6,128,1024]{2,1,0:T(8,128)S(1)} %shard_map.80.part, f32[128,640]{1,0:T(8,128)S(1)} %get-tuple-element.27.fine, ...), custom_call_target="tpu_custom_call", output_to_operand_aliasing={{0}: (0, {})} | custom-call | tf_op jit(solution)/shard_map/pallas_call | solution.py:352
Async XLA Ops:
  1.9 23.3 %collective-permute-start = (bf16[784,128]{1,0:T(8,128)(2,1)S(1)}, bf16[784,128]{1,0:T(8,128)(2,1)S(1)}, u32[]{:S(2)}, u32[]{:S(2)}) collective-permute-start(bf16[784,128]{1,0:T(8,128)(2,1)S(1)} %get-tuple-element.21), channel_id=1, source_target_pairs={{0,1},{1,2},{2,3},{3,4},{4,5},{5,6},{6,7},{7,8},{8,9},{9,10},{10,1... | collective-permute-start | bytes 602120 | tf_op jit(solution)/shard_map/ppermute | solution.py:391
  3.5 21.6 %collective-permute-start.1 = (bf16[784,128]{1,0:T(8,128)(2,1)S(1)}, bf16[784,128]{1,0:T(8,128)(2,1)S(1)}, u32[]{:S(2)}, u32[]{:S(2)}) collective-permute-start(bf16[784,128]{1,0:T(8,128)(2,1)S(1)} %get-tuple-element.22), channel_id=1, source_target_pairs={{1,0},{2,1},{3,2},{4,3},{5,4},{6,5},{7,6},{8,7},{9,8},{10,9},{11,1... | collective-permute-start | bytes 602120 | tf_op jit(solution)/shard_map/ppermute | solution.py:412
  10.2 16.0 %collective-permute-start.2 = (bf16[528,128]{1,0:T(8,128)(2,1)S(1)}, bf16[528,128]{1,0:T(8,128)(2,1)S(1)}, u32[]{:S(2)}, u32[]{:S(2)}) collective-permute-start(bf16[528,128]{1,0:T(8,128)(2,1)S(1)} %get-tuple-element.25), channel_id=1, source_target_pairs={{0,1},{1,2},{2,3},{3,4},{4,5},{5,6},{6,7},{7,8},{8,9},{9,10},{10,1... | collective-permute-start | bytes 405512 | tf_op jit(solution)/shard_map/ppermute | solution.py:392
  10.3 16.0 %collective-permute-start.3 = (bf16[528,128]{1,0:T(8,128)(2,1)S(1)}, bf16[528,128]{1,0:T(8,128)(2,1)S(1)}, u32[]{:S(2)}, u32[]{:S(2)}) collective-permute-start(bf16[528,128]{1,0:T(8,128)(2,1)S(1)} %get-tuple-element.26), channel_id=1, source_target_pairs={{1,0},{2,1},{3,2},{4,3},{5,4},{6,5},{7,6},{8,7},{9,8},{10,9},{11,1... | collective-permute-start | bytes 405512 | tf_op jit(solution)/shard_map/ppermute | solution.py:413
  27.7 17.4 %collective-permute-start.4 = (bf16[1280,128]{1,0:T(8,128)(2,1)S(1)}, bf16[1280,128]{1,0:T(8,128)(2,1)S(1)}, u32[]{:S(2)}, u32[]{:S(2)}) collective-permute-start(bf16[1280,128]{1,0:T(8,128)(2,1)S(1)} %get-tuple-element.28), channel_id=1, source_target_pairs={{0,1},{1,2},{2,3},{3,4},{4,5},{5,6},{6,7},{7,8},{8,9},{9,10},{10,1... | collective-permute-start | bytes 983048 | tf_op jit(solution)/shard_map/ppermute | solution.py:468
  27.8 17.3 %collective-permute-start.5 = (bf16[1280,128]{1,0:T(8,128)(2,1)S(1)}, bf16[1280,128]{1,0:T(8,128)(2,1)S(1)}, u32[]{:S(2)}, u32[]{:S(2)}) collective-permute-start(bf16[1280,128]{1,0:T(8,128)(2,1)S(1)} %get-tuple-element.29), channel_id=1, source_target_pairs={{1,0},{2,1},{3,2},{4,3},{5,4},{6,5},{7,6},{8,7},{9,8},{10,9},{11,1... | collective-permute-start | bytes 983048 | tf_op jit(solution)/shard_map/ppermute | solution.py:470
  34.9 10.1 %collective-permute-start.6 = (bf16[512,128]{1,0:T(8,128)(2,1)S(1)}, bf16[512,128]{1,0:T(8,128)(2,1)S(1)}, u32[]{:S(2)}, u32[]{:S(2)}) collective-permute-start(bf16[512,128]{1,0:T(8,128)(2,1)S(1)} %get-tuple-element.30), channel_id=1, source_target_pairs={{0,2},{1,3},{2,4},{3,5},{4,6},{5,7},{6,8},{7,9},{8,10},{9,11},{10,... | collective-permute-start | bytes 393224 | tf_op jit(solution)/shard_map/ppermute | solution.py:469
  34.9 10.1 %collective-permute-start.7 = (bf16[512,128]{1,0:T(8,128)(2,1)S(1)}, bf16[512,128]{1,0:T(8,128)(2,1)S(1)}, u32[]{:S(2)}, u32[]{:S(2)}) collective-permute-start(bf16[512,128]{1,0:T(8,128)(2,1)S(1)} %get-tuple-element.31), channel_id=1, source_target_pairs={{2,0},{3,1},{4,2},{5,3},{6,4},{7,5},{8,6},{9,7},{10,8},{11,9},{12,... | collective-permute-start | bytes 393224 | tf_op jit(solution)/shard_map/ppermute | solution.py:471

commit v6 on v5

--- a/solution.py
+++ b/solution.py
@@ -104,6 +104,10 @@
 
 def is_early():
     return lax.axis_index("gy") % 4 == 0
+
+
+def is_first():
+    return jnp.logical_and(lax.axis_index("gx") < 2, lax.axis_index("gy") == 0)
 
 
 def group_products(g, a_cols, p_cols, a_ref, p_ref, accs, nfine, ncoarse, store):
@@ -150,16 +154,24 @@
             copy.wait()
 
         def store(r, s, value):
-            prod[blk(4 * (r // 12) + r % 4), s * B : (s + 1) * B] = value.astype(BF)
+            prod[blk(r), s * B : (s + 1) * B] = value.astype(BF)
 
         for g in (0, 3):
             group_products(g, a_cols, p_cols, a_ref, p_ref, accs, nfine, ncoarse, store)
+
+        @pl.when(is_first())
+        def _():
+            pairs = [(a_hbm.at[group_rows(g)], a_ref.at[group_rows(g)]) for g in (1, 2)]
+            for copy in start_all(pairs, sems):
+                copy.wait()
+            for g in (1, 2):
+                group_products(g, a_cols, p_cols, a_ref, p_ref, accs, nfine, ncoarse, store)
 
 
 def inner_kernel(
     nfine, ncoarse, ncoarsest, prod_in, ac_hbm, pc_hbm, qc_hbm, a_hbm, p_hbm, p2_hbm,
     prod, part_out, edge_out, wt_out, own_out, ownt_out,
-    a_cols, p_cols, p2_cols, a_ref, p_ref, p2_ref, middle, sems, *accs,
+    a_cols, p_cols, p2_cols, a_ref, p_ref, p2_ref, sems, *accs,
 ):
     pairs = [(ac_hbm, a_cols), (pc_hbm, p_cols), (qc_hbm, p2_cols), (p_hbm, p_ref)]
     pairs += [(a_hbm.at[group_rows(g)], a_ref.at[group_rows(g)]) for g in (0, 3, 1, 2)]
@@ -171,7 +183,7 @@
     @pl.when(jnp.logical_not(is_early()))
     def _():
         def store(r, s, value):
-            prod[blk(4 * (r // 12) + r % 4), s * B : (s + 1) * B] = value.astype(BF)
+            prod[blk(r), s * B : (s + 1) * B] = value.astype(BF)
 
         for g in (0, 3):
             group_products(g, a_cols, p_cols, a_ref, p_ref, accs, nfine, ncoarse, store)
@@ -179,11 +191,14 @@
     for copy in copies[6:]:
         copy.wait()
 
-    def store_middle(r, s, value):
-        middle[blk(r - 4), s * B : (s + 1) * B] = value.astype(BF)
-
-    for g in (1, 2):
-        group_products(g, a_cols, p_cols, a_ref, p_ref, accs, nfine, ncoarse, store_middle)
+    @pl.when(jnp.logical_not(is_first()))
+    def _():
+        def store(r, s, value):
+            prod[blk(r), s * B : (s + 1) * B] = value.astype(BF)
+
+        for g in (1, 2):
+            group_products(g, a_cols, p_cols, a_ref, p_ref, accs, nfine, ncoarse, store)
+
     for side in (0, 1):
         first = 0 if side == 0 else ROWS - 3
         for n in range(3):
@@ -211,8 +226,7 @@
     part_out[...] = jnp.zeros_like(part_out)
     for g in (1, 2, 0, 3):
         bands = stack_bands(bands_of(p_ref, p_cols, range(4 * g, 4 * g + 4), ncoarse))
-        rows = middle[blk(4 * (g - 1), 4), :] if g in (1, 2) else prod[blk(4 * (g // 3), 4), :]
-        terms = dot_t(bands, rows)
+        terms = dot_t(bands, prod[blk(4 * g, 4), :])
         for m in range(3):
             at = slice(g * B, (g + 5) * B)
             part_out[g + m, :, at] = part_out[g + m, :, at] + terms[m * B : (m + 1) * B, :]
@@ -397,7 +411,7 @@
     (prod,) = call(
         early,
         "hhhh",
-        [("v", (8 * B, 5 * B), BF)],
+        [("v", (ROWS * B, 5 * B), BF)],
         (a_cols, p_cols, a, p),
         [
             pltpu.SMEM((K, 1, ROWS), jnp.int32),
@@ -419,7 +433,7 @@
         inner,
         "vhhhhhh",
         [
-            ("v", (8 * B, 5 * B), BF),
+            ("v", (ROWS * B, 5 * B), BF),
             ("v", (6, B, 8 * B), F32),
             ("v", (6 * B, 3 * B), BF),
             ("v", (6 * B, 3 * B), BF),
@@ -434,7 +448,6 @@
             pltpu.VMEM((ROWS * K * B, B), BF),
             pltpu.VMEM((ROWS * 2 * B, B), BF),
             pltpu.VMEM((CROWS * 2 * B, B), BF),
-            pltpu.VMEM((8 * B, 5 * B), BF),
             pltpu.SemaphoreType.DMA((9,)),
             *[pltpu.VMEM((8, B, B), F32) for _ in range(NACC)],
         ],

time: 46.1 us -> 47.6 us (1.033)
  Pallas kernels: 13.3 us -> 14.8 us
    pallas_call x7, Pallas kernels: 13.3 us -> 14.8 us  [call(): pl.pallas_call(kernel, in_specs=[kinds[c] for c in ins], out_specs=tuple(...]
  transfers between devices with their start and end apart: 8 -> 8, of which waited for: 1 -> 1; matrix products, arithmetic and copies ran while one was open for 0% -> 0% of each run, Pallas kernels for 21% -> 24%
where the time goes in v6:
time: 47.6 us; the launch traced here: 47.4 us
  starting transfers between devices  30.3 us (64%)
  Pallas kernels  14.8 us (31%)
  waiting for transfers between devices  1.68 us (4%)
  between operations  0.72 us (2%)
    pallas_call x7, Pallas kernels, call(): pl.pallas_call(kernel, in_specs=[kinds[c] for c in ins], out_specs=tuple(...  14.8 us
    ppermute x1, starting transfers between devices, body(): nd = lax.ppermute(nd, AXES, down2)  7.47 us
    ppermute x1, starting transfers between devices, body(): q_high = lax.ppermute(qd, AXES, down)  7.17 us
    ppermute x1, starting transfers between devices, body(): md = lax.ppermute(md, AXES, down)  7.16 us
    ppermute x1, starting transfers between devices, body(): p_high = lax.ppermute(pd, AXES, down)  6.71 us
    ppermute x1, starting transfers between devices, body(): p_low = lax.ppermute(pu, AXES, up)  1.68 us
    ppermute x1, waiting for transfers between devices, body(): nu = lax.ppermute(nu, AXES, up2)  1.66 us
  transfers between devices with their start and end apart: 8, of which 1 were waited for; matrix products, arithmetic and copies ran while one was open for 0% of the time, Pallas kernels for 24%

profile of v6, /device:TPU:0, one launch (start us, length us, event | category | flops | bytes accessed | tf_op | source)
XLA Modules:
  0.0 47.4 jit_solution(3105640490788889628)
XLA Ops:
  0.6 1.2 %shard_map.79 = (bf16[784,128]{1,0:T(8,128)(2,1)S(1)}, bf16[528,128]{1,0:T(8,128)(2,1)S(1)}, bf16[784,128]{1,0:T(8,128)(2,1)S(1)}, bf16[528,128]{1,0:T(8,128)(2,1)S(1)}) custom-call(s32[2,16]{1,0:T(2,128)} %bitcast.22, s32[2,4]{1,0:T(2,128)} %bitcast.25, bf16[4096,128]{1,0:T(8,128)(2,1)} %bitcast.14, bf16[1024,128]{1,0:T(8,128)(2,1)} %bitcast.18), custom_call_target="tpu_custom_call" | custom-call | tf_op jit(solution)/shard_map/pallas_call | solution.py:366
  1.9 1.7 %collective-permute-start = (bf16[784,128]{1,0:T(8,128)(2,1)S(1)}, bf16[784,128]{1,0:T(8,128)(2,1)S(1)}, u32[]{:S(2)}, u32[]{:S(2)}) collective-permute-start(bf16[784,128]{1,0:T(8,128)(2,1)S(1)} %get-tuple-element.21), channel_id=1, source_target_pairs={{0,1},{1,2},{2,3},{3,4},{4,5},{5,6},{6,7},{7,8},{8,9},{9,10},{10,1... | collective-permute-start | bytes 602120 | tf_op jit(solution)/shard_map/ppermute | solution.py:405
  3.5 6.7 %collective-permute-start.1 = (bf16[784,128]{1,0:T(8,128)(2,1)S(1)}, bf16[784,128]{1,0:T(8,128)(2,1)S(1)}, u32[]{:S(2)}, u32[]{:S(2)}) collective-permute-start(bf16[784,128]{1,0:T(8,128)(2,1)S(1)} %get-tuple-element.22), channel_id=1, source_target_pairs={{1,0},{2,1},{3,2},{4,3},{5,4},{6,5},{7,6},{8,7},{9,8},{10,9},{11,1... | collective-permute-start | bytes 602120 | tf_op jit(solution)/shard_map/ppermute | solution.py:426
  10.2 0.0 collective-permute-start.2
  10.3 7.2 %collective-permute-start.3 = (bf16[528,128]{1,0:T(8,128)(2,1)S(1)}, bf16[528,128]{1,0:T(8,128)(2,1)S(1)}, u32[]{:S(2)}, u32[]{:S(2)}) collective-permute-start(bf16[528,128]{1,0:T(8,128)(2,1)S(1)} %get-tuple-element.26), channel_id=1, source_target_pairs={{1,0},{2,1},{3,2},{4,3},{5,4},{6,5},{7,6},{8,7},{9,8},{10,9},{11,1... | collective-permute-start | bytes 405512 | tf_op jit(solution)/shard_map/ppermute | solution.py:427
  17.4 5.5 %shard_map.77.refs_0_ = bf16[2048,640]{1,0:T(8,128)(2,1)S(1)} custom-call(s32[5,1,16]{2,1,0:T(1,128)} %bitcast.20, s32[2,16]{1,0:T(2,128)} %bitcast.23, bf16[10240,128]{1,0:T(8,128)(2,1)} %bitcast.12, bf16[4096,128]{1,0:T(8,128)(2,1)} %bitcast.15), custom_call_target="tpu_custom_call" | custom-call | flops 1000000 | bytes 1000000 | tf_op jit(solution)/shard_map/pallas_call | solution.py:366
  22.9 3.7 %shard_map.78 = (bf16[2048,640]{1,0:T(8,128)(2,1)S(1)}, f32[6,128,1024]{2,1,0:T(8,128)S(1)}, bf16[768,384]{1,0:T(8,128)(2,1)S(1)}, bf16[768,384]{1,0:T(8,128)(2,...) custom-call(bf16[2048,640]{1,0:T(8,128)(2,1)S(1)} %shard_map.77.refs_0_, ...), custom_call_target="tpu_custom_call", output_to_operand_aliasing={{0}: (0, {})} | custom-call | flops 1000000000 | bytes 8000000 | tf_op jit(solution)/shard_map/pallas_call | solution.py:366
  26.6 0.0 collective-permute-done.p_low
  26.7 0.0 collective-permute-done.1.p_high
  26.7 1.1 %shard_map.80.part = f32[6,128,1024]{2,1,0:T(8,128)S(1)} custom-call(f32[6,128,1024]{2,1,0:T(8,128)S(1)} %get-tuple-element.18.part_in, bf16[768,384]{1,0:T(8,128)(2,1)S(1)} %get-tuple-element.19.edge, bf16[768,384]{1,0:T(8,128)(2,1)S(1)} %get-tuple-element.20.wt, bf16[784,128]{1,0:T(8,128)(2,1)S(1)} %collective-permute-done.p_low, ...), custom_call_target="tpu_custom_call", output_to_operand_aliasing={{}: (0, {})} | custom-call | flops 1000000000 | bytes 4000000 | tf_op jit(solution)/shard_map/pallas_call | solution.py:366
  27.7 0.0 collective-permute-done.2.q_low
  27.8 0.0 collective-permute-done.3.q_high
  27.8 1.4 %shard_map.82 = (f32[128,640]{1,0:T(8,128)S(1)}, bf16[1280,128]{1,0:T(8,128)(2,1)S(1)}, bf16[1280,128]{1,0:T(8,128)(2,1)S(1)}, bf16[512,128]{1,0:T(8,128)(2,1)S(1)}, bf16[512,128]{1,0:T(8,128)(2,1)S(1)}) custom-call(f32[6,128,1024]{2,1,0:T(8,128)S(1)} %shard_map.80.part, bf16[512,384]{1,0:T(8,128)(2,1)S(1)} %get-tuple-element.23.own, ...), custom_call_target="tpu_custom_call" | custom-call | flops 1000000000 | bytes 4000000 | tf_op jit(solution)/shard_map/pallas_call | solution.py:366
  29.2 0.1 collective-permute-start.4
  29.2 7.2 %collective-permute-start.5 = (bf16[1280,128]{1,0:T(8,128)(2,1)S(1)}, bf16[1280,128]{1,0:T(8,128)(2,1)S(1)}, u32[]{:S(2)}, u32[]{:S(2)}) collective-permute-start(bf16[1280,128]{1,0:T(8,128)(2,1)S(1)} %get-tuple-element.29), channel_id=1, source_target_pairs={{1,0},{2,1},{3,2},{4,3},{5,4},{6,5},{7,6},{8,7},{9,8},{10,9},{11,1... | collective-permute-start | bytes 983048 | tf_op jit(solution)/shard_map/ppermute | solution.py:483
  36.4 0.0 collective-permute-start.6
  36.4 7.5 %collective-permute-start.7 = (bf16[512,128]{1,0:T(8,128)(2,1)S(1)}, bf16[512,128]{1,0:T(8,128)(2,1)S(1)}, u32[]{:S(2)}, u32[]{:S(2)}) collective-permute-start(bf16[512,128]{1,0:T(8,128)(2,1)S(1)} %get-tuple-element.31), channel_id=1, source_target_pairs={{2,0},{3,1},{4,2},{5,3},{6,4},{7,5},{8,6},{9,7},{10,8},{11,9},{12,... | collective-permute-start | bytes 393224 | tf_op jit(solution)/shard_map/ppermute | solution.py:484
  43.9 1.0 %shard_map.81.coarse_in = bf16[3584,128]{1,0:T(8,128)(2,1)} custom-call(f32[6,128,1024]{2,1,0:T(8,128)S(1)} %shard_map.80.part), custom_call_target="tpu_custom_call" | custom-call | flops 1000000 | bytes 3000000 | tf_op jit(solution)/shard_map/pallas_call | solution.py:366
  44.9 1.7 %collective-permute-done.6.nu = bf16[512,128]{1,0:T(8,128)(2,1)S(1)} collective-permute-done((bf16[512,128]{1,0:T(8,128)(2,1)S(1)}, bf16[512,128]{1,0:T(8,128)(2,1)S(1)}, u32[]{:S(2)}, u32[]{:S(2)}) %collective-permute-start.6) | collective-permute-done | bytes 131104 | tf_op jit(solution)/shard_map/ppermute | solution.py:482
  46.5 0.0 collective-permute-done.7.nd
  46.5 0.0 collective-permute-done.4.mu
  46.5 0.0 collective-permute-done.5.md
  46.5 0.9 %shard_map.83 = (bf16[3584,128]{1,0:T(8,128)(2,1)}, bf16[896,128]{1,0:T(8,128)(2,1)}) custom-call(bf16[3584,128]{1,0:T(8,128)(2,1)} %shard_map.81.coarse_in, f32[6,128,1024]{2,1,0:T(8,128)S(1)} %shard_map.80.part, f32[128,640]{1,0:T(8,128)S(1)} %get-tuple-element.27.fine, ...), custom_call_target="tpu_custom_call", output_to_operand_aliasing={{0}: (0, {})} | custom-call | tf_op jit(solution)/shard_map/pallas_call | solution.py:366
Async XLA Ops:
  1.9 24.8 %collective-permute-start = (bf16[784,128]{1,0:T(8,128)(2,1)S(1)}, bf16[784,128]{1,0:T(8,128)(2,1)S(1)}, u32[]{:S(2)}, u32[]{:S(2)}) collective-permute-start(bf16[784,128]{1,0:T(8,128)(2,1)S(1)} %get-tuple-element.21), channel_id=1, source_target_pairs={{0,1},{1,2},{2,3},{3,4},{4,5},{5,6},{6,7},{7,8},{8,9},{9,10},{10,1... | collective-permute-start | bytes 602120 | tf_op jit(solution)/shard_map/ppermute | solution.py:405
  3.5 23.1 %collective-permute-start.1 = (bf16[784,128]{1,0:T(8,128)(2,1)S(1)}, bf16[784,128]{1,0:T(8,128)(2,1)S(1)}, u32[]{:S(2)}, u32[]{:S(2)}) collective-permute-start(bf16[784,128]{1,0:T(8,128)(2,1)S(1)} %get-tuple-element.22), channel_id=1, source_target_pairs={{1,0},{2,1},{3,2},{4,3},{5,4},{6,5},{7,6},{8,7},{9,8},{10,9},{11,1... | collective-permute-start | bytes 602120 | tf_op jit(solution)/shard_map/ppermute | solution.py:426
  10.2 17.5 %collective-permute-start.2 = (bf16[528,128]{1,0:T(8,128)(2,1)S(1)}, bf16[528,128]{1,0:T(8,128)(2,1)S(1)}, u32[]{:S(2)}, u32[]{:S(2)}) collective-permute-start(bf16[528,128]{1,0:T(8,128)(2,1)S(1)} %get-tuple-element.25), channel_id=1, source_target_pairs={{0,1},{1,2},{2,3},{3,4},{4,5},{5,6},{6,7},{7,8},{8,9},{9,10},{10,1... | collective-permute-start | bytes 405512 | tf_op jit(solution)/shard_map/ppermute | solution.py:406
  10.3 17.5 %collective-permute-start.3 = (bf16[528,128]{1,0:T(8,128)(2,1)S(1)}, bf16[528,128]{1,0:T(8,128)(2,1)S(1)}, u32[]{:S(2)}, u32[]{:S(2)}) collective-permute-start(bf16[528,128]{1,0:T(8,128)(2,1)S(1)} %get-tuple-element.26), channel_id=1, source_target_pairs={{1,0},{2,1},{3,2},{4,3},{5,4},{6,5},{7,6},{8,7},{9,8},{10,9},{11,1... | collective-permute-start | bytes 405512 | tf_op jit(solution)/shard_map/ppermute | solution.py:427
  29.2 17.4 %collective-permute-start.4 = (bf16[1280,128]{1,0:T(8,128)(2,1)S(1)}, bf16[1280,128]{1,0:T(8,128)(2,1)S(1)}, u32[]{:S(2)}, u32[]{:S(2)}) collective-permute-start(bf16[1280,128]{1,0:T(8,128)(2,1)S(1)} %get-tuple-element.28), channel_id=1, source_target_pairs={{0,1},{1,2},{2,3},{3,4},{4,5},{5,6},{6,7},{7,8},{8,9},{9,10},{10,1... | collective-permute-start | bytes 983048 | tf_op jit(solution)/shard_map/ppermute | solution.py:481
  29.2 17.3 %collective-permute-start.5 = (bf16[1280,128]{1,0:T(8,128)(2,1)S(1)}, bf16[1280,128]{1,0:T(8,128)(2,1)S(1)}, u32[]{:S(2)}, u32[]{:S(2)}) collective-permute-start(bf16[1280,128]{1,0:T(8,128)(2,1)S(1)} %get-tuple-element.29), channel_id=1, source_target_pairs={{1,0},{2,1},{3,2},{4,3},{5,4},{6,5},{7,6},{8,7},{9,8},{10,9},{11,1... | collective-permute-start | bytes 983048 | tf_op jit(solution)/shard_map/ppermute | solution.py:483
  36.4 10.1 %collective-permute-start.6 = (bf16[512,128]{1,0:T(8,128)(2,1)S(1)}, bf16[512,128]{1,0:T(8,128)(2,1)S(1)}, u32[]{:S(2)}, u32[]{:S(2)}) collective-permute-start(bf16[512,128]{1,0:T(8,128)(2,1)S(1)} %get-tuple-element.30), channel_id=1, source_target_pairs={{0,2},{1,3},{2,4},{3,5},{4,6},{5,7},{6,8},{7,9},{8,10},{9,11},{10,... | collective-permute-start | bytes 393224 | tf_op jit(solution)/shard_map/ppermute | solution.py:482
  36.4 10.1 %collective-permute-start.7 = (bf16[512,128]{1,0:T(8,128)(2,1)S(1)}, bf16[512,128]{1,0:T(8,128)(2,1)S(1)}, u32[]{:S(2)}, u32[]{:S(2)}) collective-permute-start(bf16[512,128]{1,0:T(8,128)(2,1)S(1)} %get-tuple-element.31), channel_id=1, source_target_pairs={{2,0},{3,1},{4,2},{5,3},{6,4},{7,5},{8,6},{9,7},{10,8},{11,9},{12,... | collective-permute-start | bytes 393224 | tf_op jit(solution)/shard_map/ppermute | solution.py:484
